TPU v7x, 32 devices: a whole 2x2x4 slice. The times are simulated.
32 devices in a mesh: dp: 8 (over y, x, core), tensor: 4 (over z).
Axes of the slice: x: 2, y: 2, z: 4, core: 2. Of those that a mesh axis runs over, the one named last changes fastest.
Arguments:
- block_in: float32 [4096, 1152], P(('dp', 'tensor')), may hold values from -6 to 6
- out_grad: float32 [4096, 1152], P(('dp', 'tensor')), may hold values from -6 to 6
- segments: int32 [4096], replicated, may hold values from 0 to 7, never falling along the last dimension, each value on 1 to 3072 neighbouring positions
- w_query: bfloat16 [1152, 1024], P('dp', 'tensor'), may hold values from -0.1875 to 0.1875
- w_keyval: bfloat16 [1152, 512], P(('dp', 'tensor')), may hold values from -0.1875 to 0.1875
- w_out: bfloat16 [1024, 1152], P('tensor', 'dp'), may hold values from -0.1875 to 0.1875
- w_gate: bfloat16 [1152, 6912], P('dp', 'tensor'), may hold values from -0.1875 to 0.1875
- w_up: bfloat16 [1152, 6912], P('dp', 'tensor'), may hold values from -0.1875 to 0.1875
- w_down: bfloat16 [6912, 1152], P('tensor', 'dp'), may hold values from -0.078125 to 0.078125
- gain_pre_attn: bfloat16 [1152], P(('dp', 'tensor')), may hold values from 0.5 to 1.5
- gain_post_attn: bfloat16 [1152], P(('dp', 'tensor')), may hold values from 0.5 to 1.5
- gain_pre_ffn: bfloat16 [1152], P(('dp', 'tensor')), may hold values from 0.5 to 1.5
- gain_post_ffn: bfloat16 [1152], P(('dp', 'tensor')), may hold values from 0.5 to 1.5
- gain_query: bfloat16 [256], P(('dp', 'tensor')), may hold values from 0.5 to 1.5
- gain_key: bfloat16 [256], P(('dp', 'tensor')), may hold values from 0.5 to 1.5
Outputs:
- block_out: float32 [4096, 1152], P(('dp', 'tensor'))
- grad_in: float32 [4096, 1152], P(('dp', 'tensor'))
- grad_w_query: float32 [1152, 1024], P('dp', 'tensor')
- grad_w_keyval: float32 [1152, 512], P(('dp', 'tensor'))
- grad_w_out: float32 [1024, 1152], P('tensor', 'dp')
- grad_w_gate: float32 [1152, 6912], P('dp', 'tensor')
- grad_w_up: float32 [1152, 6912], P('dp', 'tensor')
- grad_w_down: float32 [6912, 1152], P('tensor', 'dp')
- grad_pre_attn: float32 [1152], P(('dp', 'tensor'))
- grad_post_attn: float32 [1152], P(('dp', 'tensor'))
- grad_pre_ffn: float32 [1152], P(('dp', 'tensor'))
- grad_post_ffn: float32 [1152], P(('dp', 'tensor'))
- grad_gain_query: float32 [256], P(('dp', 'tensor'))
- grad_gain_key: float32 [256], P(('dp', 'tensor'))
Inputs may be any that keep to these rules, and one draw needn't show every extreme that they name: `segments`: document ids never fall along the stream; every document holds 1 to 3072 tokens and one holds exactly 3072.
All inputs are finite; a program needn't handle non-finite values.
Results may differ from a plain program's by a relative error of at most 0.02.
Values may be sent and summed in bfloat16 or wider, within the bound.
No kernel may reach another device: no remote copies, remote signals or barrier semaphores. Data moves between devices by JAX's collectives and lax.ppermute only.
A program may use at most 256 MiB of HBM per device.

v0:
```python
import jax
import jax.numpy as jnp
from jax import lax
from jax.sharding import PartitionSpec as P

HD = 256


EPSILON = 1e-06
ROPE_BASE = 1000000.0
QUERY_SCALE = 0.0625
MASKED = -1e30
GELU_COEF = 0.7978845608028654
GELU_CUBIC = 0.044715


def as_sent(value):
    return jax.tree.map(lambda a: a.astype(jnp.bfloat16) if a.dtype == jnp.float32 else a, value)


def shifted(value, axis, steps):
    count = lax.axis_size(axis)
    pairs = [(source, (source + steps) % count) for source in range(count)]
    return lax.ppermute(value, axis, pairs)


def rms_forward(values, scales):
    inverse = lax.rsqrt(jnp.mean(values * values, axis=-1, keepdims=True) + EPSILON)
    return (values * inverse * scales, inverse)


def rms_backward(values, inverse, scales, upstream):
    weighted = upstream * scales
    inner_mean = jnp.mean(values * weighted, axis=-1, keepdims=True)
    grad_values = inverse * weighted - values * (inverse * inverse * inverse) * inner_mean
    grad_scales = jnp.sum((upstream * values * inverse).reshape(-1, values.shape[-1]), axis=0)
    return (grad_values, grad_scales)


def gelu_pair(values):
    inside = GELU_COEF * (values + GELU_CUBIC * values * values * values)
    tangent = jnp.tanh(inside)
    output = 0.5 * values * (1.0 + tangent)
    derivative = 0.5 * (1.0 + tangent) + 0.5 * values * (1.0 - tangent * tangent) * GELU_COEF * (
        1.0 + 3.0 * GELU_CUBIC * values * values
    )
    return (output, derivative)


def rotate_half(values):
    halfway = values.shape[-1] // 2
    return jnp.concatenate([-values[..., halfway:], values[..., :halfway]], axis=-1)


def rope_tables(positions):
    halfway = HD // 2
    frequency = ROPE_BASE ** (-2.0 * jnp.arange(halfway, dtype=jnp.float32) / HD)
    angles = positions.astype(jnp.float32)[:, None] * frequency[None, :]
    angles = jnp.concatenate([angles, angles], axis=1)
    return (jnp.cos(angles), jnp.sin(angles))


def apply_rope(values, cosine, sine_part):
    return values * cosine + rotate_half(values) * sine_part


def rope_back(upstream, cosine, sine_part):
    return upstream * cosine - rotate_half(upstream * sine_part)


def head_rows(values, head_count):
    number = values.shape[0]
    return (
        values.reshape(number, head_count, HD).transpose(1, 0, 2).reshape(head_count * number, HD)
    )


def token_rows(values, head_count):
    number = values.shape[0] // head_count
    return (
        values.reshape(head_count, number, HD).transpose(1, 0, 2).reshape(number, head_count * HD)
    )


def contract_first(left, right):
    return lax.dot_general(
        left, right, (((0,), (0,)), ((), ())), preferred_element_type=jnp.float32
    )


def contract_last(left, right):
    return lax.dot_general(
        left, right, (((1,), (1,)), ((), ())), preferred_element_type=jnp.float32
    )


def gather_rows(values):
    return lax.all_gather(values, "tensor", axis=0, tiled=True)


def reduce_rows(values):
    return lax.psum_scatter(values, "tensor", scatter_dimension=0, tiled=True)


def fold_keys(pair, update_fn, start_state):
    return update_fn(
        start_state,
        jax.tree.map(lambda part: lax.all_gather(part, "dp", axis=0, tiled=True), as_sent(pair)),
        jnp.int32(0),
    )


def piece_grads(query_rows, grad_rows, log_rows, delta_rows, key_part, value_part, visible):
    scores = contract_last(query_rows, key_part)
    weights = jnp.where(visible, jnp.exp(scores - log_rows[:, None]), 0.0)
    grad_prob = contract_last(grad_rows, value_part)
    grad_score = (weights * (grad_prob - delta_rows[:, None])).astype(jnp.bfloat16)
    return (weights.astype(jnp.bfloat16), grad_score)


def per_device(
    block_in,
    out_grad,
    segments,
    w_query,
    w_keyval,
    w_out,
    w_gate,
    w_up,
    w_down,
    gain_pre_attn,
    gain_post_attn,
    gain_pre_ffn,
    gain_post_ffn,
    gain_query,
    gain_key,
):
    splits = lax.axis_size("tensor")
    row_count = block_in.shape[0]
    block_len = row_count * splits
    data_index = lax.axis_index("dp")
    tensor_index = lax.axis_index("tensor")
    block_start = data_index * block_len
    shared_params = (
        lax.all_gather(w_keyval, ("dp", "tensor"), axis=0, tiled=True),
        lax.all_gather(gain_pre_attn, ("dp", "tensor"), axis=0, tiled=True),
        lax.all_gather(gain_post_attn, ("dp", "tensor"), axis=0, tiled=True),
        lax.all_gather(gain_pre_ffn, ("dp", "tensor"), axis=0, tiled=True),
        lax.all_gather(gain_post_ffn, ("dp", "tensor"), axis=0, tiled=True),
        lax.all_gather(gain_query, ("dp", "tensor"), axis=0, tiled=True),
        lax.all_gather(gain_key, ("dp", "tensor"), axis=0, tiled=True),
    )
    keyval_full = shared_params[0]
    scale_pre_attn = shared_params[1].astype(jnp.float32)
    scale_post_attn = shared_params[2].astype(jnp.float32)
    scale_pre_ffn = shared_params[3].astype(jnp.float32)
    scale_post_ffn = shared_params[4].astype(jnp.float32)
    scale_query = shared_params[5].astype(jnp.float32)
    scale_key = shared_params[6].astype(jnp.float32)
    query_full, out_full = (
        lax.all_gather(w_query, "dp", axis=0, tiled=True),
        lax.all_gather(w_out, "dp", axis=1, tiled=True),
    )
    head_count = query_full.shape[1] // HD
    normed_in, inv_in = rms_forward(block_in, scale_pre_attn)
    normed_bf = normed_in.astype(jnp.bfloat16)
    gathered_in = gather_rows(normed_bf)
    queries = jnp.dot(gathered_in, query_full, preferred_element_type=jnp.float32).reshape(
        block_len, head_count, HD
    )
    keyval = jnp.dot(gathered_in, keyval_full, preferred_element_type=jnp.float32)
    cosine, sine_part = rope_tables(block_start + jnp.arange(block_len, dtype=jnp.int32))
    query_norm, inv_query = rms_forward(queries, scale_query)
    query_rot = (
        apply_rope(query_norm, cosine[:, None, :], sine_part[:, None, :]) * QUERY_SCALE
    ).astype(jnp.bfloat16)
    query_tok = query_rot.reshape(block_len, head_count * HD)
    query_rows = head_rows(query_tok, head_count)
    key_proj = keyval[:, :HD]
    key_norm, inv_key = rms_forward(key_proj, scale_key)
    key_rot = apply_rope(key_norm, cosine, sine_part).astype(jnp.bfloat16)
    value_proj = keyval[:, HD:].astype(jnp.bfloat16)
    own_segment = lax.dynamic_slice_in_dim(segments, block_start, block_len)
    own_index = block_start + jnp.arange(block_len, dtype=jnp.int32)
    row_segment = jnp.tile(own_segment, head_count)
    row_index = jnp.tile(own_index, head_count)

    def key_mask(number):
        key_index = jnp.arange(number, dtype=jnp.int32)
        return (row_segment[:, None] == segments[None, :]) & (
            key_index[None, :] <= row_index[:, None]
        )

    def attend(running, pieces, offset):
        key_part, value_part = pieces
        visible = key_mask(key_part.shape[0])

        def attend_update(current):
            row_max, row_sum, row_acc = current
            scores = jnp.where(visible, contract_last(query_rows, key_part), MASKED)
            new_max = jnp.maximum(row_max, jnp.max(scores, axis=1))
            weights = jnp.where(visible, jnp.exp(scores - new_max[:, None]), 0.0)
            row_sum = jnp.sum(weights, axis=1)
            row_acc = jnp.dot(
                weights.astype(jnp.bfloat16), value_part, preferred_element_type=jnp.float32
            )
            return (new_max, row_sum, row_acc)

        return lax.cond(jnp.any(visible), attend_update, lambda current: current, running)

    row_total = head_count * block_len
    start_state = (
        jnp.full((row_total,), MASKED, jnp.float32),
        jnp.zeros((row_total,), jnp.float32),
        jnp.zeros((row_total, HD), jnp.float32),
    )
    row_max, row_sum, row_acc = fold_keys((key_rot, value_proj), attend, start_state)
    log_norm = row_max + jnp.log(row_sum)
    mixed_rows = (row_acc / row_sum[:, None]).astype(jnp.bfloat16)
    mixed_tok = token_rows(mixed_rows, head_count)
    attn_out = reduce_rows(jnp.dot(mixed_tok, out_full, preferred_element_type=jnp.float32))
    attn_norm, inv_attn = rms_forward(attn_out, scale_post_attn)
    resid_mid = block_in + attn_norm
    gate_full, up_full, down_full = (
        lax.all_gather(w_gate, "dp", axis=0, tiled=True),
        lax.all_gather(w_up, "dp", axis=0, tiled=True),
        lax.all_gather(w_down, "dp", axis=1, tiled=True),
    )
    normed_mid, inv_mid = rms_forward(resid_mid, scale_pre_ffn)
    gathered_mid = gather_rows(normed_mid.astype(jnp.bfloat16))
    gate_pre = jnp.dot(gathered_mid, gate_full, preferred_element_type=jnp.float32)
    up_proj = jnp.dot(gathered_mid, up_full, preferred_element_type=jnp.float32)
    gate_act, gate_deriv = gelu_pair(gate_pre)
    hidden = (gate_act * up_proj).astype(jnp.bfloat16)
    ffn_out = reduce_rows(jnp.dot(hidden, down_full, preferred_element_type=jnp.float32))
    ffn_norm, inv_ffn = rms_forward(ffn_out, scale_post_ffn)
    block_out = resid_mid + ffn_norm
    grad_ffn, grad_post_ffn = rms_backward(ffn_out, inv_ffn, scale_post_ffn, out_grad)
    grad_ffn_all = gather_rows(grad_ffn.astype(jnp.bfloat16))
    grad_hidden = contract_last(grad_ffn_all, down_full)
    grad_w_down = contract_first(hidden, grad_ffn_all)
    grad_gate = (grad_hidden * up_proj * gate_deriv).astype(jnp.bfloat16)
    grad_up = (grad_hidden * gate_act).astype(jnp.bfloat16)
    grad_w_gate = contract_first(gathered_mid, grad_gate)
    grad_w_up = contract_first(gathered_mid, grad_up)
    grad_mid = reduce_rows(contract_last(grad_gate, gate_full) + contract_last(grad_up, up_full))
    grad_resid, grad_pre_ffn = rms_backward(resid_mid, inv_mid, scale_pre_ffn, grad_mid)
    grad_resid_mid = out_grad + grad_resid
    grad_attn, grad_post_attn = rms_backward(attn_out, inv_attn, scale_post_attn, grad_resid_mid)
    grad_attn_all = gather_rows(grad_attn.astype(jnp.bfloat16))
    grad_w_out = contract_first(mixed_tok, grad_attn_all)
    grad_mixed_tok = contract_last(grad_attn_all, out_full).astype(jnp.bfloat16)
    grad_mixed_rows = head_rows(grad_mixed_tok, head_count)
    delta_rows = jnp.sum(
        grad_mixed_rows.astype(jnp.float32) * mixed_rows.astype(jnp.float32), axis=1
    )

    def query_fold(running, pieces, offset):
        key_part, value_part = pieces
        visible = key_mask(key_part.shape[0])

        def query_update(current):
            weight_bf, grad_score = piece_grads(
                query_rows, grad_mixed_rows, log_norm, delta_rows, key_part, value_part, visible
            )
            return jnp.dot(grad_score, key_part, preferred_element_type=jnp.float32)

        return lax.cond(jnp.any(visible), query_update, lambda current: current, running)

    grad_query_rows = fold_keys(
        (key_rot, value_proj), query_fold, jnp.zeros((row_total, HD), jnp.float32)
    )
    log_tok = jnp.transpose(log_norm.reshape(head_count, block_len))
    delta_tok = jnp.transpose(delta_rows.reshape(head_count, block_len))
    log_stream, delta_stream = (
        lax.all_gather(log_tok, "dp", axis=0, tiled=True),
        lax.all_gather(delta_tok, "dp", axis=0, tiled=True),
    )
    dp_count = lax.axis_size("dp")
    prior_key, prior_value = shifted((key_rot, value_proj), "dp", 1)
    target_start = (data_index + dp_count - 1) % dp_count * block_len
    target_segment = lax.dynamic_slice_in_dim(segments, target_start, block_len)
    target_index = target_start + jnp.arange(block_len, dtype=jnp.int32)
    query_part = lax.all_gather(query_tok, "dp", axis=0, tiled=True)
    grad_part = lax.all_gather(grad_mixed_tok, "dp", axis=0, tiled=True)
    number = query_part.shape[0]
    part_queries = head_rows(query_part, head_count)
    part_grads = head_rows(grad_part, head_count)
    part_log = jnp.transpose(log_stream).reshape(-1)
    part_delta = jnp.transpose(delta_stream).reshape(-1)
    part_index = jnp.tile(jnp.arange(number, dtype=jnp.int32), head_count)
    part_segment = jnp.tile(segments, head_count)
    visible = (part_segment[:, None] == target_segment[None, :]) & (
        target_index[None, :] <= part_index[:, None]
    )

    def key_update(current):
        weight_bf, grad_score = piece_grads(
            part_queries, part_grads, part_log, part_delta, prior_key, prior_value, visible
        )
        extra = jnp.concatenate(
            [contract_first(grad_score, part_queries), contract_first(weight_bf, part_grads)],
            axis=1,
        )
        return extra

    grad_keyval_target = lax.cond(
        jnp.any(visible),
        key_update,
        lambda current: current,
        jnp.zeros((block_len, 2 * HD), jnp.float32),
    )
    grad_keyval_split = lax.psum_scatter(
        grad_keyval_target.astype(jnp.bfloat16), "tensor", scatter_dimension=0, tiled=True
    ).astype(jnp.float32)
    grad_keyval_rows = shifted(grad_keyval_split.astype(jnp.bfloat16), "dp", -1).astype(
        grad_keyval_split.dtype
    )
    grad_query_rot = token_rows(grad_query_rows, head_count).reshape(block_len, head_count, HD)
    grad_query_norm = (
        rope_back(grad_query_rot, cosine[:, None, :], sine_part[:, None, :]) * QUERY_SCALE
    )
    grad_queries, grad_gain_query = rms_backward(queries, inv_query, scale_query, grad_query_norm)
    grad_query_bf = grad_queries.reshape(block_len, head_count * HD).astype(jnp.bfloat16)
    grad_w_query = contract_first(gathered_in, grad_query_bf)
    local_start = tensor_index * row_count
    key_local = lax.dynamic_slice_in_dim(key_proj, local_start, row_count, 0)
    inv_local = lax.dynamic_slice_in_dim(inv_key, local_start, row_count, 0)
    cosine_local = lax.dynamic_slice_in_dim(cosine, local_start, row_count, 0)
    sine_local = lax.dynamic_slice_in_dim(sine_part, local_start, row_count, 0)
    grad_key_norm = rope_back(grad_keyval_rows[:, :HD], cosine_local, sine_local)
    grad_key_proj, grad_gain_key = rms_backward(key_local, inv_local, scale_key, grad_key_norm)
    grad_keyval_bf = jnp.concatenate([grad_key_proj, grad_keyval_rows[:, HD:]], axis=1).astype(
        jnp.bfloat16
    )
    grad_w_keyval = contract_first(normed_bf, grad_keyval_bf)
    grad_normed = reduce_rows(contract_last(grad_query_bf, query_full)) + contract_last(
        grad_keyval_bf, keyval_full
    )
    grad_in_norm, grad_pre_attn = rms_backward(block_in, inv_in, scale_pre_attn, grad_normed)
    grad_in = grad_resid_mid + grad_in_norm
    owned_small = (
        lax.psum_scatter(grad_w_keyval, ("dp", "tensor"), scatter_dimension=0, tiled=True),
        lax.psum_scatter(grad_pre_attn, ("dp", "tensor"), scatter_dimension=0, tiled=True),
        lax.psum_scatter(grad_post_attn, ("dp", "tensor"), scatter_dimension=0, tiled=True),
        lax.psum_scatter(grad_pre_ffn, ("dp", "tensor"), scatter_dimension=0, tiled=True),
        lax.psum_scatter(grad_post_ffn, ("dp", "tensor"), scatter_dimension=0, tiled=True),
        lax.psum_scatter(grad_gain_query, ("dp", "tensor"), scatter_dimension=0, tiled=True),
        lax.psum_scatter(grad_gain_key, ("dp", "tensor"), scatter_dimension=0, tiled=True),
    )
    owned_query, owned_out = (
        lax.psum_scatter(
            grad_w_query.astype(jnp.bfloat16), "dp", scatter_dimension=0, tiled=True
        ).astype(jnp.float32),
        lax.psum_scatter(
            grad_w_out.astype(jnp.bfloat16), "dp", scatter_dimension=1, tiled=True
        ).astype(jnp.float32),
    )
    owned_gate, owned_up, owned_down = (
        lax.psum_scatter(
            grad_w_gate.astype(jnp.bfloat16), "dp", scatter_dimension=0, tiled=True
        ).astype(jnp.float32),
        lax.psum_scatter(
            grad_w_up.astype(jnp.bfloat16), "dp", scatter_dimension=0, tiled=True
        ).astype(jnp.float32),
        lax.psum_scatter(
            grad_w_down.astype(jnp.bfloat16), "dp", scatter_dimension=1, tiled=True
        ).astype(jnp.float32),
    )
    return (
        block_out,
        grad_in,
        owned_query,
        owned_small[0],
        owned_out,
        owned_gate,
        owned_up,
        owned_down,
        owned_small[1],
        owned_small[2],
        owned_small[3],
        owned_small[4],
        owned_small[5],
        owned_small[6],
    )


def solution(mesh):
    return jax.shard_map(
        per_device,
        mesh=mesh,
        in_specs=(
            P(("dp", "tensor"), None),
            P(("dp", "tensor"), None),
            P(),
            P("dp", "tensor"),
            P(("dp", "tensor"), None),
            P("tensor", "dp"),
            P("dp", "tensor"),
            P("dp", "tensor"),
            P("tensor", "dp"),
            P(("dp", "tensor")),
            P(("dp", "tensor")),
            P(("dp", "tensor")),
            P(("dp", "tensor")),
            P(("dp", "tensor")),
            P(("dp", "tensor")),
        ),
        out_specs=(
            P(("dp", "tensor"), None),
            P(("dp", "tensor"), None),
            P("dp", "tensor"),
            P(("dp", "tensor"), None),
            P("tensor", "dp"),
            P("dp", "tensor"),
            P("dp", "tensor"),
            P("tensor", "dp"),
            P(("dp", "tensor")),
            P(("dp", "tensor")),
            P(("dp", "tensor")),
            P(("dp", "tensor")),
            P(("dp", "tensor")),
            P(("dp", "tensor")),
        ),
        check_vma=False,
    )
```

profile of v0, /device:TPU:0, one launch (start us, length us, event | category | flops | bytes accessed | tf_op | source)
XLA Modules:
  0.0 1136.8 jit_solution(17095509604098788834)
XLA Ops:
  12.3 42.4 %all-reduce.15 = (bf16[1152]{0:T(1024)(128)(2,1)S(1)}, bf16[256]{0:T(256)(128)(2,1)S(1)}, bf16[256]{0:T(256)(128)(2,1)S(1)}, bf16[1152]{0:T(1024)(128)(2,1)S(1)}...) all-reduce(bf16[1152]{0:T(1024)(128)(2,1)S(1)} %dynamic-update-slic, ...), channel_id=1, replica_groups=mesh['dp'=8,'tensor'=4] {'dp','tensor'}, use_global_device_ids=true, to_apply=%add | all-reduce | flops 5120 | bytes 20480
  59.2 11.3 all_gather.70
  70.7 18.7 %all-gather.18.cloned.1.call-done = bf16[512,1152]{1,0:T(8,128)(2,1)} async-done(((bf16[128,1152]{1,0:T(8,128)(2,1)}), bf16[512,1152]{1,0:T(8,128)(2,1)}) %all-gather.18.cloned.1.call-update) | async-done | bytes 1179664 | tf_op jit(solution)/shard_map/all_gather | solution.py:98
  92.0 53.7 %all-gather.40.cloned.1.call-done = bf16[32,36,512]{2,1,0:T(8,128)(2,1)} async-done(((bf16[1,36,512]{2,1,0:T(8,128)(2,1)}), bf16[32,36,512]{2,1,0:T(8,128)(2,1)}) %all-gather.40.cloned.1.call-update) | async-done | bytes 1179664 | tf_op jit(solution)/shard_map/all_gather | solution.py:145
  145.7 2.1 reshape.237
  147.8 2.6 fusion.45
  151.6 3.2 fusion.28
  157.5 3.9 fusion.13
  162.0 10.4 all_gather.76
  172.5 10.6 all-gather.20.cloned.1.call-done
  183.0 30.0 %all-gather.22.cloned.1.call-done = bf16[4096,256]{0,1:T(8,128)(2,1)} async-done(((bf16[512,256]{0,1:T(8,128)(2,1)}), bf16[4096,256]{0,1:T(8,128)(2,1)}) %all-gather.22.cloned.1.call-update) | async-done | bytes 2097168 | tf_op jit(solution)/shard_map/all_gather | solution.py:108
  213.0 10.9 conditional.3
  213.1 3.2 fusion.41
  217.0 3.6 fusion.2
  221.3 2.6 fusion.3
  228.6 46.9 %reduce-scatter.15.cloned.1.call-done = f32[128,1152]{1,0:T(8,128)} async-done(((f32[512,1152]{1,0:T(8,128)}), f32[128,1152]{1,0:T(8,128)}) %reduce-scatter.15.cloned.1.call-update) | async-done | bytes 589840 | tf_op jit(solution)/shard_map/reduce_scatter | solution.py:102
  282.8 30.5 %all-gather.26.cloned.1.call-done = bf16[1152,1728]{1,0:T(8,128)(2,1)} async-done(((bf16[144,1728]{1,0:T(8,128)(2,1)}), bf16[1152,1728]{1,0:T(8,128)(2,1)}) %all-gather.26.cloned.1.call-update) | async-done | bytes 3981328 | tf_op jit(solution)/shard_map/all_gather | solution.py:225
  313.3 32.6 %all-gather.24.cloned.1.call-done = bf16[512,1152]{1,0:T(8,128)(2,1)} async-done(((bf16[128,1152]{1,0:T(8,128)(2,1)}), bf16[512,1152]{1,0:T(8,128)(2,1)}) %all-gather.24.cloned.1.call-update) | async-done | bytes 1179664 | tf_op jit(solution)/shard_map/all_gather | solution.py:98
  346.0 6.8 fusion.47
  352.7 30.7 %all-gather.28.cloned.1.call-done = bf16[1152,1728]{1,0:T(8,128)(2,1)} async-done(((bf16[144,1728]{1,0:T(8,128)(2,1)}), bf16[1152,1728]{1,0:T(8,128)(2,1)}) %all-gather.28.cloned.1.call-update) | async-done | bytes 3981328 | tf_op jit(solution)/shard_map/all_gather | solution.py:226
  383.4 9.3 multiply_convert_fusion.3
  392.7 29.1 %all-gather.30.cloned.1.call-done = bf16[1728,1152]{0,1:T(8,128)(2,1)} async-done(((bf16[1728,144]{0,1:T(8,128)(2,1)}), bf16[1728,1152]{0,1:T(8,128)(2,1)}) %all-gather.30.cloned.1.call-update) | async-done | bytes 3981328 | tf_op jit(solution)/shard_map/all_gather | solution.py:227
  421.8 6.7 fusion.48
  429.9 46.9 %reduce-scatter.17.cloned.1.call-done = f32[128,1152]{1,0:T(8,128)} async-done(((f32[512,1152]{1,0:T(8,128)}), f32[128,1152]{1,0:T(8,128)}) %reduce-scatter.17.cloned.1.call-update) | async-done | bytes 589840 | tf_op jit(solution)/shard_map/reduce_scatter | solution.py:102
  477.9 2.0 multiply_reduce_fusion
  480.0 2.4 subtract_convert_fusion.1
  482.9 29.7 %all-gather.32.cloned.1.call-done = bf16[512,1152]{1,0:T(8,128)(2,1)} async-done(((bf16[128,1152]{1,0:T(8,128)(2,1)}), bf16[512,1152]{1,0:T(8,128)(2,1)}) %all-gather.32.cloned.1.call-update) | async-done | bytes 1179664 | tf_op jit(solution)/shard_map/all_gather | solution.py:98
  512.5 9.5 multiply_convert_fusion.2
  522.1 2.6 fusion.49
  525.5 4.1 convolution_add_fusion
  529.7 47.3 %reduce-scatter.19.cloned.1.call-done = f32[128,1152]{1,0:T(8,128)} async-done(((f32[512,1152]{1,0:T(8,128)}), f32[128,1152]{1,0:T(8,128)}) %reduce-scatter.19.cloned.1.call-update) | async-done | bytes 589840 | tf_op jit(solution)/shard_map/reduce_scatter | solution.py:102
  578.9 2.5 multiply_reduce_fusion.2
  583.8 29.4 %all-gather.34.cloned.1.call-done = bf16[512,1152]{1,0:T(8,128)(2,1)} async-done(((bf16[128,1152]{1,0:T(8,128)(2,1)}), bf16[512,1152]{1,0:T(8,128)(2,1)}) %all-gather.34.cloned.1.call-update) | async-done | bytes 1179664 | tf_op jit(solution)/shard_map/all_gather | solution.py:98
  613.2 2.7 multiply_reduce_fusion.14
  617.9 3.9 fusion.14
  623.2 8.8 all-gather.3
  632.0 8.0 all-gather.4
  640.0 2.4 all-gather.36.cloned.1.call-done
  642.4 29.9 %all-gather.38.cloned.1.call-done = bf16[4096,256]{0,1:T(8,128)(2,1)} async-done(((bf16[512,256]{0,1:T(8,128)(2,1)}), bf16[4096,256]{0,1:T(8,128)(2,1)}) %all-gather.38.cloned.1.call-update) | async-done | bytes 2097168 | tf_op jit(solution)/shard_map/all_gather | solution.py:285
  672.3 17.5 %conditional.5 = (bf16[512,512]{0,1:T(8,128)(2,1)S(1)}) conditional(s32[]{:T(128)} %convert_element_type.147, () %tuple.34, (bf16[4096,256]{0,1:T(8,128)(2,1)}, bf16[512,256]{0,1:T(8,128)(2,1)}, f32[4096,1]{0,1:T(1,128)S(1)}, pred[4096,512]{1,0:T(32,128)(4,1)}, bf16[4096,256]{0,1:T(8,128)(2,1)}, /*index=5*/bf16[512,256]{0,1:T(8,128)(2,1)}, ...), branch_computations={%region_23.24_spmd, %region_24.25_spmd} | conditional | flops 4308598784 | bytes 79724608 | solution.py:307
  672.3 4.7 exponential_select_fusion.1
  677.1 2.5 fusion.10
  680.5 8.3 fusion.12
  690.9 6.2 convolution_convert_fusion.2
  697.4 6.1 convolution_convert_fusion.1
  703.6 6.1 convolution_convert_fusion
  710.3 15.2 %conditional.4 = (f32[512,256]{0,1:T(8,128)S(1)}) conditional(s32[]{:T(128)} %convert_element_type.125, () %tuple.32, (bf16[512,256]{0,1:T(8,128)(2,1)}, bf16[4096,256]{0,1:T(8,128)(2,1)}, f32[512]{0:T(512)S(1)}, pred[512,4096]{1,0:T(32,128)(4,1)S(1)}, bf16[512,256]{0,1:T(8,128)(2,1)}, /*index=5*/bf16[4096,256]{0,1:T(8,128)(2,1)}, ...), branch_computations={%region_18.19_spmd, %region_19.20_spmd} | conditional | flops 3231711232 | bytes 26218504 | solution.py:268
  710.3 6.3 fusion.44
  716.6 8.7 fusion.8
  725.5 2.8 fusion.23
  728.4 2.2 multiply_reduce_fusion.12
  732.2 2.7 convolution_convert_fusion.3
  735.0 2.0 fusion.50
  740.1 26.5 %reduce-scatter.27.cloned.1.call-done = bf16[144,1728]{1,0:T(8,128)(2,1)} async-done(((bf16[1152,1728]{1,0:T(8,128)(2,1)}), bf16[144,1728]{1,0:T(8,128)(2,1)}) %reduce-scatter.27.cloned.1.call-update) | async-done | bytes 497680 | tf_op jit(solution)/shard_map/reduce_scatter | solution.py:360
  766.7 2.1 convert_element_type.154
  768.7 52.3 %reduce-scatter.29.cloned.1.call-done = bf16[144,1728]{1,0:T(8,128)(2,1)} async-done(((bf16[1152,1728]{1,0:T(8,128)(2,1)}), bf16[144,1728]{1,0:T(8,128)(2,1)}) %reduce-scatter.29.cloned.1.call-update) | async-done | bytes 497680 | tf_op jit(solution)/shard_map/reduce_scatter | solution.py:363
  821.0 2.1 convert_element_type.156
  823.1 52.4 %reduce-scatter.31.cloned.1.call-done = bf16[1728,144]{0,1:T(8,128)(2,1)} async-done(((bf16[1728,1152]{0,1:T(8,128)(2,1)}), bf16[1728,144]{0,1:T(8,128)(2,1)}) %reduce-scatter.31.cloned.1.call-update) | async-done | bytes 497680 | tf_op jit(solution)/shard_map/reduce_scatter | solution.py:366
  875.5 2.1 convert_element_type.158
  877.6 35.3 %reduce-scatter.23.cloned.1.call-done = bf16[144,256]{1,0:T(8,128)(2,1)} async-done(((bf16[1152,256]{1,0:T(8,128)(2,1)}), bf16[144,256]{1,0:T(8,128)(2,1)}) %reduce-scatter.23.cloned.1.call-update) | async-done | bytes 73744 | tf_op jit(solution)/shard_map/reduce_scatter | solution.py:352
  914.4 36.0 %reduce-scatter.25.cloned.1.call-done = bf16[256,144]{0,1:T(8,128)(2,1)} async-done(((bf16[256,1152]{0,1:T(8,128)(2,1)}), bf16[256,144]{0,1:T(8,128)(2,1)}) %reduce-scatter.25.cloned.1.call-update) | async-done | bytes 73744 | tf_op jit(solution)/shard_map/reduce_scatter | solution.py:355
  956.1 115.1 %fusion = f32[40,512]{1,0:T(8,128)S(1)} fusion(f32[1152,512]{1,0:T(8,128)} %fusion.33), kind=kCustom, calls=%all-reduce-scatter | all-reduce-scatter fusion | flops 655361 | bytes 2441216
  1077.3 2.2 collective-permute-start.6
  1080.5 44.4 %all-reduce.14 = (f32[1152]{0:T(1024)S(1)}, f32[1152]{0:T(1024)S(1)}, f32[1152]{0:T(1024)S(1)}, f32[1152]{0:T(1024)S(1)}, f32[256]{0:T(256)S(1)}, /*index=5*/f32[256]{0:T(256)S(1)}) all-reduce(f32[1152]{0:T(1024)S(1)} %get-tuple-element.145, f32[1152]{0:T(1024)S(1)} %copy-done.29, ...), channel_id=15, replica_groups=mesh['dp'=8,'tensor'=4] {'dp','tensor'}, use_global_device_ids=true, to_apply=%region_35.36.clone | all-reduce | flops 5120 | bytes 40960
  (243 shorter events, 67.4 us)
Async XLA Ops:
  7.2 82.1 %all-gather.18.cloned.1.call-start = ((), (), s32[]{:S(2)}) async-start(), calls=%async_computation.10 | async-start | bytes 1474560 | tf_op jit(solution)/shard_map/all_gather | solution.py:98
  54.7 4.5 copy-start.47
  56.4 14.2 %copy-start.37 = (f32[128]{0:T(128)}, f32[128]{0:T(128)S(1)}, u32[]{:S(2)}) copy-start(f32[128]{0:T(128)S(1)} %get-tuple-element.200) | copy-start | bytes 1540
  58.3 87.3 %all-gather.40.cloned.1.call-start = ((), (), s32[]{:S(2)}) async-start(), calls=%async_computation.30 | async-start | bytes 1351680 | tf_op jit(solution)/shard_map/all_gather | solution.py:145
  59.1 123.9 %all-gather.20.cloned.1.call-start = ((), (), s32[]{:S(2)}) async-start(), calls=%async_computation.11 | async-start | bytes 2359296 | tf_op jit(solution)/shard_map/all_gather | solution.py:108
  59.2 92.4 %copy-start.31 = (f32[256]{0:T(256)}, f32[256]{0:T(256)S(1)}, u32[]{:S(2)}) copy-start(f32[256]{0:T(256)S(1)} %convert_element_type.131) | copy-start | bytes 3076
  70.6 77.3 %copy-start.7 = (bf16[1152,256]{1,0:T(8,128)(2,1)}, bf16[1152,256]{1,0:T(8,128)(2,1)S(1)}, u32[]{:S(2)}) copy-start(bf16[1152,256]{1,0:T(8,128)(2,1)S(1)} %all_gather.70) | copy-start | bytes 1769476
  91.2 60.4 %copy-start.1 = (f32[512,256]{0,1:T(8,128)}, f32[512,256]{0,1:T(8,128)S(1)}, u32[]{:S(2)}) copy-start(f32[512,256]{0,1:T(8,128)S(1)} %get-tuple-element.208) | copy-start | bytes 1572868
  91.8 59.8 %copy-start.25 = (f32[512]{0:T(512)}, f32[512]{0:T(512)S(1)}, u32[]{:S(2)}) copy-start(f32[512]{0:T(512)S(1)} %get-tuple-element.198) | copy-start | bytes 6148
  150.4 4.4 copy-start.15
  151.5 5.3 copy-start.22
  154.8 7.2 copy-start.24
  154.8 58.1 %all-gather.22.cloned.1.call-start = ((), (), s32[]{:S(2)}) async-start(), calls=%async_computation.12 | async-start | bytes 2359296 | tf_op jit(solution)/shard_map/all_gather | solution.py:108
  156.7 118.9 %reduce-scatter.15.cloned.1.call-start = ((), (), s32[]{:S(2)}) async-start(), calls=%async_computation.13 | async-start | bytes 2949120 | tf_op jit(solution)/shard_map/reduce_scatter | solution.py:102
  172.4 52.2 %copy-start.9 = (bf16[256,1152]{0,1:T(8,128)(2,1)}, bf16[256,1152]{0,1:T(8,128)(2,1)S(1)}, u32[]{:S(2)}) copy-start(bf16[256,1152]{0,1:T(8,128)(2,1)S(1)} %all_gather.76) | copy-start | bytes 1769476
  217.0 4.3 copy-start.46
  227.4 50.5 %copy-start = (f32[128,1152]{1,0:T(8,128)S(1)}, f32[128,1152]{1,0:T(8,128)}, u32[]{:S(2)}) copy-start(f32[128,1152]{1,0:T(8,128)} %param.21) | copy-start | bytes 1769476
  227.4 85.9 %all-gather.26.cloned.1.call-start = ((), (), s32[]{:S(2)}) async-start(), calls=%async_computation.15 | async-start | bytes 4644864 | tf_op jit(solution)/shard_map/all_gather | solution.py:225
  228.0 118.0 %all-gather.24.cloned.1.call-start = ((), (), s32[]{:S(2)}) async-start(), calls=%async_computation.14 | async-start | bytes 1474560 | tf_op jit(solution)/shard_map/all_gather | solution.py:98
  275.6 4.6 copy-start.21
  281.0 102.4 %all-gather.28.cloned.1.call-start = ((), (), s32[]{:S(2)}) async-start(), calls=%async_computation.16 | async-start | bytes 4644864 | tf_op jit(solution)/shard_map/all_gather | solution.py:226
  281.8 140.0 %all-gather.30.cloned.1.call-start = ((), (), s32[]{:S(2)}) async-start(), calls=%async_computation.17 | async-start | bytes 4644864 | tf_op jit(solution)/shard_map/all_gather | solution.py:227
  282.5 194.2 %reduce-scatter.17.cloned.1.call-start = ((), (), s32[]{:S(2)}) async-start(), calls=%async_computation.18 | async-start | bytes 2949120 | tf_op jit(solution)/shard_map/reduce_scatter | solution.py:102
  428.6 84.0 %all-gather.32.cloned.1.call-start = ((), (), s32[]{:S(2)}) async-start(), calls=%async_computation.19 | async-start | bytes 1474560 | tf_op jit(solution)/shard_map/all_gather | solution.py:98
  482.4 94.6 %reduce-scatter.19.cloned.1.call-start = ((), (), s32[]{:S(2)}) async-start(), calls=%async_computation.20 | async-start | bytes 2949120 | tf_op jit(solution)/shard_map/reduce_scatter | solution.py:102
  512.5 9.6 copy-start.44
  529.7 83.5 %all-gather.34.cloned.1.call-start = ((), (), s32[]{:S(2)}) async-start(), calls=%async_computation.21 | async-start | bytes 1474560 | tf_op jit(solution)/shard_map/all_gather | solution.py:98
  577.0 5.2 copy-start.3
  577.0 5.2 copy-start.40
  577.0 5.2 copy-start.43
  581.4 34.6 %copy-start.19 = (bf16[512,256]{0,1:T(8,128)(2,1)S(1)}, bf16[512,256]{0,1:T(8,128)(2,1)}, u32[]{:S(2)}) copy-start(bf16[512,256]{0,1:T(8,128)(2,1)} %get-tuple-element.187) | copy-start | bytes 786436
  581.4 34.7 %copy-start.20 = (bf16[512,256]{0,1:T(8,128)(2,1)S(1)}, bf16[512,256]{0,1:T(8,128)(2,1)}, u32[]{:S(2)}) copy-start(bf16[512,256]{0,1:T(8,128)(2,1)} %slice.86) | copy-start | bytes 786436
  581.4 36.5 %copy-start.23 = (s32[4096]{0:T(1024)S(1)}, s32[4096]{0:T(1024)}, u32[]{:S(2)}) copy-start(s32[4096]{0:T(1024)} %param.23) | copy-start | bytes 49156
  581.4 36.5 %copy-start.34 = (s32[512]{0:T(512)S(1)}, s32[512]{0:T(512)}, u32[]{:S(2)}) copy-start(s32[512]{0:T(512)} %get-tuple-element.195) | copy-start | bytes 6148
  583.1 59.3 %all-gather.36.cloned.1.call-start = ((), (), s32[]{:S(2)}) async-start(), calls=%async_computation.23 | async-start | bytes 2359296 | tf_op jit(solution)/shard_map/all_gather | solution.py:284
  583.7 38.8 %copy-start.36 = (f32[512]{0:T(512)S(1)}, f32[512]{0:T(512)}, u32[]{:S(2)}) copy-start(f32[512]{0:T(512)} %copy-done.35) | copy-start | bytes 6148
  583.7 88.6 %all-gather.38.cloned.1.call-start = ((), (), s32[]{:S(2)}) async-start(), calls=%async_computation.24 | async-start | bytes 2359296 | tf_op jit(solution)/shard_map/all_gather | solution.py:285
  616.0 121.0 %reduce-scatter.33.cloned.1.call-start = ((), (), s32[]{:S(2)}) async-start(), calls=%async_computation.31 | async-start | bytes 655360
  616.0 23.9 %collective-permute-start = (bf16[512,256]{0,1:T(8,128)(2,1)S(1)}, bf16[512,256]{0,1:T(8,128)(2,1)}, u32[]{:S(2)}, u32[]{:S(2)}) collective-permute-start(bf16[512,256]{0,1:T(8,128)(2,1)S(1)} %copy-done.19), channel_id=1, source_target_pairs={{0,4},{4,8},{8,12},{12,16},{16,20},{20,24},{24,28},{28,0},{1,5},{5... | collective-permute-start | bytes 786440 | tf_op jit(solution)/shard_map/ppermute | solution.py:24
  616.1 23.8 %collective-permute-start.1 = (bf16[512,256]{0,1:T(8,128)(2,1)S(1)}, bf16[512,256]{0,1:T(8,128)(2,1)}, u32[]{:S(2)}, u32[]{:S(2)}) collective-permute-start(bf16[512,256]{0,1:T(8,128)(2,1)S(1)} %copy-done.20), channel_id=1, source_target_pairs={{0,4},{4,8},{8,12},{12,16},{16,20},{20,24},{24,28},{28,0},{1,5},{5... | collective-permute-start | bytes 786440 | tf_op jit(solution)/shard_map/ppermute | solution.py:24
  672.3 4.7 copy-start.17
  690.8 75.8 %reduce-scatter.27.cloned.1.call-start = ((), (), s32[]{:S(2)}) async-start(), calls=%async_computation.27 | async-start | bytes 4644864 | tf_op jit(solution)/shard_map/reduce_scatter | solution.py:360
  697.1 123.9 %reduce-scatter.29.cloned.1.call-start = ((), (), s32[]{:S(2)}) async-start(), calls=%async_computation.28 | async-start | bytes 4644864 | tf_op jit(solution)/shard_map/reduce_scatter | solution.py:363
  703.5 172.0 %reduce-scatter.31.cloned.1.call-start = ((), (), s32[]{:S(2)}) async-start(), calls=%async_computation.29 | async-start | bytes 4644864 | tf_op jit(solution)/shard_map/reduce_scatter | solution.py:366
  709.7 203.1 %reduce-scatter.23.cloned.1.call-start = ((), (), s32[]{:S(2)}) async-start(), calls=%async_computation.25 | async-start | bytes 663552 | tf_op jit(solution)/shard_map/reduce_scatter | solution.py:352
  725.5 5.1 copy-start.33
  730.8 4.2 copy-start.8
  732.1 218.2 %reduce-scatter.25.cloned.1.call-start = ((), (), s32[]{:S(2)}) async-start(), calls=%async_computation.26 | async-start | bytes 663552 | tf_op jit(solution)/shard_map/reduce_scatter | solution.py:355
  734.9 340.7 %reduce-scatter.21.cloned.1.call-start = ((), (), s32[]{:S(2)}) async-start(), calls=%async_computation.22 | async-start | bytes 2949120 | tf_op jit(solution)/shard_map/reduce_scatter | solution.py:102
  738.1 213.9 %collective-permute-start.2 = (bf16[128,512]{0,1:T(8,128)(2,1)S(1)}, bf16[128,512]{0,1:T(8,128)(2,1)S(1)}, u32[]{:S(2)}, u32[]{:S(2)}) collective-permute-start(bf16[128,512]{0,1:T(8,128)(2,1)S(1)} %copy.83), channel_id=1, source_target_pairs={{0,28},{4,0},{8,4},{12,8},{16,12},{20,16},{24,20},{28,24},{1,29},{... | collective-permute-start | bytes 393224 | tf_op jit(solution)/shard_map/ppermute | solution.py:24
  768.7 184.2 %copy-start.18 = (f32[512,256]{0,1:T(8,128)S(1)}, f32[512,256]{0,1:T(8,128)}, u32[]{:S(2)}) copy-start(f32[512,256]{0,1:T(8,128)} %get-tuple-element.174) | copy-start | bytes 1572868
  768.7 184.2 %copy-start.32 = (f32[256]{0:T(256)S(1)}, f32[256]{0:T(256)}, u32[]{:S(2)}) copy-start(f32[256]{0:T(256)} %copy-done.31) | copy-start | bytes 3076
  768.7 185.4 %copy-start.16 = (bf16[128,1152]{1,0:T(8,128)(2,1)S(1)}, bf16[128,1152]{1,0:T(8,128)(2,1)}, u32[]{:S(2)}) copy-start(bf16[128,1152]{1,0:T(8,128)(2,1)} %multiply_convert_fusion.5) | copy-start | bytes 884740
  954.1 121.5 %copy-start.11 = (bf16[1152,512]{1,0:T(8,128)(2,1)S(1)}, bf16[1152,512]{1,0:T(8,128)(2,1)}, u32[]{:S(2)}) copy-start(bf16[1152,512]{1,0:T(8,128)(2,1)} %copy-done.10) | copy-start | bytes 3538948
  954.1 121.5 %copy-start.38 = (f32[128]{0:T(128)S(1)}, f32[128]{0:T(128)}, u32[]{:S(2)}) copy-start(f32[128]{0:T(128)} %copy-done.37) | copy-start | bytes 1540
  956.1 123.4 %copy-start.6 = (f32[128,1152]{1,0:T(8,128)S(1)}, f32[128,1152]{1,0:T(8,128)}, u32[]{:S(2)}) copy-start(f32[128,1152]{1,0:T(8,128)} %copy-done.5) | copy-start | bytes 1769476
  956.1 123.4 %copy-start.42 = (f32[128]{0:T(128)S(1)}, f32[128]{0:T(128)}, u32[]{:S(2)}) copy-start(f32[128]{0:T(128)} %get-tuple-element.199) | copy-start | bytes 1540
  1071.2 9.3 copy-start.27
  1071.2 9.3 copy-start.28
  1071.2 9.3 copy-start.29
  1071.2 57.2 %collective-permute-start.5 = (f32[40,512]{1,0:T(8,128)S(1)}, f32[40,512]{1,0:T(8,128)S(1)}, u32[]{:S(2)}, u32[]{:S(2)}) collective-permute-start(f32[40,512]{1,0:T(8,128)S(1)} %fusion), channel_id=1, source_target_pairs={{0,3},{1,4},{2,5},{3,6},{4,7},{5,8},{6,9},{7,10},{8,11},{9,12},{10... | collective-permute-start | bytes 245768
  1072.6 55.8 %collective-permute-start.4 = (f32[40,512]{1,0:T(8,128)S(1)}, f32[40,512]{1,0:T(8,128)S(1)}, u32[]{:S(2)}, u32[]{:S(2)}) collective-permute-start(f32[40,512]{1,0:T(8,128)S(1)} %fusion), channel_id=1, source_target_pairs={{0,2},{1,3},{2,4},{3,5},{4,6},{5,7},{6,8},{7,9},{8,10},{9,11},{10,... | collective-permute-start | bytes 245768
  1073.9 54.5 %collective-permute-start.3 = (f32[40,512]{1,0:T(8,128)S(1)}, f32[40,512]{1,0:T(8,128)S(1)}, u32[]{:S(2)}, u32[]{:S(2)}) collective-permute-start(f32[40,512]{1,0:T(8,128)S(1)} %fusion), channel_id=1, source_target_pairs={{0,1},{1,2},{2,3},{3,4},{4,5},{5,6},{6,7},{7,8},{8,9},{9,10},{10,1... | collective-permute-start | bytes 245768
  1077.3 51.1 %collective-permute-start.6 = (f32[4,512]{1,0:T(4,128)S(1)}, f32[4,512]{1,0:T(4,128)S(1)}, u32[]{:S(2)}, u32[]{:S(2)}) collective-permute-start(f32[4,512]{1,0:T(4,128)S(1)} %slice.66), channel_id=1, source_target_pairs={{0,4},{1,5},{2,6},{3,7},{4,8},{5,9},{6,10},{7,11},{8,12},{9,13},{1... | collective-permute-start | bytes 24584
  (16 other events, 35.4 us)
Sparse Core Ops, SparseCore 0:
  58.5 30.8 all-gather.17
  92.2 53.4 all-gather.39
  155.0 28.0 all-gather.19
  184.8 28.1 all-gather.21
  227.5 48.0 reduce-scatter.14
  277.3 35.9 all-gather.25
  315.5 30.4 all-gather.23
  347.8 35.5 all-gather.27
  385.3 36.4 all-gather.29
  428.7 48.0 reduce-scatter.16
  482.5 29.9 all-gather.31
  529.8 47.1 reduce-scatter.18
  583.2 29.9 all-gather.33
  614.9 27.4 all-gather.35
  644.1 28.1 all-gather.37
  690.9 21.6 reduce-scatter.32
  715.9 50.7 reduce-scatter.26
  769.9 51.0 reduce-scatter.28
  824.4 51.0 reduce-scatter.30
  878.5 34.3 reduce-scatter.22
  916.0 34.3 reduce-scatter.24
  952.7 72.0 reduce-scatter.20
where the time goes:
time: 1140 us
  waiting for transfers between devices  674 us (59%)
  blocking collectives  240 us (21%)
  matrix products  113 us (10%)
  other arithmetic  59.5 us (5%)
  local copies, waits for them, and re-layouts  21.3 us (2%)
  between operations  16.8 us (1%)
  starting transfers between devices  11.4 us (1%)
    unnamed x3, blocking collectives  202 us
    reduce_scatter x4, waiting for transfers between devices, reduce_rows(): return lax.psum_scatter(values, 'tensor', scatter_dimension=0, tiled=True)  141 us
    all_gather x4, waiting for transfers between devices, gather_rows(): return lax.all_gather(values, 'tensor', axis=0, tiled=True)  110 us
    all_gather x1, waiting for transfers between devices, per_device(): lax.all_gather(w_keyval, ('dp', 'tensor'), axis=0, tiled=True)  53.7 us
    reduce_scatter x1, waiting for transfers between devices, per_device(): lax.psum_scatter(grad_w_down.astype(jnp.bfloat16), 'dp', scatter_dimensio...  52.4 us
    reduce_scatter x1, waiting for transfers between devices, per_device(): lax.psum_scatter(grad_w_up.astype(jnp.bfloat16), 'dp', scatter_dimension=...  52.3 us
    all_gather x2, waiting for transfers between devices, fold_keys(): lax.all_gather(part, 'dp', axis=0, tiled=True)  40.5 us
    dot_general x9, matrix products, contract_last(): lax.dot_general(left, right, (((1,), (1,)), ((), ())), preferred_element_...  37 us
  transfers between devices with their start and end apart: 29, of which 20 were waited for; matrix products, arithmetic and copies ran while one was open for 19% of the time, Pallas kernels for 0%

commit v1 on v0

v1 whole, which is shorter than its diff:
```python
import jax
import jax.numpy as jnp
from jax import lax
from jax.sharding import PartitionSpec as P

HD = 256

EPSILON = 1e-06
ROPE_BASE = 1000000.0
QUERY_SCALE = 0.0625
MASKED = -1e30
GELU_COEF = 0.7978845608028654
GELU_CUBIC = 0.044715
BF = jnp.bfloat16
F32 = jnp.float32


def rms_inverse(values):
    return lax.rsqrt(jnp.mean(values * values, axis=-1, keepdims=True) + EPSILON)


def rms_backward(values, inverse, scales, upstream):
    weighted = upstream * scales
    inner_mean = jnp.mean(values * weighted, axis=-1, keepdims=True)
    grad_values = inverse * weighted - values * (inverse * inverse * inverse) * inner_mean
    grad_scales = jnp.sum(upstream * values * inverse, axis=0)
    return (grad_values, grad_scales)


def gelu_pair(values):
    inside = GELU_COEF * (values + GELU_CUBIC * values * values * values)
    tangent = jnp.tanh(inside)
    output = 0.5 * values * (1.0 + tangent)
    derivative = 0.5 * (1.0 + tangent) + 0.5 * values * (1.0 - tangent * tangent) * GELU_COEF * (
        1.0 + 3.0 * GELU_CUBIC * values * values
    )
    return (output, derivative)


def rotate_half(values):
    halfway = values.shape[-1] // 2
    return jnp.concatenate([-values[..., halfway:], values[..., :halfway]], axis=-1)


def rope_tables(positions):
    halfway = HD // 2
    frequency = ROPE_BASE ** (-2.0 * jnp.arange(halfway, dtype=F32) / HD)
    angles = positions.astype(F32)[:, None] * frequency[None, :]
    angles = jnp.concatenate([angles, angles], axis=1)
    return (jnp.cos(angles), jnp.sin(angles))


def apply_rope(values, cosine, sine_part):
    return values * cosine + rotate_half(values) * sine_part


def rope_back(upstream, cosine, sine_part):
    return upstream * cosine - rotate_half(upstream * sine_part)


def dot(left, right):
    return jnp.dot(left, right, preferred_element_type=F32)


def contract_first(left, right):
    return lax.dot_general(left, right, (((0,), (0,)), ((), ())), preferred_element_type=F32)


def contract_last(left, right):
    return lax.dot_general(left, right, (((1,), (1,)), ((), ())), preferred_element_type=F32)


def ring(value, steps):
    count = lax.axis_size("tensor")
    return lax.ppermute(value, "tensor", [(s, (s + steps) % count) for s in range(count)])


def swap(value, mask):
    count = lax.axis_size("dp")
    return lax.ppermute(value, "dp", [(s, s ^ mask) for s in range(count)])


def gather_rows(values):
    count = lax.axis_size("tensor")
    return jnp.concatenate([values] + [ring(values, k) for k in range(1, count)], axis=0)


def scatter_rows(partial):
    count = lax.axis_size("tensor")
    length = partial.shape[0] // count
    total = partial[:length]
    for k in range(1, count):
        piece = partial[k * length : (k + 1) * length].astype(BF)
        total = total + ring(piece, -k).astype(F32)
    return total


def gather_blocks(values):
    count = lax.axis_size("dp")
    near = [values] + [swap(values, 2 * k) for k in range(1, count // 2)]
    far = [swap(piece, 1) for piece in near]
    return jnp.stack(near + far)


def block_order():
    count = lax.axis_size("dp")
    return [2 * k for k in range(count // 2)] + [2 * k + 1 for k in range(count // 2)]


def scatter_blocks(blocks):
    count = lax.axis_size("dp")
    own = lax.axis_index("dp")

    def pick(mask):
        return lax.dynamic_index_in_dim(blocks, own ^ mask, 0, keepdims=False)

    far = swap(jnp.stack([pick(2 * k + 1) for k in range(count // 2)]), 1).astype(F32)
    paired = [far[k] + pick(2 * k).astype(F32) for k in range(count // 2)]
    total = paired[0]
    for k in range(1, count // 2):
        total = total + swap(paired[k].astype(BF), 2 * k).astype(F32)
    return total


def three_terms(values):
    first = lax.reduce_precision(values, 8, 7)
    rest = values - first
    second = lax.reduce_precision(rest, 8, 7)
    third = lax.reduce_precision(rest - second, 8, 7)
    return jnp.concatenate([first, second, third]).astype(BF)


def with_vector(rows, vector):
    terms = three_terms(vector).reshape(-1, HD)
    padding = jnp.zeros((-terms.shape[0] % 16, HD), BF)
    return jnp.concatenate([rows, terms, padding], axis=0)


def split_vector(stacked, length):
    count = stacked.shape[0]
    extra = length // HD
    rows = stacked[:, :length].reshape(count * length, HD)
    terms = stacked[:, length : length + 3 * extra].astype(F32).reshape(count, 3, length)
    return rows, jnp.sum(terms, axis=1).reshape(count * length)


def per_device(
    block_in,
    out_grad,
    segments,
    w_query,
    w_keyval,
    w_out,
    w_gate,
    w_up,
    w_down,
    gain_pre_attn,
    gain_post_attn,
    gain_pre_ffn,
    gain_post_ffn,
    gain_query,
    gain_key,
):
    splits = lax.axis_size("tensor")
    blocks = lax.axis_size("dp")
    row_count, width = block_in.shape
    block_len = row_count * splits
    own_block = lax.axis_index("dp")
    own_part = lax.axis_index("tensor")
    small_rows = w_keyval.shape[0]
    weight_rows = w_query.shape[0]
    big = gain_pre_attn.shape[0]
    little = gain_query.shape[0]
    per_owner = 4 * big + 2 * little

    inv_in = rms_inverse(block_in)
    unit_in = block_in * inv_in
    unit_all = gather_rows(unit_in.astype(BF))
    gains_own = jnp.concatenate(
        [gain_pre_attn, gain_post_attn, gain_pre_ffn, gain_post_ffn, gain_query, gain_key]
    )
    gains_row = jnp.pad(gains_own, (0, 2 * HD - per_owner))[None, :]
    small = jnp.concatenate([w_keyval, gains_row], axis=0)
    small = lax.all_gather(small, "tensor", axis=0, tiled=False)
    keyval_rows = small[:, :small_rows].reshape(weight_rows, 2 * HD)
    gains_rows = jnp.pad(
        small[:, small_rows, :per_owner].reshape(-1), (0, 4 * HD - splits * per_owner)
    )[None, :]
    packed = jnp.concatenate([w_query, w_out.T, keyval_rows], axis=1)
    packed = jnp.concatenate([packed, gains_rows, jnp.zeros((7, 4 * HD), BF)], axis=0)
    w_gate, w_up, w_down, packed = lax.optimization_barrier((w_gate, w_up, w_down, packed))
    packed = lax.all_gather(packed, "dp", axis=0, tiled=False)
    weights_in = packed[:, :weight_rows]
    query_full = weights_in[:, :, :HD].reshape(width, HD)
    out_full = weights_in[:, :, HD : 2 * HD].reshape(width, HD)
    keyval_full = weights_in[:, :, 2 * HD :].reshape(width, 2 * HD)
    gains = packed[:, weight_rows, : splits * per_owner].astype(F32)
    gains = gains.reshape(blocks * splits, per_owner)
    scale_pre_attn = gains[:, :big].reshape(width)
    scale_post_attn = gains[:, big : 2 * big].reshape(width)
    scale_pre_ffn = gains[:, 2 * big : 3 * big].reshape(width)
    scale_post_ffn = gains[:, 3 * big : 4 * big].reshape(width)
    scale_query = gains[:, 4 * big : 4 * big + little].reshape(HD)
    scale_key = gains[:, 4 * big + little :].reshape(HD)
    gate_full = lax.all_gather(w_gate, "dp", axis=0, tiled=True)
    up_full = lax.all_gather(w_up, "dp", axis=0, tiled=True)
    down_full = lax.all_gather(w_down, "dp", axis=1, tiled=True)

    part_order = [(own_part - k) % splits for k in range(splits)]
    offsets = jnp.concatenate(
        [part * row_count + jnp.arange(row_count, dtype=jnp.int32) for part in part_order]
    )
    seg_parts = segments.reshape(blocks, splits, row_count)
    seg_parts = jnp.concatenate(
        [lax.dynamic_index_in_dim(seg_parts, part, 1, keepdims=False) for part in part_order], axis=1
    )
    own_segment = lax.dynamic_index_in_dim(seg_parts, own_block, 0, keepdims=False)
    own_index = own_block * block_len + offsets
    order = block_order()
    all_segment = jnp.concatenate(
        [lax.dynamic_index_in_dim(seg_parts, own_block ^ m, 0, keepdims=False) for m in order]
    )
    all_index = jnp.concatenate([(own_block ^ m) * block_len + offsets for m in order])

    gathered_in = (unit_all.astype(F32) * scale_pre_attn).astype(BF)
    queries = dot(gathered_in, query_full)
    keyval = dot(gathered_in, keyval_full)
    cosine, sine_part = rope_tables(own_index)
    key_proj = keyval[:, :HD]
    inv_key = rms_inverse(key_proj)
    key_rot = apply_rope(key_proj * inv_key * scale_key, cosine, sine_part).astype(BF)
    value_proj = keyval[:, HD:].astype(BF)
    keyval_all = gather_blocks(jnp.concatenate([key_rot, value_proj], axis=1))
    key_all = keyval_all[:, :, :HD].reshape(blocks * block_len, HD)
    value_all = keyval_all[:, :, HD:].reshape(blocks * block_len, HD)
    inv_query = rms_inverse(queries)
    query_rot = (
        apply_rope(queries * inv_query * scale_query, cosine, sine_part) * QUERY_SCALE
    ).astype(BF)

    visible = (own_segment[:, None] == all_segment[None, :]) & (
        all_index[None, :] <= own_index[:, None]
    )
    scores = jnp.where(visible, contract_last(query_rot, key_all), MASKED)
    row_max = jnp.max(scores, axis=1)
    weights = jnp.where(visible, jnp.exp(scores - row_max[:, None]), 0.0)
    row_sum = jnp.sum(weights, axis=1)
    row_acc = dot(weights.astype(BF), value_all)
    log_norm = row_max + jnp.log(row_sum)
    mixed = (row_acc / row_sum[:, None]).astype(BF)
    query_part = gather_blocks(with_vector(query_rot, log_norm))
    attn_out = scatter_rows(contract_last(mixed, out_full))
    inv_attn = rms_inverse(attn_out)
    resid_mid = block_in + attn_out * inv_attn * scale_post_attn

    inv_mid = rms_inverse(resid_mid)
    gathered_mid = gather_rows((resid_mid * inv_mid * scale_pre_ffn).astype(BF))
    gate_pre = dot(gathered_mid, gate_full)
    up_proj = dot(gathered_mid, up_full)
    gate_act, gate_deriv = gelu_pair(gate_pre)
    hidden = (gate_act * up_proj).astype(BF)
    ffn_out = scatter_rows(dot(hidden, down_full))
    inv_ffn = rms_inverse(ffn_out)
    block_out = resid_mid + ffn_out * inv_ffn * scale_post_ffn
    grad_ffn, grad_post_ffn = rms_backward(ffn_out, inv_ffn, scale_post_ffn, out_grad)
    grad_ffn_all = gather_rows(grad_ffn.astype(BF))
    grad_hidden = contract_last(grad_ffn_all, down_full)
    grad_gate = (grad_hidden * up_proj * gate_deriv).astype(BF)
    grad_up = (grad_hidden * gate_act).astype(BF)
    grad_mid = scatter_rows(contract_last(grad_gate, gate_full) + contract_last(grad_up, up_full))
    grad_w_down = contract_first(hidden, grad_ffn_all).astype(BF)
    owned_down = lax.psum_scatter(grad_w_down, "dp", scatter_dimension=1, tiled=True)
    grad_w_gate = contract_first(gathered_mid, grad_gate).astype(BF)
    owned_gate = lax.psum_scatter(grad_w_gate, "dp", scatter_dimension=0, tiled=True)
    grad_w_up = contract_first(gathered_mid, grad_up).astype(BF)
    owned_up = lax.psum_scatter(grad_w_up, "dp", scatter_dimension=0, tiled=True)
    grad_resid, grad_pre_ffn = rms_backward(resid_mid, inv_mid, scale_pre_ffn, grad_mid)
    grad_resid_mid = out_grad + grad_resid

    grad_attn, grad_post_attn = rms_backward(attn_out, inv_attn, scale_post_attn, grad_resid_mid)
    grad_attn_all = gather_rows(grad_attn.astype(BF))
    grad_mixed = dot(grad_attn_all, out_full).astype(BF)
    delta = jnp.sum(grad_mixed.astype(F32) * mixed.astype(F32), axis=1)
    grad_part = gather_blocks(with_vector(grad_mixed, delta))
    grad_w_out = contract_first(grad_attn_all, mixed).astype(BF)
    owned_out = lax.psum_scatter(grad_w_out, "dp", scatter_dimension=0, tiled=True)

    scores = contract_last(query_rot, key_all)
    weights = jnp.where(visible, jnp.exp(scores - log_norm[:, None]), 0.0)
    grad_prob = contract_last(grad_mixed, value_all)
    grad_score = (weights * (grad_prob - delta[:, None])).astype(BF)
    grad_query_rot = dot(grad_score, key_all)

    part_query, part_log = split_vector(query_part, block_len)
    part_grad, part_delta = split_vector(grad_part, block_len)
    shown = (own_segment[:, None] == all_segment[None, :]) & (
        own_index[:, None] <= all_index[None, :]
    )
    scores = contract_last(key_rot, part_query)
    weights = jnp.where(shown, jnp.exp(scores - part_log[None, :]), 0.0)
    grad_prob = contract_last(value_proj, part_grad)
    grad_score = (weights * (grad_prob - part_delta[None, :])).astype(BF)
    grad_keyval_part = jnp.concatenate(
        [dot(grad_score, part_query), dot(weights.astype(BF), part_grad)], axis=1
    )
    grad_keyval_rows = scatter_rows(grad_keyval_part)

    grad_query_norm = rope_back(grad_query_rot, cosine, sine_part) * QUERY_SCALE
    grad_queries, grad_gain_query = rms_backward(queries, inv_query, scale_query, grad_query_norm)
    grad_query_bf = grad_queries.astype(BF)
    grad_w_query = contract_first(gathered_in, grad_query_bf)
    grad_key_norm = rope_back(grad_keyval_rows[:, :HD], cosine[:row_count], sine_part[:row_count])
    grad_key_proj, grad_gain_key = rms_backward(
        key_proj[:row_count], inv_key[:row_count], scale_key, grad_key_norm
    )
    grad_keyval_bf = jnp.concatenate([grad_key_proj, grad_keyval_rows[:, HD:]], axis=1).astype(BF)
    grad_w_keyval = contract_first(gathered_in, gather_rows(grad_keyval_bf))
    normed_query = contract_last(grad_query_bf, query_full)
    normed_keyval = contract_last(grad_keyval_bf, keyval_full)
    grad_pre_attn = jnp.sum(normed_query * unit_all.astype(F32), axis=0) + jnp.sum(
        normed_keyval * unit_in, axis=0
    )
    grad_normed = scatter_rows(normed_query) + normed_keyval
    grad_in_norm, _ = rms_backward(block_in, inv_in, scale_pre_attn, grad_normed)
    grad_in = grad_resid_mid + grad_in_norm

    gain_grads = jnp.concatenate(
        [
            g.reshape(blocks, splits, -1)
            for g in (
                grad_pre_attn,
                grad_post_attn,
                grad_pre_ffn,
                grad_post_ffn,
                grad_gain_query,
                grad_gain_key,
            )
        ],
        axis=2,
    )

    def gains_of(part):
        return lax.dynamic_index_in_dim(gain_grads, part, 1, keepdims=False)

    gains_sum = gains_of(own_part)
    for k in range(1, splits):
        gains_sum = gains_sum + ring(gains_of((own_part - k) % splits), -k)
    gains_high = lax.reduce_precision(gains_sum, 8, 7)
    gains_pair = jnp.stack([gains_high, gains_sum - gains_high], axis=1).astype(BF)
    gains_pair = jnp.pad(gains_pair, ((0, 0), (0, 6), (0, HD - per_owner)))
    keyval_own = lax.dynamic_index_in_dim(
        grad_w_keyval.astype(BF).reshape(blocks, splits, small_rows, 2 * HD),
        own_part,
        1,
        keepdims=False,
    )
    owned = scatter_blocks(
        jnp.concatenate(
            [
                grad_w_query.astype(BF).reshape(blocks, weight_rows, HD),
                keyval_own[:, :, :HD],
                keyval_own[:, :, HD:],
                gains_pair,
            ],
            axis=1,
        )
    )
    owned_query = owned[:weight_rows]
    after = weight_rows + small_rows
    owned_keyval = jnp.concatenate(
        [owned[weight_rows:after], owned[after : after + small_rows]], axis=1
    )
    after = after + small_rows
    owned_gains = owned[after, :per_owner] + owned[after + 1, :per_owner]
    return (
        block_out,
        grad_in,
        owned_query,
        owned_keyval,
        owned_out.astype(F32).T,
        owned_gate.astype(F32),
        owned_up.astype(F32),
        owned_down.astype(F32),
        owned_gains[:big],
        owned_gains[big : 2 * big],
        owned_gains[2 * big : 3 * big],
        owned_gains[3 * big : 4 * big],
        owned_gains[4 * big : 4 * big + little],
        owned_gains[4 * big + little :],
    )


def solution(mesh):
    return jax.shard_map(
        per_device,
        mesh=mesh,
        in_specs=(
            P(("dp", "tensor"), None),
            P(("dp", "tensor"), None),
            P(),
            P("dp", "tensor"),
            P(("dp", "tensor"), None),
            P("tensor", "dp"),
            P("dp", "tensor"),
            P("dp", "tensor"),
            P("tensor", "dp"),
            P(("dp", "tensor")),
            P(("dp", "tensor")),
            P(("dp", "tensor")),
            P(("dp", "tensor")),
            P(("dp", "tensor")),
            P(("dp", "tensor")),
        ),
        out_specs=(
            P(("dp", "tensor"), None),
            P(("dp", "tensor"), None),
            P("dp", "tensor"),
            P(("dp", "tensor"), None),
            P("tensor", "dp"),
            P("dp", "tensor"),
            P("dp", "tensor"),
            P("tensor", "dp"),
            P(("dp", "tensor")),
            P(("dp", "tensor")),
            P(("dp", "tensor")),
            P(("dp", "tensor")),
            P(("dp", "tensor")),
            P(("dp", "tensor")),
        ),
        check_vma=False,
    )
```

time: 1140 us -> 580 us (0.51)
  waiting for transfers between devices: 674 us -> 246 us
  blocking collectives: 240 us -> 15.1 us
  starting transfers between devices: 11.4 us -> 80.7 us
  local copies, waits for them, and re-layouts: 21.3 us -> 63.2 us
  other arithmetic: 59.5 us -> 41.9 us
    reduce_scatter x9 -> x4, waiting for transfers between devices: 344 us -> 9.22 us  [the longest x1 9.22 us: per_device(): lax.psum_scatter(grad_w_down, 'dp', scatter_dimension=1, tiled=True)]
    all_gather x12 -> x4, waiting for transfers between devices: 327 us -> 21.1 us  [the longest x1 21.1 us: per_device(): packed = lax.all_gather(packed, 'dp', axis=0, tiled=False)]
    ppermute x3 -> x58, waiting for transfers between devices: 0.01 us -> 214 us  [the longest x33 141 us: ring(): lax.ppermute(value, 'tensor', [(s, (s + steps) % count) for s in range(co...]
    unnamed x3 -> x0, blocking collectives: 202 us -> none
    ppermute x3 -> x58, starting transfers between devices: 3.19 us -> 80 us  [the longest x33 64.9 us: ring(): lax.ppermute(value, 'tensor', [(s, (s + steps) % count) for s in range(co...]
    another operation x0 -> x17, local copies, waits for them, and re-layouts: none -> 26.1 us  [the longest x11 24.9 us: gather_blocks(): return jnp.stack(near + far)]
    dot_general x6 -> x10, matrix products: 29.2 us -> 53.8 us  [dot(): return jnp.dot(left, right, preferred_element_type=F32)]
    all_gather x4 -> x1, blocking collectives: 38.5 us -> 15.1 us  [per_device(): small = lax.all_gather(small, 'tensor', axis=0, tiled=False)]
  transfers between devices with their start and end apart: 29 -> 66, of which waited for: 20 -> 33; matrix products, arithmetic and copies ran while one was open for 19% -> 29% of each run, Pallas kernels for 0% -> 0%
where the time goes in v1:
time: 580 us; the launch traced here: 570 us
  waiting for transfers between devices  246 us (42%)
  matrix products  106 us (18%)
  starting transfers between devices  80.7 us (14%)
  local copies, waits for them, and re-layouts  63.2 us (11%)
  other arithmetic  41.9 us (7%)
  between operations  16.6 us (3%)
  blocking collectives  15.1 us (3%)
    ppermute x33, waiting for transfers between devices, ring(): lax.ppermute(value, 'tensor', [(s, (s + steps) % count) for s in range(co...  141 us
    ppermute x25, waiting for transfers between devices, swap(): return lax.ppermute(value, 'dp', [(s, s ^ mask) for s in range(count)])  73.6 us
    ppermute x33, starting transfers between devices, ring(): lax.ppermute(value, 'tensor', [(s, (s + steps) % count) for s in range(co...  64.9 us
    dot_general x10, matrix products, dot(): return jnp.dot(left, right, preferred_element_type=F32)  53.8 us
    dot_general x8, matrix products, contract_last(): lax.dot_general(left, right, (((1,), (1,)), ((), ())), preferred_element_...  29.4 us
    another operation x11, local copies, waits for them, and re-layouts, gather_blocks(): return jnp.stack(near + far)  24.9 us
    dot_general x6, matrix products, contract_first(): lax.dot_general(left, right, (((0,), (0,)), ((), ())), preferred_element_...  22.6 us
    all_gather x1, waiting for transfers between devices, per_device(): packed = lax.all_gather(packed, 'dp', axis=0, tiled=False)  21.1 us
  transfers between devices with their start and end apart: 66, of which 33 were waited for; matrix products, arithmetic and copies ran while one was open for 29% of the time, Pallas kernels for 0%

profile of v1, /device:TPU:0, one launch (start us, length us, event | category | flops | bytes accessed | tf_op | source)
XLA Modules:
  0.0 569.5 jit_solution(2342351882694654727)
XLA Ops:
  7.2 4.2 concatenate.99
  12.2 15.1 %all-gather.2 = bf16[4,37,512]{2,1,0:T(8,128)(2,1)S(1)} all-gather(bf16[1,37,512]{2,1,0:T(8,128)(2,1)S(1)} %maximum_bitcast_fusion), channel_id=2, replica_groups=mesh['dp'=8,'tensor'=4] {'tensor'}, dimensions={0}, use_global_device_ids=true | all-gather | bytes 189440 | tf_op jit(solution)/shard_map/all_gather | solution.py:184
  31.7 3.9 collective-permute-start.2
  39.5 21.1 %all-gather.14.cloned.1.call-done = bf16[1216,1024]{1,0:T(8,128)(2,1)} async-done(((bf16[152,1024]{1,0:T(8,128)(2,1)}), bf16[1216,1024]{1,0:T(8,128)(2,1)}) %all-gather.14.cloned.1.call-update) | async-done | bytes 2490384 | tf_op jit(solution)/shard_map/all_gather | solution.py:192
  79.7 15.6 %collective-permute-done.3 = bf16[512,512]{1,0:T(8,128)(2,1)S(1)} collective-permute-done((bf16[512,512]{1,0:T(8,128)(2,1)S(1)}, bf16[512,512]{1,0:T(8,128)(2,1)S(1)}, u32[]{:S(2)}, u32[]{:S(2)}) %collective-permute-start.3) | collective-permute-done | bytes 524320 | tf_op jit(solution)/shard_map/ppermute | solution.py:80
  95.4 4.9 collective-permute-done.4
  100.3 12.9 %collective-permute-done.5 = bf16[512,512]{1,0:T(8,128)(2,1)S(1)} collective-permute-done((bf16[512,512]{1,0:T(8,128)(2,1)S(1)}, bf16[512,512]{1,0:T(8,128)(2,1)S(1)}, u32[]{:S(2)}, u32[]{:S(2)}) %collective-permute-start.5) | collective-permute-done | bytes 524320 | tf_op jit(solution)/shard_map/ppermute | solution.py:80
  115.9 2.3 fusion.8
  118.3 2.9 fusion
  121.6 3.4 fusion.25
  128.8 2.4 collective-permute-start.11
  133.3 5.8 %collective-permute-done.12 = bf16[128,1152]{1,0:T(8,128)(2,1)S(1)} collective-permute-done((bf16[128,1152]{1,0:T(8,128)(2,1)S(1)}, bf16[128,1152]{1,0:T(8,128)(2,1)S(1)}, u32[]{:S(2)}, u32[]{:S(2)}) %collective-permute-start.12) | collective-permute-done | bytes 294944 | tf_op jit(solution)/shard_map/ppermute | solution.py:75
  139.1 11.8 %collective-permute-done.11 = bf16[128,1152]{1,0:T(8,128)(2,1)S(1)} collective-permute-done((bf16[128,1152]{1,0:T(8,128)(2,1)S(1)}, bf16[128,1152]{1,0:T(8,128)(2,1)S(1)}, u32[]{:S(2)}, u32[]{:S(2)}) %collective-permute-start.11) | collective-permute-done | bytes 294944 | tf_op jit(solution)/shard_map/ppermute | solution.py:75
  153.7 7.7 %collective-permute-start.15 = (bf16[128,1152]{1,0:T(8,128)(2,1)S(1)}, bf16[128,1152]{1,0:T(8,128)(2,1)S(1)}, u32[]{:S(2)}, u32[]{:S(2)}) collective-permute-start(bf16[128,1152]{1,0:T(8,128)(2,1)S(1)} %multiply_convert_fusion.4), channel_id=1, source_target_pairs={{0,3},{1,0},{2,1},{3,2},{4,7},{5,4},{6,5},{7,6},{8,11},{9,8},{10,9... | collective-permute-start | bytes 884744 | tf_op jit(solution)/shard_map/ppermute | solution.py:75
  162.0 6.9 %collective-permute-done.15 = bf16[128,1152]{1,0:T(8,128)(2,1)S(1)} collective-permute-done((bf16[128,1152]{1,0:T(8,128)(2,1)S(1)}, bf16[128,1152]{1,0:T(8,128)(2,1)S(1)}, u32[]{:S(2)}, u32[]{:S(2)}) %collective-permute-start.15) | collective-permute-done | bytes 294944 | tf_op jit(solution)/shard_map/ppermute | solution.py:75
  168.9 18.9 %collective-permute-done.14 = bf16[128,1152]{1,0:T(8,128)(2,1)S(1)} collective-permute-done((bf16[128,1152]{1,0:T(8,128)(2,1)S(1)}, bf16[128,1152]{1,0:T(8,128)(2,1)S(1)}, u32[]{:S(2)}, u32[]{:S(2)}) %collective-permute-start.14) | collective-permute-done | bytes 294944 | tf_op jit(solution)/shard_map/ppermute | solution.py:75
  188.6 6.7 %fusion.99 = f32[512,1728]{0,1:T(8,128)} fusion(bf16[1152,1728]{1,0:T(8,128)(2,1)} %all-gather.8.cloned.1.call-done, bf16[128,1152]{1,0:T(8,128)(2,1)S(1)} %collective-permute-done.15, bf16[128,1152]{1,0:T(8,128)(2,1)} %copy-done.118, bf16[128,1152]{1,0:T(8,128)(2,1)} %collective-permute-done.13, bf16[128,1152]{1,0:T(8,128)(2,1)S(1)} %multiply_convert_fusion.4), kind=kOutput, calls=%fused_computation.286 | convolution fusion | flops 2043150336 | bytes 8699904 | tf_op jit(solution)/shard_map/dot_general | solution.py:62
  195.3 9.2 %multiply_convert_fusion.3 = (bf16[512,1728]{0,1:T(8,128)(2,1)}, f32[512,1728]{0,1:T(8,128)}) fusion(f32[512,1728]{0,1:T(8,128)} %fusion.99, bf16[1152,1728]{1,0:T(8,128)(2,1)} %all-gather.10.cloned.1.call-done, bf16[128,1152]{1,0:T(8,128)(2,1)S(1)} %collective-permute-done.15, bf16[128,1152]{1,0:T(8,128)(2,1)} %copy-done.118, ...), kind=kOutput, calls=%fused_computation.28 | convolution fusion | flops 2051997696 | bytes 14008320 | tf_op jit(solution)/shard_map/dot_general | solution.py:62
  204.5 6.7 %fusion.118 = (bf16[512,1152]{1,0:T(8,128)(2,1)S(1)}, f32[512,1152]{1,0:T(8,128)}) fusion(bf16[512,1728]{0,1:T(8,128)(2,1)} %get-tuple-element.147, bf16[1728,1152]{0,1:T(8,128)(2,1)} %all-gather.12.cloned.1.call-done), kind=kOutput, calls=%fused_computation.299 | convolution fusion | flops 2039021568 | bytes 9289728 | tf_op jit(solution)/shard_map/dot_general | solution.py:62
  212.3 3.6 collective-permute-start.16
  217.3 6.8 %collective-permute-done.18 = bf16[128,1152]{1,0:T(8,128)(2,1)S(1)} collective-permute-done((bf16[128,1152]{1,0:T(8,128)(2,1)}, bf16[128,1152]{1,0:T(8,128)(2,1)S(1)}, u32[]{:S(2)}, u32[]{:S(2)}) %collective-permute-start.18) | collective-permute-done | bytes 294944 | tf_op jit(solution)/shard_map/ppermute | solution.py:75
  224.2 10.9 %collective-permute-done.17 = bf16[128,1152]{1,0:T(8,128)(2,1)S(1)} collective-permute-done((bf16[128,1152]{1,0:T(8,128)(2,1)}, bf16[128,1152]{1,0:T(8,128)(2,1)S(1)}, u32[]{:S(2)}, u32[]{:S(2)}) %collective-permute-start.17) | collective-permute-done | bytes 294944 | tf_op jit(solution)/shard_map/ppermute | solution.py:75
  239.2 5.3 collective-permute-start.21
  244.5 2.1 collective-permute-start.20
  246.8 5.3 collective-permute-done.21
  252.0 19.5 %collective-permute-done.20 = bf16[128,1152]{1,0:T(8,128)(2,1)S(1)} collective-permute-done((bf16[128,1152]{1,0:T(8,128)(2,1)S(1)}, bf16[128,1152]{1,0:T(8,128)(2,1)S(1)}, u32[]{:S(2)}, u32[]{:S(2)}) %collective-permute-start.20) | collective-permute-done | bytes 294944 | tf_op jit(solution)/shard_map/ppermute | solution.py:75
  271.5 8.5 %multiply_convert_fusion.2 = (bf16[512,1728]{0,1:T(8,128)(2,1)S(1)}, bf16[512,1728]{0,1:T(8,128)(2,1)S(1)}) fusion(f32[512,1728]{0,1:T(8,128)} %fusion.99, f32[512,1728]{0,1:T(8,128)} %get-tuple-element.148, bf16[1728,1152]{0,1:T(8,128)(2,1)S(1)} %copy-done.100, bf16[128,1152]{1,0:T(8,128)(2,1)S(1)} %collective-permute-done.21, ...), kind=kOutput, calls=%fused_computation.27 | convolution fusion | flops 2063499264 | bytes 15777792 | tf_op jit(solution)/shard_map/dot_general | solution.py:70
  280.1 2.6 fusion.122
  283.5 2.6 fusion.119
  286.4 3.7 collective-permute-start.22
  290.1 8.0 %collective-permute-done.24 = bf16[128,1152]{1,0:T(8,128)(2,1)S(1)} collective-permute-done((bf16[128,1152]{1,0:T(8,128)(2,1)S(1)}, bf16[128,1152]{1,0:T(8,128)(2,1)S(1)}, u32[]{:S(2)}, u32[]{:S(2)}) %collective-permute-start.24) | collective-permute-done | bytes 294944 | tf_op jit(solution)/shard_map/ppermute | solution.py:75
  298.1 9.9 %collective-permute-done.23 = bf16[128,1152]{1,0:T(8,128)(2,1)S(1)} collective-permute-done((bf16[128,1152]{1,0:T(8,128)(2,1)S(1)}, bf16[128,1152]{1,0:T(8,128)(2,1)S(1)}, u32[]{:S(2)}, u32[]{:S(2)}) %collective-permute-start.23) | collective-permute-done | bytes 294944 | tf_op jit(solution)/shard_map/ppermute | solution.py:75
  310.1 7.1 %collective-permute-start.27 = (bf16[128,1152]{1,0:T(8,128)(2,1)S(1)}, bf16[128,1152]{1,0:T(8,128)(2,1)S(1)}, u32[]{:S(2)}, u32[]{:S(2)}) collective-permute-start(bf16[128,1152]{1,0:T(8,128)(2,1)S(1)} %subtract_convert_fusion), channel_id=1, source_target_pairs={{0,3},{1,0},{2,1},{3,2},{4,7},{5,4},{6,5},{7,6},{8,11},{9,8},{10,9... | collective-permute-start | bytes 884744 | tf_op jit(solution)/shard_map/ppermute | solution.py:75
  317.8 6.9 %collective-permute-done.27 = bf16[128,1152]{1,0:T(8,128)(2,1)S(1)} collective-permute-done((bf16[128,1152]{1,0:T(8,128)(2,1)S(1)}, bf16[128,1152]{1,0:T(8,128)(2,1)S(1)}, u32[]{:S(2)}, u32[]{:S(2)}) %collective-permute-start.27) | collective-permute-done | bytes 294944 | tf_op jit(solution)/shard_map/ppermute | solution.py:75
  324.6 17.8 %collective-permute-done.26 = bf16[128,1152]{1,0:T(8,128)(2,1)S(1)} collective-permute-done((bf16[128,1152]{1,0:T(8,128)(2,1)S(1)}, bf16[128,1152]{1,0:T(8,128)(2,1)S(1)}, u32[]{:S(2)}, u32[]{:S(2)}) %collective-permute-start.26) | collective-permute-done | bytes 294944 | tf_op jit(solution)/shard_map/ppermute | solution.py:75
  345.3 6.0 %convolution_convert_fusion.2 = bf16[1152,1728]{1,0:T(8,128)(2,1)} fusion(bf16[512,1728]{0,1:T(8,128)(2,1)} %copy-done.126, bf16[128,1152]{1,0:T(8,128)(2,1)S(1)} %copy-done.117, bf16[128,1152]{1,0:T(8,128)(2,1)S(1)} %copy-done.119, bf16[128,1152]{1,0:T(8,128)(2,1)} %collective-permute-done.13, bf16[128,1152]{1,0:T(8,128)(2,1)S(1)} %copy-done.28), kind=kOutput, calls=%fused_computation.8 | convolution fusion | flops 2045140992 | bytes 6930432 | tf_op jit(solution)/shard_map/dot_general | solution.py:66
  351.4 6.0 %convolution_convert_fusion.1 = bf16[1152,1728]{1,0:T(8,128)(2,1)} fusion(bf16[512,1728]{0,1:T(8,128)(2,1)} %copy-done.125, bf16[128,1152]{1,0:T(8,128)(2,1)S(1)} %copy-done.117, bf16[128,1152]{1,0:T(8,128)(2,1)S(1)} %copy-done.119, bf16[128,1152]{1,0:T(8,128)(2,1)} %collective-permute-done.13, bf16[128,1152]{1,0:T(8,128)(2,1)S(1)} %copy-done.28), kind=kOutput, calls=%fused_computation.7 | convolution fusion | flops 2045140992 | bytes 6930432 | tf_op jit(solution)/shard_map/dot_general | solution.py:66
  363.5 6.4 %collective-permute-done.31 = bf16[528,256]{1,0:T(8,128)(2,1)S(1)} collective-permute-done((bf16[528,256]{1,0:T(8,128)(2,1)S(1)}, bf16[528,256]{1,0:T(8,128)(2,1)S(1)}, u32[]{:S(2)}, u32[]{:S(2)}) %collective-permute-start.31) | collective-permute-done | bytes 270368 | tf_op jit(solution)/shard_map/ppermute | solution.py:80
  370.0 4.2 collective-permute-done.32
  377.8 6.3 %exponential_select_fusion = f32[512,4096]{1,0:T(8,128)} fusion(bf16[512,256]{1,0:T(8,128)(2,1)S(1)} %copy-done.13, bf16[4096,256]{1,0:T(8,128)(2,1)} %bitcast.166, f32[4096]{0:T(1024)S(1)} %bitcast.191, s32[4096]{0:T(1024)S(1)} %copy-done.66, s32[4096]{0:T(1024)S(1)} %copy-done.63, s32[512]{0:T(512)S(1)} %bitcast.187, s32[512]{0:T(512)S(1)} %copy-done.57), kind=kOutput, calls=%fused_computation.3 | convolution fusion | flops 1084227584 | bytes 10801152 | tf_op jit(solution)/shard_map/dot_general | solution.py:70
  384.3 5.9 %convolution_convert_fusion = bf16[1728,1152]{0,1:T(8,128)(2,1)} fusion(bf16[512,1728]{0,1:T(8,128)(2,1)} %get-tuple-element.147, bf16[128,1152]{1,0:T(8,128)(2,1)S(1)} %copy-done.112, bf16[128,1152]{1,0:T(8,128)(2,1)S(1)} %copy-done.114, bf16[128,1152]{1,0:T(8,128)(2,1)} %copy-done.115, bf16[128,1152]{1,0:T(8,128)(2,1)S(1)} %copy-done.30), kind=kOutput, calls=%fused_computation.6 | convolution fusion | flops 2045140992 | bytes 6930432 | tf_op jit(solution)/shard_map/dot_general | solution.py:66
  394.6 9.1 %fusion.77 = (f32[512,256]{1,0:T(8,128)S(1)}, f32[512,256]{1,0:T(8,128)S(1)}) fusion(f32[512,128]{1,0:T(8,128)S(1)} %copy-done.10, bf16[4096,256]{1,0:T(8,128)(2,1)} %bitcast.169, f32[512,4096]{1,0:T(8,128)} %copy-done.1, bf16[512,256]{0,1:T(8,128)(2,1)S(1)} %get-tuple-element.154, bf16[4096,256]{1,0:T(8,128)(2,1)} %bitcast.171, f32[512]{0:T(512)} %copy-done.93, ...), kind=kOutput, calls=%fused_computation.178 | convolution fusion | flops 2164523008 | bytes 14196736 | tf_op jit(solution)/shard_map/dot_general | solution.py:62
  409.6 3.8 multiply_reduce_fusion.12
  413.8 2.6 fusion.17
  416.4 6.9 %collective-permute-done.38 = bf16[528,256]{0,1:T(8,128)(2,1)} collective-permute-done((bf16[528,256]{0,1:T(8,128)(2,1)S(1)}, bf16[528,256]{0,1:T(8,128)(2,1)}, u32[]{:S(2)}, u32[]{:S(2)}) %collective-permute-start.38) | collective-permute-done | bytes 270368 | tf_op jit(solution)/shard_map/ppermute | solution.py:80
  423.3 2.5 collective-permute-done.39
  425.8 8.9 %collective-permute-done.40 = bf16[528,256]{0,1:T(8,128)(2,1)} collective-permute-done((bf16[528,256]{0,1:T(8,128)(2,1)S(1)}, bf16[528,256]{0,1:T(8,128)(2,1)}, u32[]{:S(2)}, u32[]{:S(2)}) %collective-permute-start.40) | collective-permute-done | bytes 270368 | tf_op jit(solution)/shard_map/ppermute | solution.py:80
  438.0 2.0 copy.229
  442.1 2.1 copy.231
  445.6 2.1 copy.232
  451.4 11.8 %stack.126 = bf16[8,528,256]{2,0,1:T(8,128)(2,1)S(1)} concatenate(bf16[1,528,256]{2,0,1:T(2,128)(2,1)} %copy.228, bf16[1,528,256]{2,0,1:T(2,128)(2,1)} %copy.229, bf16[1,528,256]{2,0,1:T(2,128)(2,1)} %copy.230, bf16[1,528,256]{2,0,1:T(2,128)(2,1)} %copy.231, bf16[1,528,256]{2,0,1:T(2,128)(2,1)} %copy.232, bf16[1,528,256]{2,0,1:T(2,128)(2,1)} %copy.233, ...), dimensions={0} | concatenate | bytes 4325376 | tf_op jit(solution)/shard_map/stack | solution.py:102
  463.9 5.5 fusion.4
  469.3 8.1 %fusion.20 = f32[512,256]{1,0:T(8,128)} fusion(bf16[4096,256]{1,0:T(8,128)(2,1)} %bitcast.167, f32[512,4096]{1,0:T(8,128)} %exponential_select_fusion, bf16[4096,256]{1,0:T(8,128)(2,1)S(1)} %bitcast.158, f32[4096]{0:T(1024)S(1)} %bitcast.190, f32[512,512]{1,0:T(8,128)} %copy-done.8), kind=kOutput, calls=%fused_computation.49 | convolution fusion | flops 2153775104 | bytes 13385728 | tf_op jit(solution)/shard_map/dot_general | solution.py:62
  488.9 4.2 collective-permute-done.46
  498.0 9.5 %collective-permute-start.50 = (bf16[128,512]{1,0:T(8,128)(2,1)S(1)}, bf16[128,512]{1,0:T(8,128)(2,1)}, u32[]{:S(2)}, u32[]{:S(2)}) collective-permute-start(bf16[128,512]{1,0:T(8,128)(2,1)S(1)} %pad_maximum_fusion.12), channel_id=1, source_target_pairs={{0,3},{1,0},{2,1},{3,2},{4,7},{5,4},{6,5},{7,6},{8,11},{9,8},{10,9... | collective-permute-start | bytes 393224 | tf_op jit(solution)/shard_map/ppermute | solution.py:75
  507.6 2.4 multiply_reduce_fusion.3
  512.5 2.4 collective-permute-start.52
  514.9 2.8 collective-permute-start.51
  519.2 6.0 %collective-permute-done.48 = bf16[128,512]{1,0:T(8,128)(2,1)S(1)} collective-permute-done((bf16[128,512]{1,0:T(8,128)(2,1)S(1)}, bf16[128,512]{1,0:T(8,128)(2,1)S(1)}, u32[]{:S(2)}, u32[]{:S(2)}) %collective-permute-start.48) | collective-permute-done | bytes 131104 | tf_op jit(solution)/shard_map/ppermute | solution.py:75
  536.9 4.3 collective-permute-done.57
  547.1 2.1 convert_element_type.280
  549.1 2.1 convert_element_type.282
  551.2 9.2 %reduce-scatter.11.cloned.1.call-done = bf16[1728,144]{0,1:T(8,128)(2,1)} async-done(((bf16[1728,1152]{0,1:T(8,128)(2,1)}), bf16[1728,144]{0,1:T(8,128)(2,1)}) %reduce-scatter.11.cloned.1.call-update) | async-done | bytes 497680 | tf_op jit(solution)/shard_map/reduce_scatter | solution.py:272
  560.4 2.1 convert_element_type.284
  (541 shorter events, 122.8 us)
Async XLA Ops:
  7.2 53.4 %all-gather.14.cloned.1.call-start = ((), (), s32[]{:S(2)}) async-start(), calls=%async_computation.11 | async-start | bytes 2801664 | tf_op jit(solution)/shard_map/all_gather | solution.py:192
  29.4 159.1 %all-gather.8.cloned.1.call-start = ((), (), s32[]{:S(2)}) async-start(), calls=%async_computation.4 | async-start | bytes 4644864 | tf_op jit(solution)/shard_map/all_gather | solution.py:205
  30.2 165.1 %all-gather.10.cloned.1.call-start = ((), (), s32[]{:S(2)}) async-start(), calls=%async_computation.5 | async-start | bytes 4644864 | tf_op jit(solution)/shard_map/all_gather | solution.py:206
  30.9 173.6 %all-gather.12.cloned.1.call-start = ((), (), s32[]{:S(2)}) async-start(), calls=%async_computation.6 | async-start | bytes 4644864 | tf_op jit(solution)/shard_map/all_gather | solution.py:207
  31.7 33.0 %collective-permute-start.2 = (bf16[128,1152]{1,0:T(8,128)(2,1)S(1)}, bf16[128,1152]{1,0:T(8,128)(2,1)S(1)}, u32[]{:S(2)}, u32[]{:S(2)}) collective-permute-start(bf16[128,1152]{1,0:T(8,128)(2,1)S(1)} %multiply_convert_fusion.5), channel_id=1, source_target_pairs={{0,3},{1,0},{2,1},{3,2},{4,7},{5,4},{6,5},{7,6},{8,11},{9,8},{10,9... | collective-permute-start | bytes 884744 | tf_op jit(solution)/shard_map/ppermute | solution.py:75
  35.6 29.1 %collective-permute-start.1 = (bf16[128,1152]{1,0:T(8,128)(2,1)S(1)}, bf16[128,1152]{1,0:T(8,128)(2,1)S(1)}, u32[]{:S(2)}, u32[]{:S(2)}) collective-permute-start(bf16[128,1152]{1,0:T(8,128)(2,1)S(1)} %multiply_convert_fusion.5), channel_id=1, source_target_pairs={{0,2},{1,3},{2,0},{3,1},{4,6},{5,7},{6,4},{7,5},{8,10},{9,11},{10,... | collective-permute-start | bytes 884744 | tf_op jit(solution)/shard_map/ppermute | solution.py:75
  35.6 29.2 %collective-permute-start = (bf16[128,1152]{1,0:T(8,128)(2,1)S(1)}, bf16[128,1152]{1,0:T(8,128)(2,1)S(1)}, u32[]{:S(2)}, u32[]{:S(2)}) collective-permute-start(bf16[128,1152]{1,0:T(8,128)(2,1)S(1)} %multiply_convert_fusion.5), channel_id=1, source_target_pairs={{0,1},{1,2},{2,3},{3,0},{4,5},{5,6},{6,7},{7,4},{8,9},{9,10},{10,1... | collective-permute-start | bytes 884744 | tf_op jit(solution)/shard_map/ppermute | solution.py:75
  36.2 499.1 %reduce-scatter.5.cloned.1.call-start = ((), (), s32[]{:S(2)}) async-start(), calls=%async_computation.7 | async-start | bytes 663552 | tf_op jit(solution)/shard_map/reduce_scatter | solution.py:286
  75.9 19.5 %collective-permute-start.3 = (bf16[512,512]{1,0:T(8,128)(2,1)S(1)}, bf16[512,512]{1,0:T(8,128)(2,1)S(1)}, u32[]{:S(2)}, u32[]{:S(2)}) collective-permute-start(bf16[512,512]{1,0:T(8,128)(2,1)S(1)} %pad_maximum_fusion.6), channel_id=1, source_target_pairs={{0,8},{4,12},{8,0},{12,4},{16,24},{20,28},{24,16},{28,20},{1,9},{5... | collective-permute-start | bytes 1572872 | tf_op jit(solution)/shard_map/ppermute | solution.py:80
  77.5 22.8 %collective-permute-start.4 = (bf16[512,512]{1,0:T(8,128)(2,1)S(1)}, bf16[512,512]{1,0:T(8,128)(2,1)S(1)}, u32[]{:S(2)}, u32[]{:S(2)}) collective-permute-start(bf16[512,512]{1,0:T(8,128)(2,1)S(1)} %pad_maximum_fusion.6), channel_id=1, source_target_pairs={{0,16},{4,20},{8,24},{12,28},{16,0},{20,4},{24,8},{28,12},{1,17},{... | collective-permute-start | bytes 1572872 | tf_op jit(solution)/shard_map/ppermute | solution.py:80
  78.0 35.2 %collective-permute-start.5 = (bf16[512,512]{1,0:T(8,128)(2,1)S(1)}, bf16[512,512]{1,0:T(8,128)(2,1)S(1)}, u32[]{:S(2)}, u32[]{:S(2)}) collective-permute-start(bf16[512,512]{1,0:T(8,128)(2,1)S(1)} %pad_maximum_fusion.6), channel_id=1, source_target_pairs={{0,24},{4,28},{8,16},{12,20},{16,8},{20,12},{24,0},{28,4},{1,25},{... | collective-permute-start | bytes 1572872 | tf_op jit(solution)/shard_map/ppermute | solution.py:80
  79.7 33.6 %collective-permute-start.6 = (bf16[512,512]{1,0:T(8,128)(2,1)S(1)}, bf16[512,512]{1,0:T(8,128)(2,1)S(1)}, u32[]{:S(2)}, u32[]{:S(2)}) collective-permute-start(bf16[512,512]{1,0:T(8,128)(2,1)S(1)} %pad_maximum_fusion.6), channel_id=1, source_target_pairs={{0,4},{4,0},{8,12},{12,8},{16,20},{20,16},{24,28},{28,24},{1,5},{5... | collective-permute-start | bytes 1572872 | tf_op jit(solution)/shard_map/ppermute | solution.py:80
  95.3 18.0 %collective-permute-start.7 = (bf16[512,512]{1,0:T(8,128)(2,1)S(1)}, bf16[512,512]{1,0:T(8,128)(2,1)S(1)}, u32[]{:S(2)}, u32[]{:S(2)}) collective-permute-start(bf16[512,512]{1,0:T(8,128)(2,1)S(1)} %collective-permute-done.3), channel_id=1, source_target_pairs={{0,4},{4,0},{8,12},{12,8},{16,20},{20,16},{24,28},{28,24},{1,5},{5... | collective-permute-start | bytes 1572872 | tf_op jit(solution)/shard_map/ppermute | solution.py:80
  100.3 13.1 %collective-permute-start.8 = (bf16[512,512]{1,0:T(8,128)(2,1)S(1)}, bf16[512,512]{1,0:T(8,128)(2,1)S(1)}, u32[]{:S(2)}, u32[]{:S(2)}) collective-permute-start(bf16[512,512]{1,0:T(8,128)(2,1)S(1)} %collective-permute-done.4), channel_id=1, source_target_pairs={{0,4},{4,0},{8,12},{12,8},{16,20},{20,16},{24,28},{28,24},{1,5},{5... | collective-permute-start | bytes 1572872 | tf_op jit(solution)/shard_map/ppermute | solution.py:80
  113.2 1.9 collective-permute-start.9
  127.2 11.8 %collective-permute-start.12 = (bf16[128,1152]{1,0:T(8,128)(2,1)S(1)}, bf16[128,1152]{1,0:T(8,128)(2,1)S(1)}, u32[]{:S(2)}, u32[]{:S(2)}) collective-permute-start(bf16[128,1152]{1,0:T(8,128)(2,1)S(1)} %get-tuple-element.70), channel_id=1, source_target_pairs={{0,1},{1,2},{2,3},{3,0},{4,5},{5,6},{6,7},{7,4},{8,9},{9,10},{10,1... | collective-permute-start | bytes 884744 | tf_op jit(solution)/shard_map/ppermute | solution.py:75
  128.8 22.1 %collective-permute-start.11 = (bf16[128,1152]{1,0:T(8,128)(2,1)S(1)}, bf16[128,1152]{1,0:T(8,128)(2,1)S(1)}, u32[]{:S(2)}, u32[]{:S(2)}) collective-permute-start(bf16[128,1152]{1,0:T(8,128)(2,1)S(1)} %get-tuple-element.71), channel_id=1, source_target_pairs={{0,2},{1,3},{2,0},{3,1},{4,6},{5,7},{6,4},{7,5},{8,10},{9,11},{10,... | collective-permute-start | bytes 884744 | tf_op jit(solution)/shard_map/ppermute | solution.py:75
  131.2 19.8 %collective-permute-start.10 = (bf16[128,1152]{1,0:T(8,128)(2,1)S(1)}, bf16[128,1152]{1,0:T(8,128)(2,1)S(1)}, u32[]{:S(2)}, u32[]{:S(2)}) collective-permute-start(bf16[128,1152]{1,0:T(8,128)(2,1)S(1)} %get-tuple-element.69), channel_id=1, source_target_pairs={{0,3},{1,0},{2,1},{3,2},{4,7},{5,4},{6,5},{7,6},{8,11},{9,8},{10,9... | collective-permute-start | bytes 884744 | tf_op jit(solution)/shard_map/ppermute | solution.py:75
  153.7 15.2 %collective-permute-start.15 = (bf16[128,1152]{1,0:T(8,128)(2,1)S(1)}, bf16[128,1152]{1,0:T(8,128)(2,1)S(1)}, u32[]{:S(2)}, u32[]{:S(2)}) collective-permute-start(bf16[128,1152]{1,0:T(8,128)(2,1)S(1)} %multiply_convert_fusion.4), channel_id=1, source_target_pairs={{0,3},{1,0},{2,1},{3,2},{4,7},{5,4},{6,5},{7,6},{8,11},{9,8},{10,9... | collective-permute-start | bytes 884744 | tf_op jit(solution)/shard_map/ppermute | solution.py:75
  161.4 26.4 %collective-permute-start.14 = (bf16[128,1152]{1,0:T(8,128)(2,1)S(1)}, bf16[128,1152]{1,0:T(8,128)(2,1)S(1)}, u32[]{:S(2)}, u32[]{:S(2)}) collective-permute-start(bf16[128,1152]{1,0:T(8,128)(2,1)S(1)} %multiply_convert_fusion.4), channel_id=1, source_target_pairs={{0,2},{1,3},{2,0},{3,1},{4,6},{5,7},{6,4},{7,5},{8,10},{9,11},{10,... | collective-permute-start | bytes 884744 | tf_op jit(solution)/shard_map/ppermute | solution.py:75
  162.0 26.6 %collective-permute-start.13 = (bf16[128,1152]{1,0:T(8,128)(2,1)S(1)}, bf16[128,1152]{1,0:T(8,128)(2,1)}, u32[]{:S(2)}, u32[]{:S(2)}) collective-permute-start(bf16[128,1152]{1,0:T(8,128)(2,1)S(1)} %multiply_convert_fusion.4), channel_id=1, source_target_pairs={{0,1},{1,2},{2,3},{3,0},{4,5},{5,6},{6,7},{7,4},{8,9},{9,10},{10,1... | collective-permute-start | bytes 884744 | tf_op jit(solution)/shard_map/ppermute | solution.py:75
  212.1 12.1 %collective-permute-start.18 = (bf16[128,1152]{1,0:T(8,128)(2,1)}, bf16[128,1152]{1,0:T(8,128)(2,1)S(1)}, u32[]{:S(2)}, u32[]{:S(2)}) collective-permute-start(bf16[128,1152]{1,0:T(8,128)(2,1)} %get-tuple-element.67), channel_id=1, source_target_pairs={{0,1},{1,2},{2,3},{3,0},{4,5},{5,6},{6,7},{7,4},{8,9},{9,10},{10,1... | collective-permute-start | bytes 884744 | tf_op jit(solution)/shard_map/ppermute | solution.py:75
  212.1 23.0 %collective-permute-start.17 = (bf16[128,1152]{1,0:T(8,128)(2,1)}, bf16[128,1152]{1,0:T(8,128)(2,1)S(1)}, u32[]{:S(2)}, u32[]{:S(2)}) collective-permute-start(bf16[128,1152]{1,0:T(8,128)(2,1)} %get-tuple-element.68), channel_id=1, source_target_pairs={{0,2},{1,3},{2,0},{3,1},{4,6},{5,7},{6,4},{7,5},{8,10},{9,11},{10,... | collective-permute-start | bytes 884744 | tf_op jit(solution)/shard_map/ppermute | solution.py:75
  212.3 22.8 %collective-permute-start.16 = (bf16[128,1152]{1,0:T(8,128)(2,1)}, bf16[128,1152]{1,0:T(8,128)(2,1)}, u32[]{:S(2)}, u32[]{:S(2)}) collective-permute-start(bf16[128,1152]{1,0:T(8,128)(2,1)} %get-tuple-element.66), channel_id=1, source_target_pairs={{0,3},{1,0},{2,1},{3,2},{4,7},{5,4},{6,5},{7,6},{8,11},{9,8},{10,9... | collective-permute-start | bytes 884744 | tf_op jit(solution)/shard_map/ppermute | solution.py:75
  239.2 12.8 %collective-permute-start.21 = (bf16[128,1152]{1,0:T(8,128)(2,1)S(1)}, bf16[128,1152]{1,0:T(8,128)(2,1)S(1)}, u32[]{:S(2)}, u32[]{:S(2)}) collective-permute-start(bf16[128,1152]{1,0:T(8,128)(2,1)S(1)} %get-tuple-element.76), channel_id=1, source_target_pairs={{0,3},{1,0},{2,1},{3,2},{4,7},{5,4},{6,5},{7,6},{8,11},{9,8},{10,9... | collective-permute-start | bytes 884744 | tf_op jit(solution)/shard_map/ppermute | solution.py:75
  244.5 27.0 %collective-permute-start.20 = (bf16[128,1152]{1,0:T(8,128)(2,1)S(1)}, bf16[128,1152]{1,0:T(8,128)(2,1)S(1)}, u32[]{:S(2)}, u32[]{:S(2)}) collective-permute-start(bf16[128,1152]{1,0:T(8,128)(2,1)S(1)} %get-tuple-element.76), channel_id=1, source_target_pairs={{0,2},{1,3},{2,0},{3,1},{4,6},{5,7},{6,4},{7,5},{8,10},{9,11},{10,... | collective-permute-start | bytes 884744 | tf_op jit(solution)/shard_map/ppermute | solution.py:75
  246.6 24.9 %collective-permute-start.19 = (bf16[128,1152]{1,0:T(8,128)(2,1)S(1)}, bf16[128,1152]{1,0:T(8,128)(2,1)S(1)}, u32[]{:S(2)}, u32[]{:S(2)}) collective-permute-start(bf16[128,1152]{1,0:T(8,128)(2,1)S(1)} %get-tuple-element.76), channel_id=1, source_target_pairs={{0,1},{1,2},{2,3},{3,0},{4,5},{5,6},{6,7},{7,4},{8,9},{9,10},{10,1... | collective-permute-start | bytes 884744 | tf_op jit(solution)/shard_map/ppermute | solution.py:75
  286.2 11.9 %collective-permute-start.24 = (bf16[128,1152]{1,0:T(8,128)(2,1)S(1)}, bf16[128,1152]{1,0:T(8,128)(2,1)S(1)}, u32[]{:S(2)}, u32[]{:S(2)}) collective-permute-start(bf16[128,1152]{1,0:T(8,128)(2,1)S(1)} %get-tuple-element.64), channel_id=1, source_target_pairs={{0,1},{1,2},{2,3},{3,0},{4,5},{5,6},{6,7},{7,4},{8,9},{9,10},{10,1... | collective-permute-start | bytes 884744 | tf_op jit(solution)/shard_map/ppermute | solution.py:75
  286.3 21.7 %collective-permute-start.23 = (bf16[128,1152]{1,0:T(8,128)(2,1)S(1)}, bf16[128,1152]{1,0:T(8,128)(2,1)S(1)}, u32[]{:S(2)}, u32[]{:S(2)}) collective-permute-start(bf16[128,1152]{1,0:T(8,128)(2,1)S(1)} %get-tuple-element.65), channel_id=1, source_target_pairs={{0,2},{1,3},{2,0},{3,1},{4,6},{5,7},{6,4},{7,5},{8,10},{9,11},{10,... | collective-permute-start | bytes 884744 | tf_op jit(solution)/shard_map/ppermute | solution.py:75
  286.4 21.6 %collective-permute-start.22 = (bf16[128,1152]{1,0:T(8,128)(2,1)S(1)}, bf16[128,1152]{1,0:T(8,128)(2,1)S(1)}, u32[]{:S(2)}, u32[]{:S(2)}) collective-permute-start(bf16[128,1152]{1,0:T(8,128)(2,1)S(1)} %get-tuple-element.63), channel_id=1, source_target_pairs={{0,3},{1,0},{2,1},{3,2},{4,7},{5,4},{6,5},{7,6},{8,11},{9,8},{10,9... | collective-permute-start | bytes 884744 | tf_op jit(solution)/shard_map/ppermute | solution.py:75
  310.1 14.6 %collective-permute-start.27 = (bf16[128,1152]{1,0:T(8,128)(2,1)S(1)}, bf16[128,1152]{1,0:T(8,128)(2,1)S(1)}, u32[]{:S(2)}, u32[]{:S(2)}) collective-permute-start(bf16[128,1152]{1,0:T(8,128)(2,1)S(1)} %subtract_convert_fusion), channel_id=1, source_target_pairs={{0,3},{1,0},{2,1},{3,2},{4,7},{5,4},{6,5},{7,6},{8,11},{9,8},{10,9... | collective-permute-start | bytes 884744 | tf_op jit(solution)/shard_map/ppermute | solution.py:75
  317.1 25.3 %collective-permute-start.26 = (bf16[128,1152]{1,0:T(8,128)(2,1)S(1)}, bf16[128,1152]{1,0:T(8,128)(2,1)S(1)}, u32[]{:S(2)}, u32[]{:S(2)}) collective-permute-start(bf16[128,1152]{1,0:T(8,128)(2,1)S(1)} %subtract_convert_fusion), channel_id=1, source_target_pairs={{0,2},{1,3},{2,0},{3,1},{4,6},{5,7},{6,4},{7,5},{8,10},{9,11},{10,... | collective-permute-start | bytes 884744 | tf_op jit(solution)/shard_map/ppermute | solution.py:75
  317.5 25.0 %collective-permute-start.25 = (bf16[128,1152]{1,0:T(8,128)(2,1)S(1)}, bf16[128,1152]{1,0:T(8,128)(2,1)S(1)}, u32[]{:S(2)}, u32[]{:S(2)}) collective-permute-start(bf16[128,1152]{1,0:T(8,128)(2,1)S(1)} %subtract_convert_fusion), channel_id=1, source_target_pairs={{0,1},{1,2},{2,3},{3,0},{4,5},{5,6},{6,7},{7,4},{8,9},{9,10},{10,1... | collective-permute-start | bytes 884744 | tf_op jit(solution)/shard_map/ppermute | solution.py:75
  345.3 201.8 %reduce-scatter.7.cloned.1.call-start = ((), (), s32[]{:S(2)}) async-start(), calls=%async_computation.8 | async-start | bytes 4644864 | tf_op jit(solution)/shard_map/reduce_scatter | solution.py:274
  351.3 197.8 %reduce-scatter.9.cloned.1.call-start = ((), (), s32[]{:S(2)}) async-start(), calls=%async_computation.9 | async-start | bytes 4644864 | tf_op jit(solution)/shard_map/reduce_scatter | solution.py:276
  357.5 203.0 %reduce-scatter.11.cloned.1.call-start = ((), (), s32[]{:S(2)}) async-start(), calls=%async_computation.10 | async-start | bytes 4644864 | tf_op jit(solution)/shard_map/reduce_scatter | solution.py:272
  358.9 11.1 %collective-permute-start.31 = (bf16[528,256]{1,0:T(8,128)(2,1)S(1)}, bf16[528,256]{1,0:T(8,128)(2,1)S(1)}, u32[]{:S(2)}, u32[]{:S(2)}) collective-permute-start(bf16[528,256]{1,0:T(8,128)(2,1)S(1)} %concatenate.111), channel_id=1, source_target_pairs={{0,8},{4,12},{8,0},{12,4},{16,24},{20,28},{24,16},{28,20},{1,9},{5... | collective-permute-start | bytes 811016 | tf_op jit(solution)/shard_map/ppermute | solution.py:80
  360.5 13.7 %collective-permute-start.32 = (bf16[528,256]{1,0:T(8,128)(2,1)S(1)}, bf16[528,256]{1,0:T(8,128)(2,1)S(1)}, u32[]{:S(2)}, u32[]{:S(2)}) collective-permute-start(bf16[528,256]{1,0:T(8,128)(2,1)S(1)} %concatenate.111), channel_id=1, source_target_pairs={{0,16},{4,20},{8,24},{12,28},{16,0},{20,4},{24,8},{28,12},{1,17},{... | collective-permute-start | bytes 811016 | tf_op jit(solution)/shard_map/ppermute | solution.py:80
  362.1 12.1 %collective-permute-start.33 = (bf16[528,256]{1,0:T(8,128)(2,1)S(1)}, bf16[528,256]{1,0:T(8,128)(2,1)S(1)}, u32[]{:S(2)}, u32[]{:S(2)}) collective-permute-start(bf16[528,256]{1,0:T(8,128)(2,1)S(1)} %concatenate.111), channel_id=1, source_target_pairs={{0,24},{4,28},{8,16},{12,20},{16,8},{20,12},{24,0},{28,4},{1,25},{... | collective-permute-start | bytes 811016 | tf_op jit(solution)/shard_map/ppermute | solution.py:80
  363.5 11.3 %collective-permute-start.34 = (bf16[528,256]{1,0:T(8,128)(2,1)S(1)}, bf16[528,256]{1,0:T(8,128)(2,1)S(1)}, u32[]{:S(2)}, u32[]{:S(2)}) collective-permute-start(bf16[528,256]{1,0:T(8,128)(2,1)S(1)} %concatenate.111), channel_id=1, source_target_pairs={{0,4},{4,0},{8,12},{12,8},{16,20},{20,16},{24,28},{28,24},{1,5},{5... | collective-permute-start | bytes 811016 | tf_op jit(solution)/shard_map/ppermute | solution.py:80
  369.9 4.9 collective-permute-start.35
  374.2 1.9 collective-permute-start.37
  406.0 17.3 %collective-permute-start.38 = (bf16[528,256]{0,1:T(8,128)(2,1)S(1)}, bf16[528,256]{0,1:T(8,128)(2,1)}, u32[]{:S(2)}, u32[]{:S(2)}) collective-permute-start(bf16[528,256]{0,1:T(8,128)(2,1)S(1)} %concatenate.112), channel_id=1, source_target_pairs={{0,8},{4,12},{8,0},{12,4},{16,24},{20,28},{24,16},{28,20},{1,9},{5... | collective-permute-start | bytes 811016 | tf_op jit(solution)/shard_map/ppermute | solution.py:80
  407.7 18.2 %collective-permute-start.39 = (bf16[528,256]{0,1:T(8,128)(2,1)S(1)}, bf16[528,256]{0,1:T(8,128)(2,1)}, u32[]{:S(2)}, u32[]{:S(2)}) collective-permute-start(bf16[528,256]{0,1:T(8,128)(2,1)S(1)} %concatenate.112), channel_id=1, source_target_pairs={{0,16},{4,20},{8,24},{12,28},{16,0},{20,4},{24,8},{28,12},{1,17},{... | collective-permute-start | bytes 811016 | tf_op jit(solution)/shard_map/ppermute | solution.py:80
  408.4 26.3 %collective-permute-start.40 = (bf16[528,256]{0,1:T(8,128)(2,1)S(1)}, bf16[528,256]{0,1:T(8,128)(2,1)}, u32[]{:S(2)}, u32[]{:S(2)}) collective-permute-start(bf16[528,256]{0,1:T(8,128)(2,1)S(1)} %concatenate.112), channel_id=1, source_target_pairs={{0,24},{4,28},{8,16},{12,20},{16,8},{20,12},{24,0},{28,4},{1,25},{... | collective-permute-start | bytes 811016 | tf_op jit(solution)/shard_map/ppermute | solution.py:80
  409.5 34.6 %collective-permute-start.41 = (bf16[528,256]{0,1:T(8,128)(2,1)S(1)}, bf16[528,256]{0,1:T(8,128)(2,1)}, u32[]{:S(2)}, u32[]{:S(2)}) collective-permute-start(bf16[528,256]{0,1:T(8,128)(2,1)S(1)} %concatenate.112), channel_id=1, source_target_pairs={{0,4},{4,0},{8,12},{12,8},{16,20},{20,16},{24,28},{28,24},{1,5},{5... | collective-permute-start | bytes 811016 | tf_op jit(solution)/shard_map/ppermute | solution.py:80
  423.3 24.4 %collective-permute-start.42 = (bf16[528,256]{0,1:T(8,128)(2,1)}, bf16[528,256]{0,1:T(8,128)(2,1)S(1)}, u32[]{:S(2)}, u32[]{:S(2)}) collective-permute-start(bf16[528,256]{0,1:T(8,128)(2,1)} %collective-permute-done.38), channel_id=1, source_target_pairs={{0,4},{4,0},{8,12},{12,8},{16,20},{20,16},{24,28},{28,24},{1,5},{5... | collective-permute-start | bytes 811016 | tf_op jit(solution)/shard_map/ppermute | solution.py:80
  425.8 23.1 %collective-permute-start.43 = (bf16[528,256]{0,1:T(8,128)(2,1)}, bf16[528,256]{0,1:T(8,128)(2,1)S(1)}, u32[]{:S(2)}, u32[]{:S(2)}) collective-permute-start(bf16[528,256]{0,1:T(8,128)(2,1)} %collective-permute-done.39), channel_id=1, source_target_pairs={{0,4},{4,0},{8,12},{12,8},{16,20},{20,16},{24,28},{28,24},{1,5},{5... | collective-permute-start | bytes 811016 | tf_op jit(solution)/shard_map/ppermute | solution.py:80
  434.7 15.4 %collective-permute-start.44 = (bf16[528,256]{0,1:T(8,128)(2,1)}, bf16[528,256]{0,1:T(8,128)(2,1)S(1)}, u32[]{:S(2)}, u32[]{:S(2)}) collective-permute-start(bf16[528,256]{0,1:T(8,128)(2,1)} %collective-permute-done.40), channel_id=1, source_target_pairs={{0,4},{4,0},{8,12},{12,8},{16,20},{20,16},{24,28},{28,24},{1,5},{5... | collective-permute-start | bytes 811016 | tf_op jit(solution)/shard_map/ppermute | solution.py:80
  435.7 71.9 %collective-permute-start.30 = (bf16[128,1152]{1,0:T(8,128)(2,1)}, bf16[128,1152]{1,0:T(8,128)(2,1)}, u32[]{:S(2)}, u32[]{:S(2)}) collective-permute-start(bf16[128,1152]{1,0:T(8,128)(2,1)} %get-tuple-element.61), channel_id=1, source_target_pairs={{0,1},{1,2},{2,3},{3,0},{4,5},{5,6},{6,7},{7,4},{8,9},{9,10},{10,1... | collective-permute-start | bytes 884744 | tf_op jit(solution)/shard_map/ppermute | solution.py:75
  444.1 63.4 %collective-permute-start.29 = (bf16[128,1152]{1,0:T(8,128)(2,1)}, bf16[128,1152]{1,0:T(8,128)(2,1)}, u32[]{:S(2)}, u32[]{:S(2)}) collective-permute-start(bf16[128,1152]{1,0:T(8,128)(2,1)} %get-tuple-element.62), channel_id=1, source_target_pairs={{0,2},{1,3},{2,0},{3,1},{4,6},{5,7},{6,4},{7,5},{8,10},{9,11},{10,... | collective-permute-start | bytes 884744 | tf_op jit(solution)/shard_map/ppermute | solution.py:75
  479.6 8.6 %collective-permute-start.47 = (bf16[128,512]{1,0:T(8,128)(2,1)}, bf16[128,512]{1,0:T(8,128)(2,1)}, u32[]{:S(2)}, u32[]{:S(2)}) collective-permute-start(bf16[128,512]{1,0:T(8,128)(2,1)} %get-tuple-element.81), channel_id=1, source_target_pairs={{0,1},{1,2},{2,3},{3,0},{4,5},{5,6},{6,7},{7,4},{8,9},{9,10},{10,1... | collective-permute-start | bytes 393224 | tf_op jit(solution)/shard_map/ppermute | solution.py:75
  481.6 11.6 %collective-permute-start.46 = (bf16[128,512]{1,0:T(8,128)(2,1)}, bf16[128,512]{1,0:T(8,128)(2,1)}, u32[]{:S(2)}, u32[]{:S(2)}) collective-permute-start(bf16[128,512]{1,0:T(8,128)(2,1)} %get-tuple-element.82), channel_id=1, source_target_pairs={{0,2},{1,3},{2,0},{3,1},{4,6},{5,7},{6,4},{7,5},{8,10},{9,11},{10,... | collective-permute-start | bytes 393224 | tf_op jit(solution)/shard_map/ppermute | solution.py:75
  482.7 10.5 %collective-permute-start.45 = (bf16[128,512]{1,0:T(8,128)(2,1)S(1)}, bf16[128,512]{1,0:T(8,128)(2,1)}, u32[]{:S(2)}, u32[]{:S(2)}) collective-permute-start(bf16[128,512]{1,0:T(8,128)(2,1)S(1)} %get-tuple-element.80), channel_id=1, source_target_pairs={{0,3},{1,0},{2,1},{3,2},{4,7},{5,4},{6,5},{7,6},{8,11},{9,8},{10,9... | collective-permute-start | bytes 393224 | tf_op jit(solution)/shard_map/ppermute | solution.py:75
  488.1 19.4 %collective-permute-start.28 = (bf16[128,1152]{1,0:T(8,128)(2,1)}, bf16[128,1152]{1,0:T(8,128)(2,1)S(1)}, u32[]{:S(2)}, u32[]{:S(2)}) collective-permute-start(bf16[128,1152]{1,0:T(8,128)(2,1)} %get-tuple-element.60), channel_id=1, source_target_pairs={{0,3},{1,0},{2,1},{3,2},{4,7},{5,4},{6,5},{7,6},{8,11},{9,8},{10,9... | collective-permute-start | bytes 884744 | tf_op jit(solution)/shard_map/ppermute | solution.py:75
  498.0 21.1 %collective-permute-start.50 = (bf16[128,512]{1,0:T(8,128)(2,1)S(1)}, bf16[128,512]{1,0:T(8,128)(2,1)}, u32[]{:S(2)}, u32[]{:S(2)}) collective-permute-start(bf16[128,512]{1,0:T(8,128)(2,1)S(1)} %pad_maximum_fusion.12), channel_id=1, source_target_pairs={{0,3},{1,0},{2,1},{3,2},{4,7},{5,4},{6,5},{7,6},{8,11},{9,8},{10,9... | collective-permute-start | bytes 393224 | tf_op jit(solution)/shard_map/ppermute | solution.py:75
  507.5 11.6 %collective-permute-start.49 = (bf16[128,512]{1,0:T(8,128)(2,1)S(1)}, bf16[128,512]{1,0:T(8,128)(2,1)}, u32[]{:S(2)}, u32[]{:S(2)}) collective-permute-start(bf16[128,512]{1,0:T(8,128)(2,1)S(1)} %pad_maximum_fusion.12), channel_id=1, source_target_pairs={{0,2},{1,3},{2,0},{3,1},{4,6},{5,7},{6,4},{7,5},{8,10},{9,11},{10,... | collective-permute-start | bytes 393224 | tf_op jit(solution)/shard_map/ppermute | solution.py:75
  511.8 6.6 %collective-permute-start.53 = (f32[8,160]{1,0:T(8,128)S(1)}, f32[8,160]{1,0:T(8,128)S(1)}, u32[]{:S(2)}, u32[]{:S(2)}) collective-permute-start(f32[8,160]{1,0:T(8,128)S(1)} %bitcast.204), channel_id=1, source_target_pairs={{0,1},{1,2},{2,3},{3,0},{4,5},{5,6},{6,7},{7,4},{8,9},{9,10},{10,1... | collective-permute-start | bytes 15368 | tf_op jit(solution)/shard_map/ppermute | solution.py:75
  512.5 5.9 %collective-permute-start.52 = (f32[8,160]{1,0:T(8,128)S(1)}, f32[8,160]{1,0:T(8,128)S(1)}, u32[]{:S(2)}, u32[]{:S(2)}) collective-permute-start(f32[8,160]{1,0:T(8,128)S(1)} %bitcast.203), channel_id=1, source_target_pairs={{0,2},{1,3},{2,0},{3,1},{4,6},{5,7},{6,4},{7,5},{8,10},{9,11},{10,... | collective-permute-start | bytes 15368 | tf_op jit(solution)/shard_map/ppermute | solution.py:75
  514.9 4.2 collective-permute-start.51
  518.4 6.8 %collective-permute-start.48 = (bf16[128,512]{1,0:T(8,128)(2,1)S(1)}, bf16[128,512]{1,0:T(8,128)(2,1)S(1)}, u32[]{:S(2)}, u32[]{:S(2)}) collective-permute-start(bf16[128,512]{1,0:T(8,128)(2,1)S(1)} %pad_maximum_fusion.12), channel_id=1, source_target_pairs={{0,1},{1,2},{2,3},{3,0},{4,5},{5,6},{6,7},{7,4},{8,9},{9,10},{10,1... | collective-permute-start | bytes 393224 | tf_op jit(solution)/shard_map/ppermute | solution.py:75
  531.8 9.4 %collective-permute-start.57 = (bf16[224,256]{1,0:T(8,128)(2,1)S(1)}, bf16[224,256]{1,0:T(8,128)(2,1)S(1)}, u32[]{:S(2)}, u32[]{:S(2)}) collective-permute-start(bf16[224,256]{1,0:T(8,128)(2,1)S(1)} %get-tuple-element.58), channel_id=1, source_target_pairs={{0,24},{4,28},{8,16},{12,20},{16,8},{20,12},{24,0},{28,4},{1,25},{... | collective-permute-start | bytes 344072 | tf_op jit(solution)/shard_map/ppermute | solution.py:80
  532.4 10.4 %collective-permute-start.56 = (bf16[224,256]{1,0:T(8,128)(2,1)S(1)}, bf16[224,256]{1,0:T(8,128)(2,1)S(1)}, u32[]{:S(2)}, u32[]{:S(2)}) collective-permute-start(bf16[224,256]{1,0:T(8,128)(2,1)S(1)} %get-tuple-element.59), channel_id=1, source_target_pairs={{0,16},{4,20},{8,24},{12,28},{16,0},{20,4},{24,8},{28,12},{1,17},{... | collective-permute-start | bytes 344072 | tf_op jit(solution)/shard_map/ppermute | solution.py:80
  533.4 11.1 %collective-permute-start.55 = (bf16[224,256]{1,0:T(8,128)(2,1)S(1)}, bf16[224,256]{1,0:T(8,128)(2,1)S(1)}, u32[]{:S(2)}, u32[]{:S(2)}) collective-permute-start(bf16[224,256]{1,0:T(8,128)(2,1)S(1)} %get-tuple-element.57), channel_id=1, source_target_pairs={{0,8},{4,12},{8,0},{12,4},{16,24},{20,28},{24,16},{28,20},{1,9},{5... | collective-permute-start | bytes 344072 | tf_op jit(solution)/shard_map/ppermute | solution.py:80
  (129 other events, 1297.2 us)
Sparse Core Ops, SparseCore 0:
  29.5 31.0 all-gather.13
  62.5 53.0 all-gather.7
  117.5 36.5 all-gather.9
  155.8 36.4 all-gather.11
  345.4 35.4 reduce-scatter.4
  384.2 62.2 reduce-scatter.6
  449.9 51.0 reduce-scatter.8
  504.4 55.9 reduce-scatter.10

commit v2 on v1

v2 whole, which is shorter than its diff:
```python
import jax
import jax.numpy as jnp
from jax import lax
from jax.experimental import pallas as pl
from jax.experimental.layout import Layout, with_layout_constraint
from jax.experimental.pallas import tpu as pltpu
from jax.sharding import PartitionSpec as P

HD = 256

EPSILON = 1e-06
ROPE_BASE = 1000000.0
QUERY_SCALE = 0.0625
MASKED = -1e30
GELU_COEF = 0.7978845608028654
GELU_CUBIC = 0.044715
BF = jnp.bfloat16
F32 = jnp.float32


def rms_inverse(values):
    return lax.rsqrt(jnp.mean(values * values, axis=-1, keepdims=True) + EPSILON)


def rms_backward(values, inverse, scales, upstream):
    weighted = upstream * scales
    inner_mean = jnp.mean(values * weighted, axis=-1, keepdims=True)
    grad_values = inverse * weighted - values * (inverse * inverse * inverse) * inner_mean
    grad_scales = jnp.sum(upstream * values * inverse, axis=0)
    return (grad_values, grad_scales)


def gelu_pair(values):
    inside = GELU_COEF * (values + GELU_CUBIC * values * values * values)
    tangent = jnp.tanh(inside)
    output = 0.5 * values * (1.0 + tangent)
    derivative = 0.5 * (1.0 + tangent) + 0.5 * values * (1.0 - tangent * tangent) * GELU_COEF * (
        1.0 + 3.0 * GELU_CUBIC * values * values
    )
    return (output, derivative)


def rotate_half(values):
    halfway = values.shape[-1] // 2
    return jnp.concatenate([-values[..., halfway:], values[..., :halfway]], axis=-1)


def rope_tables(positions):
    halfway = HD // 2
    frequency = ROPE_BASE ** (-2.0 * jnp.arange(halfway, dtype=F32) / HD)
    angles = positions.astype(F32)[:, None] * frequency[None, :]
    angles = jnp.concatenate([angles, angles], axis=1)
    return (jnp.cos(angles), jnp.sin(angles))


def apply_rope(values, cosine, sine_part):
    return values * cosine + rotate_half(values) * sine_part


def rope_back(upstream, cosine, sine_part):
    return upstream * cosine - rotate_half(upstream * sine_part)


def dot(left, right):
    return jnp.dot(left, right, preferred_element_type=F32)


def contract_first(left, right):
    return lax.dot_general(left, right, (((0,), (0,)), ((), ())), preferred_element_type=F32)


def contract_last(left, right):
    return lax.dot_general(left, right, (((1,), (1,)), ((), ())), preferred_element_type=F32)

AXES = ("dp", "tensor")
PAIR = 2


def place(device):
    return device >> 3, (device >> 2) & 1, (device >> 1) & 1, device & 1


def device_at(block, core, half, low):
    return (block << 3) | (core << 2) | (half << 1) | low


def device_count():
    return lax.axis_size("dp") * lax.axis_size("tensor")


def own_device():
    return lax.axis_index("dp") * lax.axis_size("tensor") + lax.axis_index("tensor")


def flip(value, mask):
    return lax.ppermute(value, AXES, [(s, s ^ mask) for s in range(device_count())])


def send(value, target):
    pairs = [(s, target(*place(s))) for s in range(device_count())]
    return lax.ppermute(value, AXES, [(s, t) for s, t in pairs if t is not None])


LOW, HALF, CORE, BLOCK = 1, 2, 4, 8
GROUP = (0, LOW, CORE, CORE | LOW)


def block_masks():
    return [BLOCK * k for k in range(lax.axis_size("dp") // PAIR)]


def natural(items, index):
    count, rows, columns = items.shape

    def body(index_ref, item_ref, out_ref):
        out_ref[...] = item_ref[...]

    return pl.pallas_call(
        body,
        out_shape=jax.ShapeDtypeStruct(items.shape, items.dtype),
        grid_spec=pltpu.PrefetchScalarGridSpec(
            num_scalar_prefetch=1,
            grid=(count,),
            in_specs=[pl.BlockSpec((1, rows, columns), lambda i, ref: (i ^ ref[0], 0, 0))],
            out_specs=pl.BlockSpec((1, rows, columns), lambda i, ref: (i, 0, 0)),
        ),
    )(index[None], items)


def shared_rows(near, far, device, rows):
    blocks, _, _, columns = near.shape
    count = 8 * blocks

    def body(index_ref, near_ref, far_ref, rows_ref, gains_ref, wide_ref):
        for owner in range(count):
            at = owner ^ index_ref[0]
            block, low = at >> 3, at & 3
            mine = near_ref[block, low].astype(F32)
            other = far_ref[block, low].astype(F32)
            piece = jnp.where((at & CORE) == 0, mine, other)
            wide_ref[owner * rows : (owner + 1) * rows, :] = piece[:rows]
            gains_ref[owner : owner + 1, :] = piece[rows : rows + 1]
        rows_ref[...] = wide_ref[...].astype(BF)

    return pl.pallas_call(
        body,
        out_shape=(
            jax.ShapeDtypeStruct((count * rows, columns), BF),
            jax.ShapeDtypeStruct((count, columns), F32),
        ),
        in_specs=[
            pl.BlockSpec(memory_space=pltpu.SMEM),
            pl.BlockSpec(memory_space=pltpu.VMEM),
            pl.BlockSpec(memory_space=pltpu.VMEM),
        ],
        out_specs=(
            pl.BlockSpec(memory_space=pltpu.VMEM),
            pl.BlockSpec(memory_space=pltpu.VMEM),
        ),
        scratch_shapes=[pltpu.VMEM((count * rows, columns), F32)],
    )(device[None], near, far)


def row_major(values):
    return with_layout_constraint(values, Layout(major_to_minor=(0, 1)))


def column_major(values):
    return with_layout_constraint(values, Layout(major_to_minor=(1, 0)))


def group_gather(values):
    near = flip(values, LOW)
    across = flip(values, CORE)
    return jnp.concatenate([values, near, across, flip(near, CORE)], axis=0)


def group_scatter(product, *rows):
    middle = rows[0].shape[0] // 2
    length = middle // 2
    far = flip(product(*[r[middle:] for r in rows]).astype(BF), CORE)
    near = product(*[r[:middle] for r in rows]) + far.astype(F32)
    return near[:length] + flip(near[length:].astype(BF), LOW).astype(F32)


def after(value, *others):
    return lax.optimization_barrier((value, *others))[0]


def column_gather(values):
    return jnp.concatenate([values] + [flip(values, mask) for mask in (1, 2, 3)], axis=0)


def column_scatter(product, *rows):
    middle = rows[0].shape[0] // 2
    length = middle // 2
    far = product(*[r[middle:] for r in rows]).astype(BF)
    far = [flip(far[length:], 3), flip(far[:length], 2)]
    near = product(*[r[:middle] for r in rows])
    near = near[:length] + flip(near[length:].astype(BF), 1).astype(F32)
    return near + far[0].astype(F32) + far[1].astype(F32)


def exchange_first(value):
    def target(block, core, half, low):
        if half == core:
            return device_at(block, core, 1 - half, low)
        return device_at(block, 1 - core, half, low)

    return send(value, target)


def exchange_second(value):
    def target(block, core, half, low):
        return None if half == core else device_at(block, 1 - core, 1 - half, low)

    return send(value, target)


def weight_pair(value, axis):
    _, core, half, _ = place(own_device())
    first, second = exchange_first(value), exchange_second(value)
    kept = jnp.where(half == core, value, second)
    return jnp.concatenate(
        [jnp.where(half == 0, kept, first), jnp.where(half == 0, first, kept)], axis=axis
    )


def grad_owner(pair):
    return jnp.sum(jnp.stack(grad_owner_parts(pair)), axis=0)


def grad_owner_parts(pair):
    _, core, half, _ = place(own_device())
    pair = pair.astype(BF)
    first = jnp.where(half == 0, pair[1], pair[0])
    second = jnp.where(half == 0, pair[0], pair[1])
    got = exchange_second(second)
    return [
        exchange_first_back(first).astype(F32),
        jnp.where(half == core, second, got).astype(F32),
    ]


def exchange_first_back(value):
    def target(block, core, half, low):
        if half == core:
            return device_at(block, 1 - core, half, low)
        return device_at(block, core, 1 - half, low)

    return send(value, target)


def scatter_blocks(values):
    own = own_device() >> 3
    total = lax.dynamic_index_in_dim(values, own, 0, keepdims=False).astype(F32)
    for mask in block_masks()[1:]:
        piece = lax.dynamic_index_in_dim(values, own ^ (mask // BLOCK), 0, keepdims=False)
        total = total + flip(piece.astype(BF), mask).astype(F32)
    return total


def head_gather(values):
    near = [flip(values, mask) for mask in block_masks()[1:]]
    other = flip(values, HALF)
    far = [flip(other, mask) for mask in block_masks()[1:]]
    return [values, *near, other, *far]


def token_gather(values):
    column = jnp.concatenate([values] + [flip(values, mask) for mask in (1, 2, 3)], axis=0)
    near = [column] + [flip(column, mask) for mask in block_masks()[1:]]
    return near, lambda later: near + [flip(after(piece, later), CORE) for piece in near]


def three_terms(values):
    first = lax.reduce_precision(values, 8, 7)
    rest = values - first
    second = lax.reduce_precision(rest, 8, 7)
    third = lax.reduce_precision(rest - second, 8, 7)
    return jnp.concatenate([first, second, third]).astype(BF)


def with_vectors(rows, *vectors):
    terms = jnp.concatenate([three_terms(vector) for vector in vectors]).reshape(-1, HD)
    padding = jnp.zeros((-terms.shape[0] % 16, HD), BF)
    return row_major(jnp.concatenate([rows, terms, padding], axis=0))


def whole(memory_space):
    return pl.BlockSpec(memory_space=memory_space)


def tile_of(rows, columns):
    return pl.BlockSpec((rows, columns), lambda i: (i, 0))


def group_mask(tile):
    return (tile >> 1) * CORE | (tile & 1) * LOW


def tile_column(document_ref, device):
    length = document_ref.shape[1]
    across = jnp.broadcast_to(document_ref[pl.ds(device, 1), :], (length, length))
    place_in = lax.broadcasted_iota(jnp.int32, (length, length), 0)
    return jnp.transpose(across), device * length + place_in


def hidden_bias(document_ref, column, device, masks, keys_across):
    documents, places = column
    length = document_ref.shape[1]
    parts = []
    for mask in masks:
        other = device ^ mask
        row = document_ref[pl.ds(other, 1), :]
        index = other * length + lax.broadcasted_iota(jnp.int32, (1, length), 1)
        ordered = index <= places if keys_across else index >= places
        parts.append(jnp.where((documents == row) & ordered, 0.0, MASKED))
    return jnp.concatenate(parts, axis=1)


def piece_masks(piece, pieces):
    blocks = pieces // 2
    return [(piece // blocks) * CORE | (piece % blocks) * BLOCK | z for z in range(4)]


def part_masks(piece, pieces):
    blocks = pieces // 2
    return [(piece // blocks) * HALF | (piece % blocks) * BLOCK | mask for mask in GROUP]


def attend(query_rot, keyval_pieces, documents, device):
    pieces, length = len(keyval_pieces), documents.shape[1]
    each = keyval_pieces[0].shape[0]

    def body(device_ref, document_ref, query_ref, *refs):
        piece_refs, (mixed_ref, log_ref, score_ref) = refs[:pieces], refs[pieces:]
        own = device_ref[0]
        column = tile_column(document_ref, own ^ group_mask(pl.program_id(0)))
        query = query_ref[...]
        row_max = jnp.full((length, 1), MASKED, F32)
        for p in range(pieces):
            bias = hidden_bias(document_ref, column, own, piece_masks(p, pieces), True)
            scores = contract_last(query, piece_refs[p][:, :HD]) + bias
            score_ref[:, p * each : (p + 1) * each] = scores
            row_max = jnp.maximum(row_max, jnp.max(scores, axis=1, keepdims=True))
        row_sum = jnp.zeros((length, 1), F32)
        total = jnp.zeros((length, HD), F32)
        for p in range(pieces):
            weights = jnp.exp(score_ref[:, p * each : (p + 1) * each] - row_max)
            row_sum = row_sum + jnp.sum(weights, axis=1, keepdims=True)
            total = total + dot(weights.astype(BF), piece_refs[p][:, HD:])
        mixed_ref[...] = (total / row_sum).astype(BF)
        log_ref[...] = row_max + jnp.log(row_sum)

    rows = query_rot.shape[0]
    return pl.pallas_call(
        body,
        grid=(rows // length,),
        out_shape=(
            jax.ShapeDtypeStruct((rows, HD), BF),
            jax.ShapeDtypeStruct((rows, 1), F32),
        ),
        in_specs=[whole(pltpu.SMEM), whole(pltpu.VMEM), tile_of(length, HD)]
        + [whole(pltpu.VMEM)] * pieces,
        out_specs=(tile_of(length, HD), tile_of(length, 1)),
        scratch_shapes=[pltpu.VMEM((length, pieces * each), F32)],
    )(device[None], documents, query_rot, *keyval_pieces)


def query_grads(query_rot, grad_mixed, mixed, log_norm, keyval_pieces, documents, device):
    pieces, length = len(keyval_pieces), documents.shape[1]

    def body(device_ref, document_ref, query_ref, grad_ref, mixed_ref, log_ref, *refs):
        piece_refs, out_ref = refs[:pieces], refs[pieces]
        own = device_ref[0]
        column = tile_column(document_ref, own ^ group_mask(pl.program_id(0)))
        query, grad, log = query_ref[...], grad_ref[...], log_ref[...]
        delta = jnp.sum(grad.astype(F32) * mixed_ref[...].astype(F32), axis=1, keepdims=True)
        total = jnp.zeros((length, HD), F32)
        for p in range(pieces):
            bias = hidden_bias(document_ref, column, own, piece_masks(p, pieces), True)
            keys = piece_refs[p][:, :HD]
            weights = jnp.exp(contract_last(query, keys) + bias - log)
            grad_prob = contract_last(grad, piece_refs[p][:, HD:])
            total = total + dot((weights * (grad_prob - delta)).astype(BF), keys)
        out_ref[...] = total

    rows = query_rot.shape[0]
    return pl.pallas_call(
        body,
        grid=(rows // length,),
        out_shape=jax.ShapeDtypeStruct((rows, HD), F32),
        in_specs=[whole(pltpu.SMEM), whole(pltpu.VMEM)]
        + [tile_of(length, HD)] * 3
        + [tile_of(length, 1)]
        + [whole(pltpu.VMEM)] * pieces,
        out_specs=tile_of(length, HD),
    )(device[None], documents, query_rot, grad_mixed, mixed, log_norm, *keyval_pieces)


def keyval_grads_of(keyval_group, part_query, part_grad, documents, device):
    pieces, length = len(part_query), documents.shape[1]
    each = part_query[0].shape[0]
    lines = each // HD

    def body(device_ref, document_ref, keyval_ref, *refs):
        query_refs, grad_refs, out_ref = refs[:pieces], refs[pieces : 2 * pieces], refs[-1]
        own = device_ref[0]
        column = tile_column(document_ref, own ^ group_mask(pl.program_id(0)))
        keys, values = keyval_ref[:, :HD], keyval_ref[:, HD:]
        grad_keys = jnp.zeros((length, HD), F32)
        grad_values = jnp.zeros((length, HD), F32)
        for p in range(pieces):
            bias = hidden_bias(document_ref, column, own, part_masks(p, pieces), False)
            terms = grad_refs[p][each:, :].astype(F32)

            def vector(first):
                sums = [
                    sum(terms[first + k * lines + j : first + k * lines + j + 1] for k in range(3))
                    for j in range(lines)
                ]
                return jnp.concatenate(sums, axis=1)

            queries, grads = query_refs[p][...], grad_refs[p][:each, :]
            weights = jnp.exp(contract_last(keys, queries) + bias - vector(0))
            grad_prob = contract_last(values, grads)
            grad_score = (weights * (grad_prob - vector(3 * lines))).astype(BF)
            grad_keys = grad_keys + dot(grad_score, queries)
            grad_values = grad_values + dot(weights.astype(BF), grads)
        out_ref[:, :HD] = grad_keys
        out_ref[:, HD:] = grad_values

    rows = keyval_group.shape[0]
    return pl.pallas_call(
        body,
        grid=(rows // length,),
        out_shape=jax.ShapeDtypeStruct((rows, 2 * HD), F32),
        in_specs=[whole(pltpu.SMEM), whole(pltpu.VMEM), tile_of(length, 2 * HD)]
        + [whole(pltpu.VMEM)] * (2 * pieces),
        out_specs=tile_of(length, 2 * HD),
    )(device[None], documents, keyval_group, *part_query, *part_grad)


def per_device(
    block_in,
    out_grad,
    segments,
    w_query,
    w_keyval,
    w_out,
    w_gate,
    w_up,
    w_down,
    gain_pre_attn,
    gain_post_attn,
    gain_pre_ffn,
    gain_post_ffn,
    gain_query,
    gain_key,
):
    devices = device_count()
    blocks = devices >> 3
    device = own_device()
    own_block, own_core, own_half, own_low = place(device)
    row_count, width = block_in.shape
    group_rows = row_count * len(GROUP)
    small_rows = w_keyval.shape[0]
    weight_rows = w_query.shape[0]
    big = gain_pre_attn.shape[0]
    little = gain_query.shape[0]
    per_owner = 4 * big + 2 * little

    gains_row, at = 0.0, 0
    for gain in (gain_pre_attn, gain_post_attn, gain_pre_ffn, gain_post_ffn, gain_query, gain_key):
        count = gain.shape[0]
        gains_row = gains_row + jnp.pad(gain.astype(F32), (at, 2 * HD - at - count))
        at = at + count
    below = 7 - small_rows % 8
    small = jnp.pad(w_keyval.astype(F32), ((0, 1 + below), (0, 0)))
    small = (small + jnp.pad(gains_row[None, :], ((small_rows, below), (0, 0)))).astype(BF)
    small = jnp.stack([small] + [flip(small, mask) for mask in (1, 2, 3)])
    near = jnp.stack([small] + [flip(small, mask) for mask in block_masks()[1:]])
    keyval_full, gains = shared_rows(near, flip(near, CORE), device, small_rows)
    gains = gains[:, :per_owner]
    scale_pre_attn = gains[:, :big].reshape(width)
    scale_post_attn = gains[:, big : 2 * big].reshape(width)
    scale_pre_ffn = gains[:, 2 * big : 3 * big].reshape(width)
    scale_post_ffn = gains[:, 3 * big : 4 * big].reshape(width)
    scale_query = gains[:, 4 * big : 4 * big + little].reshape(HD)
    scale_key = gains[:, 4 * big + little :].reshape(HD)
    head_weights = weight_pair(jnp.concatenate([w_query, w_out.T], axis=1), 0)
    head_weights = [head_weights] + [flip(head_weights, mask) for mask in block_masks()[1:]]
    gate_full = lax.all_gather(after(w_gate, near), "dp", axis=0, tiled=True)

    own_index = jnp.concatenate(
        [
            (device ^ mask) * row_count + jnp.arange(row_count, dtype=jnp.int32)
            for mask in GROUP
        ]
    )

    inv_in = rms_inverse(block_in)
    unit_in = block_in * inv_in
    unit_own = unit_in.astype(BF)
    unit_all = group_gather(unit_own)
    keyval = dot((unit_own.astype(F32) * scale_pre_attn).astype(BF), keyval_full)
    cosine, sine_part = rope_tables(own_index)
    key_proj = keyval[:, :HD]
    inv_key = rms_inverse(key_proj)
    key_rot = apply_rope(
        key_proj * inv_key * scale_key, cosine[:row_count], sine_part[:row_count]
    ).astype(BF)
    keyval_own = jnp.concatenate([key_rot, keyval[:, HD:].astype(BF)], axis=1)
    keyval_near, keyval_rest = token_gather(keyval_own)
    head_weights = [after(piece, keyval_own) for piece in head_weights]
    unit_all = after(unit_all, keyval_own)
    head_weights = natural(jnp.stack(head_weights), own_block).reshape(width, 2 * HD)
    query_full = head_weights[:, :HD]
    out_full = head_weights[:, HD:]
    gathered_in = (unit_all.astype(F32) * scale_pre_attn).astype(BF)
    queries = dot(gathered_in, query_full)
    inv_query = rms_inverse(queries)
    query_rot = (
        apply_rope(queries * inv_query * scale_query, cosine, sine_part) * QUERY_SCALE
    ).astype(BF)

    keyval_pieces = keyval_rest(query_rot)
    up_full = lax.all_gather(after(w_up, query_rot, *keyval_near), "dp", axis=0, tiled=True)
    down_full = lax.all_gather(after(w_down, query_rot, *keyval_near), "dp", axis=1, tiled=True)
    keyval_group = jnp.concatenate(
        [keyval_pieces[0][: 2 * row_count], keyval_pieces[blocks][: 2 * row_count]], axis=0
    )

    documents = segments.reshape(devices, row_count)
    mixed, log_norm = attend(query_rot, keyval_pieces, documents, device)
    attn_out = group_scatter(lambda rows: contract_last(rows, out_full), mixed)
    inv_attn = rms_inverse(attn_out)
    resid_mid = block_in + attn_out * inv_attn * scale_post_attn

    inv_mid = rms_inverse(resid_mid)
    normed_mid = (resid_mid * inv_mid * scale_pre_ffn).astype(BF)
    gathered_mid = column_gather(normed_mid)
    part_query = head_gather(after(query_rot, gathered_mid))
    gate_pre = dot(gathered_mid, gate_full)
    up_proj = dot(gathered_mid, up_full)
    gate_act, gate_deriv = gelu_pair(gate_pre)
    hidden = after((gate_act * up_proj).astype(BF), part_query[blocks])
    ffn_out = column_scatter(lambda rows: dot(rows, down_full), hidden)
    ffn_out = after(ffn_out, *part_query)
    inv_ffn = rms_inverse(ffn_out)
    block_out = resid_mid + ffn_out * inv_ffn * scale_post_ffn
    grad_ffn, grad_post_ffn = rms_backward(ffn_out, inv_ffn, scale_post_ffn, out_grad)
    grad_ffn_all = column_gather(grad_ffn.astype(BF))
    grad_w_down = column_major(contract_first(hidden, grad_ffn_all).astype(BF))
    grad_ffn_all = after(grad_ffn_all, grad_w_down)
    owned_down = lax.psum_scatter(grad_w_down, "dp", scatter_dimension=1, tiled=True)
    grad_hidden = contract_last(grad_ffn_all, down_full)
    grad_gate = (grad_hidden * up_proj * gate_deriv).astype(BF)
    grad_up = (grad_hidden * gate_act).astype(BF)
    grad_mid = column_scatter(
        lambda gate, up: contract_last(gate, gate_full) + contract_last(up, up_full),
        grad_gate,
        grad_up,
    )
    grad_w_gate = row_major(contract_first(gathered_mid, grad_gate).astype(BF))
    grad_w_up = row_major(contract_first(gathered_mid, grad_up).astype(BF))
    grad_mid = after(grad_mid, grad_w_gate)
    owned_gate = lax.psum_scatter(grad_w_gate, "dp", scatter_dimension=0, tiled=True)
    grad_resid, grad_pre_ffn = rms_backward(resid_mid, inv_mid, scale_pre_ffn, grad_mid)
    grad_resid_mid = out_grad + grad_resid

    grad_attn, grad_post_attn = rms_backward(attn_out, inv_attn, scale_post_attn, grad_resid_mid)
    grad_attn_all = group_gather(grad_attn.astype(BF))
    grad_attn_all = after(grad_attn_all, grad_w_up)
    owned_up = lax.psum_scatter(grad_w_up, "dp", scatter_dimension=0, tiled=True)
    grad_mixed = dot(grad_attn_all, out_full).astype(BF)
    delta = jnp.sum(grad_mixed.astype(F32) * mixed.astype(F32), axis=1)
    part_grad = head_gather(with_vectors(grad_mixed, log_norm[:, 0], delta))
    grad_w_out = contract_first(grad_attn_all, mixed)
    grad_query_rot = query_grads(
        query_rot, grad_mixed, mixed, log_norm, keyval_pieces, documents, device
    )
    owned_down = owned_down.astype(F32)
    part_grad = [after(part_grad[0], owned_down)] + part_grad[1:]
    grad_keyval_part = keyval_grads_of(keyval_group, part_query, part_grad, documents, device)
    grad_keyval_rows = group_scatter(lambda rows: rows, grad_keyval_part)

    grad_query_norm = rope_back(grad_query_rot, cosine, sine_part) * QUERY_SCALE
    grad_queries, grad_gain_query = rms_backward(queries, inv_query, scale_query, grad_query_norm)
    grad_query_bf = grad_queries.astype(BF)
    grad_w_query = contract_first(gathered_in, grad_query_bf)
    heads_pair = scatter_blocks(
        jnp.concatenate(
            [
                after(grad_w_query.astype(BF), *part_grad).reshape(blocks, 2, weight_rows, HD),
                grad_w_out.astype(BF).reshape(blocks, 2, weight_rows, HD),
            ],
            axis=2,
        ).reshape(blocks, 4 * weight_rows, HD)
    )
    grad_key_norm = rope_back(grad_keyval_rows[:, :HD], cosine[:row_count], sine_part[:row_count])
    grad_key_proj, grad_gain_key = rms_backward(key_proj, inv_key, scale_key, grad_key_norm)
    grad_keyval_bf = jnp.concatenate([grad_key_proj, grad_keyval_rows[:, HD:]], axis=1).astype(BF)
    keyval_grads_all = group_gather(grad_keyval_bf)
    heads_pair = after(heads_pair, keyval_grads_all)
    heads_owned = grad_owner(heads_pair.reshape(2, 2 * weight_rows, HD))
    owned_query, owned_out = heads_owned[:weight_rows], heads_owned[weight_rows:]
    grad_w_keyval = contract_first(gathered_in, keyval_grads_all)
    normed_query = contract_last(grad_query_bf, query_full)
    normed_keyval = contract_last(grad_keyval_bf, keyval_full)
    grad_pre_attn = jnp.sum(normed_query * unit_all.astype(F32), axis=0) + jnp.sum(
        normed_keyval * unit_in, axis=0
    )
    grad_normed = group_scatter(lambda rows: rows, normed_query) + normed_keyval
    grad_in_norm, _ = rms_backward(block_in, inv_in, scale_pre_attn, grad_normed)
    grad_in = grad_resid_mid + grad_in_norm

    gain_grads = jnp.concatenate(
        [
            g.reshape(devices, -1)
            for g in (
                grad_pre_attn,
                grad_post_attn,
                grad_pre_ffn,
                grad_post_ffn,
                grad_gain_query,
                grad_gain_key,
            )
        ],
        axis=1,
    ).reshape(blocks, 2, 2, 2, per_owner)

    def choose(array, index, axis):
        return lax.dynamic_index_in_dim(array, index, axis, keepdims=False)

    gain_sums = choose(gain_grads, own_core, 1) + flip(choose(gain_grads, 1 - own_core, 1), CORE)
    gain_sums = choose(gain_sums, own_low, 2) + flip(choose(gain_sums, 1 - own_low, 2), LOW)

    def two_rows(sums):
        high = lax.reduce_precision(sums, 8, 7)
        pair = jnp.stack([high, sums - high], axis=-2)
        pair = jnp.pad(pair, [(0, 0)] * (pair.ndim - 2) + [(0, 6), (0, HD - per_owner)])
        return pair

    keyval_grads = grad_w_keyval.astype(BF).reshape(blocks, 2, 2, 2, small_rows, 2 * HD)
    keyval_grads = choose(choose(keyval_grads, own_core, 1), own_low, 2)
    keyval_grads = jnp.concatenate(
        [keyval_grads[..., :HD], keyval_grads[..., HD:], two_rows(gain_sums).astype(BF)], axis=2
    )
    extra = keyval_grads.shape[2]
    others = scatter_blocks(keyval_grads.reshape(blocks, 2 * extra, HD)).reshape(2, extra, HD)
    mine, theirs = choose(others, own_half, 0), choose(others, 1 - own_half, 0)
    gains_at = 2 * small_rows
    theirs = jnp.concatenate(
        [theirs[:gains_at], two_rows(theirs[gains_at, :per_owner] + theirs[gains_at + 1, :per_owner])]
    )
    others = mine + flip(theirs.astype(BF), HALF).astype(F32)
    owned_keyval = jnp.concatenate([others[:small_rows], others[small_rows:gains_at]], axis=1)
    owned_up = after(owned_up, others).astype(F32)
    owned_gains = others[gains_at, :per_owner] + others[gains_at + 1, :per_owner]
    return (
        block_out,
        grad_in,
        owned_query,
        owned_keyval,
        owned_out.T,
        owned_gate.astype(F32),
        owned_up,
        owned_down,
        owned_gains[:big],
        owned_gains[big : 2 * big],
        owned_gains[2 * big : 3 * big],
        owned_gains[3 * big : 4 * big],
        owned_gains[4 * big : 4 * big + little],
        owned_gains[4 * big + little :],
    )


def solution(mesh):
    return jax.shard_map(
        per_device,
        mesh=mesh,
        in_specs=(
            P(("dp", "tensor"), None),
            P(("dp", "tensor"), None),
            P(),
            P("dp", "tensor"),
            P(("dp", "tensor"), None),
            P("tensor", "dp"),
            P("dp", "tensor"),
            P("dp", "tensor"),
            P("tensor", "dp"),
            P(("dp", "tensor")),
            P(("dp", "tensor")),
            P(("dp", "tensor")),
            P(("dp", "tensor")),
            P(("dp", "tensor")),
            P(("dp", "tensor")),
        ),
        out_specs=(
            P(("dp", "tensor"), None),
            P(("dp", "tensor"), None),
            P("dp", "tensor"),
            P(("dp", "tensor"), None),
            P("tensor", "dp"),
            P("dp", "tensor"),
            P("dp", "tensor"),
            P("tensor", "dp"),
            P(("dp", "tensor")),
            P(("dp", "tensor")),
            P(("dp", "tensor")),
            P(("dp", "tensor")),
            P(("dp", "tensor")),
            P(("dp", "tensor")),
        ),
        check_vma=False,
    )
```

time: 580 us -> 480 us (0.83)
  waiting for transfers between devices: 246 us -> 179 us
  Pallas kernels: 0 us -> 44.4 us
  matrix products: 106 us -> 69.2 us
  local copies, waits for them, and re-layouts: 63.2 us -> 29.4 us
  blocking collectives: 15.1 us -> 0 us
  other arithmetic: 41.9 us -> 51.6 us
    pallas_call x0 -> x5, Pallas kernels: none -> 44.4 us  [the longest x1 13.6 us: keyval_grads_of(): pl.pallas_call(body, grid=(rows // length,), out_shape=jax.ShapeDtypeStru...]
    ppermute x58 -> x74, waiting for transfers between devices: 214 us -> 178 us  [the longest x70 178 us: flip(): lax.ppermute(value, AXES, [(s, s ^ mask) for s in range(device_count())])]
    dot_general x10 -> x7, matrix products: 53.8 us -> 25.2 us  [dot(): return jnp.dot(left, right, preferred_element_type=F32)]
    another operation x17 -> x0, local copies, waits for them, and re-layouts: 26.1 us -> none  [the longest x11 24.9 us: gather_blocks(): return jnp.stack(near + far)]
    all_gather x4 -> x3, waiting for transfers between devices: 21.1 us -> 0.01 us  [the longest x1 0.01 us: per_device(): gate_full = lax.all_gather(after(w_gate, near), 'dp', axis=0, tiled=True)]
    all_gather x1 -> x0, blocking collectives: 15.1 us -> none  [per_device(): small = lax.all_gather(small, 'tensor', axis=0, tiled=False)]
    reduce_scatter x1, waiting for transfers between devices: 9.22 us -> 0.01 us  [per_device(): lax.psum_scatter(grad_w_down, 'dp', scatter_dimension=1, tiled=True)]
    add x6 -> x13, other arithmetic: 1.18 us -> 7.46 us  [the longest x2 2.78 us: column_scatter(): return near + far[0].astype(F32) + far[1].astype(F32)]
  transfers between devices with their start and end apart: 66 -> 80, of which waited for: 33 -> 39; matrix products, arithmetic and copies ran while one was open for 29% -> 26% of each run, Pallas kernels for 0% -> 9%
where the time goes in v2:
time: 480 us; the launch traced here: 473 us
  waiting for transfers between devices  179 us (37%)
  starting transfers between devices  83.4 us (17%)
  matrix products  69.2 us (14%)
  other arithmetic  51.6 us (11%)
  Pallas kernels  44.4 us (9%)
  local copies, waits for them, and re-layouts  29.4 us (6%)
  between operations  16.2 us (3%)
    ppermute x70, waiting for transfers between devices, flip(): lax.ppermute(value, AXES, [(s, s ^ mask) for s in range(device_count())])  178 us
    ppermute x70, starting transfers between devices, flip(): lax.ppermute(value, AXES, [(s, s ^ mask) for s in range(device_count())])  78.6 us
    dot_general x7, matrix products, dot(): return jnp.dot(left, right, preferred_element_type=F32)  25.2 us
    dot_general x9, matrix products, contract_last(): lax.dot_general(left, right, (((1,), (1,)), ((), ())), preferred_element_...  23.3 us
    dot_general x6, matrix products, contract_first(): lax.dot_general(left, right, (((0,), (0,)), ((), ())), preferred_element_...  20.7 us
    pallas_call x1, Pallas kernels, keyval_grads_of(): pl.pallas_call(body, grid=(rows // length,), out_shape=jax.ShapeDtypeStru...  13.6 us
    pallas_call x1, Pallas kernels, query_grads(): pl.pallas_call(body, grid=(rows // length,), out_shape=jax.ShapeDtypeStru...  12.4 us
    pallas_call x1, Pallas kernels, attend(): pl.pallas_call(body, grid=(rows // length,), out_shape=(jax.ShapeDtypeStr...  11.7 us
  transfers between devices with their start and end apart: 80, of which 39 were waited for; matrix products, arithmetic and copies ran while one was open for 26% of the time, Pallas kernels for 9%

profile of v2, /device:TPU:0, one launch (start us, length us, event | category | flops | bytes accessed | tf_op | source)
XLA Modules:
  0.0 473.4 jit_solution(18259760375186710767)
XLA Ops:
  8.9 5.1 %collective-permute-start.5 = (bf16[40,512]{1,0:T(8,128)(2,1)S(1)}, bf16[40,512]{1,0:T(8,128)(2,1)S(1)}, u32[]{:S(2)}, u32[]{:S(2)}) collective-permute-start(bf16[40,512]{1,0:T(8,128)(2,1)S(1)} %add_convert_fusion), channel_id=1, source_target_pairs={{0,3},{1,2},{2,1},{3,0},{4,7},{5,6},{6,5},{7,4},{8,11},{9,10},{10,... | collective-permute-start | bytes 122888 | tf_op jit(solution)/shard_map/ppermute | solution.py:96
  16.0 2.9 collective-permute-done.4
  19.0 2.5 collective-permute-start.8
  22.5 4.5 collective-permute-done.8
  28.2 2.1 collective-permute-start.11
  33.7 2.7 fusion.33
  36.4 6.4 %collective-permute-done = bf16[128,1152]{1,0:T(8,128)(2,1)S(1)} collective-permute-done((bf16[128,1152]{1,0:T(8,128)(2,1)S(1)}, bf16[128,1152]{1,0:T(8,128)(2,1)S(1)}, u32[]{:S(2)}, u32[]{:S(2)}) %collective-permute-start) | collective-permute-done | bytes 294944 | tf_op jit(solution)/shard_map/ppermute | solution.py:96
  44.0 1.7 collective-permute-start.14
  48.8 3.3 shard_map.254
  57.8 1.9 collective-permute-start.16
  59.7 2.3 collective-permute-start.15
  61.9 4.9 %collective-permute-done.13 = bf16[288,512]{1,0:T(8,128)(2,1)} collective-permute-done((bf16[288,512]{1,0:T(8,128)(2,1)}, bf16[288,512]{1,0:T(8,128)(2,1)}, u32[]{:S(2)}, u32[]{:S(2)}) %collective-permute-start.13) | collective-permute-done | bytes 294944 | tf_op jit(solution)/shard_map/ppermute | solution.py:96
  66.9 4.1 collective-permute-done.12
  70.9 2.4 pad_maximum_fusion.1.item_ref
  73.3 3.4 shard_map.255
  84.1 2.9 fusion.36.query_ref.refs_0_
  87.0 8.3 %collective-permute-done.18.refs_1_ = bf16[512,512]{1,0:T(8,128)(2,1)S(1)} collective-permute-done((bf16[512,512]{1,0:T(8,128)(2,1)S(1)}, bf16[512,512]{1,0:T(8,128)(2,1)S(1)}, u32[]{:S(2)}, u32[]{:S(2)}) %collective-permute-start.18) | collective-permute-done | bytes 524320 | tf_op jit(solution)/shard_map/ppermute | solution.py:96
  95.3 8.7 %collective-permute-done.19.refs_2_ = bf16[512,512]{1,0:T(8,128)(2,1)S(1)} collective-permute-done((bf16[512,512]{1,0:T(8,128)(2,1)S(1)}, bf16[512,512]{1,0:T(8,128)(2,1)S(1)}, u32[]{:S(2)}, u32[]{:S(2)}) %collective-permute-start.19) | collective-permute-done | bytes 524320 | tf_op jit(solution)/shard_map/ppermute | solution.py:96
  109.9 11.7 %shard_map.256 = (bf16[512,256]{1,0:T(8,128)(2,1)}, f32[512,1]{1,0:T(8,128)}) custom-call(s32[1]{0:T(128)} %bitcast.index_ref.device_ref, s32[32,128]{1,0:T(8,128)} %bitcast.121, bf16[512,256]{1,0:T(8,128)(2,1)} %fusion.36.query_ref.refs_0_, bf16[512,512]{1,0:T(8,128)(2,1)} %copy-done.11, bf16[512,512]{1,0:T(8,128)(2,1)} %copy-done.22, ...), custom_call_target="tpu_custom_call" | custom-call | tf_op jit(solution)/shard_map/pallas_call | solution.py:357
  123.1 2.1 collective-permute-done.25
  128.8 6.8 %collective-permute-done.26 = bf16[128,1152]{1,0:T(8,128)(2,1)S(1)} collective-permute-done((bf16[128,1152]{1,0:T(8,128)(2,1)S(1)}, bf16[128,1152]{1,0:T(8,128)(2,1)S(1)}, u32[]{:S(2)}, u32[]{:S(2)}) %collective-permute-start.26) | collective-permute-done | bytes 294944 | tf_op jit(solution)/shard_map/ppermute | solution.py:96
  137.4 1.7 collective-permute-start.28
  139.1 2.6 collective-permute-start.27
  141.7 7.5 %collective-permute-done.29 = bf16[128,1152]{1,0:T(8,128)(2,1)S(1)} collective-permute-done((bf16[128,1152]{1,0:T(8,128)(2,1)S(1)}, bf16[128,1152]{1,0:T(8,128)(2,1)S(1)}, u32[]{:S(2)}, u32[]{:S(2)}) %collective-permute-start.29) | collective-permute-done | bytes 294944 | tf_op jit(solution)/shard_map/ppermute | solution.py:96
  149.2 22.4 %collective-permute-done.28 = bf16[128,1152]{1,0:T(8,128)(2,1)S(1)} collective-permute-done((bf16[128,1152]{1,0:T(8,128)(2,1)S(1)}, bf16[128,1152]{1,0:T(8,128)(2,1)S(1)}, u32[]{:S(2)}, u32[]{:S(2)}) %collective-permute-start.28) | collective-permute-done | bytes 294944 | tf_op jit(solution)/shard_map/ppermute | solution.py:96
  172.3 6.8 %fusion.71 = f32[512,1728]{0,1:T(8,128)} fusion(bf16[1152,1728]{1,0:T(8,128)(2,1)} %all-gather.4.cloned.1.call-done, bf16[128,1152]{1,0:T(8,128)(2,1)} %copy-done.95, bf16[128,1152]{1,0:T(8,128)(2,1)} %copy-done.97, bf16[128,1152]{1,0:T(8,128)(2,1)} %collective-permute-done.27, bf16[128,1152]{1,0:T(8,128)(2,1)S(1)} %multiply_convert_fusion.2), kind=kOutput, calls=%fused_computation.240 | convolution fusion | flops 2043150336 | bytes 8699904 | tf_op jit(solution)/shard_map/dot_general | solution.py:65
  179.1 9.2 %multiply_convert_fusion.1 = (bf16[512,1728]{0,1:T(8,128)(2,1)}, f32[512,1728]{0,1:T(8,128)}) fusion(f32[512,1728]{0,1:T(8,128)} %fusion.71, bf16[1152,1728]{1,0:T(8,128)(2,1)} %all-gather.6.cloned.1.call-done, bf16[128,1152]{1,0:T(8,128)(2,1)} %copy-done.95, bf16[128,1152]{1,0:T(8,128)(2,1)} %copy-done.97, bf16[128,1152]{1,0:T(8,128)(2,1)} %collective-permute-done.27, ...), kind=kOutput, calls=%fused_computation.13 | convolution fusion | flops 2051997696 | bytes 14008320 | tf_op jit(solution)/shard_map/dot_general | solution.py:65
  189.0 4.0 convolution_convert_fusion.6
  198.0 2.6 collective-permute-start.31
  204.4 3.0 collective-permute-done.34.refs_1_
  207.4 2.3 collective-permute-start.36
  209.7 3.7 collective-permute-done.33
  215.7 1.9 collective-permute-done.31
  220.7 2.1 collective-permute-done.37.refs_5_
  222.8 5.6 %collective-permute-done.38.refs_6_ = bf16[512,256]{1,0:T(8,128)(2,1)S(1)} collective-permute-done((bf16[512,256]{1,0:T(8,128)(2,1)}, bf16[512,256]{1,0:T(8,128)(2,1)S(1)}, u32[]{:S(2)}, u32[]{:S(2)}) %collective-permute-start.38) | collective-permute-done | bytes 262176 | tf_op jit(solution)/shard_map/ppermute | solution.py:96
  230.4 2.3 collective-permute-start.42
  232.7 5.2 %collective-permute-start.41 = (bf16[128,1152]{1,0:T(8,128)(2,1)S(1)}, bf16[128,1152]{1,0:T(8,128)(2,1)S(1)}, u32[]{:S(2)}, u32[]{:S(2)}) collective-permute-start(bf16[128,1152]{1,0:T(8,128)(2,1)S(1)} %get-tuple-element.90), channel_id=1, source_target_pairs={{0,2},{1,3},{2,0},{3,1},{4,6},{5,7},{6,4},{7,5},{8,10},{9,11},{10,... | collective-permute-start | bytes 884744 | tf_op jit(solution)/shard_map/ppermute | solution.py:96
  237.9 2.7 collective-permute-done.42
  240.6 18.4 %collective-permute-done.41 = bf16[128,1152]{1,0:T(8,128)(2,1)S(1)} collective-permute-done((bf16[128,1152]{1,0:T(8,128)(2,1)S(1)}, bf16[128,1152]{1,0:T(8,128)(2,1)S(1)}, u32[]{:S(2)}, u32[]{:S(2)}) %collective-permute-start.41) | collective-permute-done | bytes 294944 | tf_op jit(solution)/shard_map/ppermute | solution.py:96
  259.8 4.4 convolution_convert_fusion.2
  266.3 10.0 %multiply_convert_fusion = (bf16[512,1728]{0,1:T(8,128)(2,1)}, bf16[512,1728]{0,1:T(8,128)(2,1)S(1)}) fusion(f32[512,1728]{0,1:T(8,128)} %fusion.71, f32[512,1728]{0,1:T(8,128)} %get-tuple-element.158, bf16[512,1152]{1,0:T(8,128)(2,1)S(1)} %pad_maximum_fusion.3, bf16[1728,1152]{0,1:T(8,128)(2,1)} %all-gather.8.cloned.1.call-done), kind=kOutput, calls=%fused_computation.12 | convolution fusion | flops 2058780672 | bytes 15777792 | tf_op jit(solution)/shard_map/dot_general | solution.py:73
  277.6 5.3 %convolution_convert_fusion.1 = bf16[1152,1728]{1,0:T(8,128)(2,1)} fusion(bf16[512,1728]{0,1:T(8,128)(2,1)S(1)} %get-tuple-element.86, bf16[128,1152]{1,0:T(8,128)(2,1)S(1)} %copy-done.96, bf16[128,1152]{1,0:T(8,128)(2,1)S(1)} %copy-done.98, bf16[128,1152]{1,0:T(8,128)(2,1)} %collective-permute-done.27, bf16[128,1152]{1,0:T(8,128)(2,1)S(1)} %copy-done.51), kind=kOutput, calls=%fused_computation.1 | convolution fusion | flops 2045140992 | bytes 6930432 | tf_op jit(solution)/shard_map/dot_general | solution.py:69
  283.2 4.3 fusion.15
  295.8 2.1 collective-permute-start.43
  299.1 12.7 %collective-permute-done.45 = bf16[128,1152]{1,0:T(8,128)(2,1)S(1)} collective-permute-done((bf16[128,1152]{1,0:T(8,128)(2,1)}, bf16[128,1152]{1,0:T(8,128)(2,1)S(1)}, u32[]{:S(2)}, u32[]{:S(2)}) %collective-permute-start.45) | collective-permute-done | bytes 294944 | tf_op jit(solution)/shard_map/ppermute | solution.py:96
  311.9 5.3 %collective-permute-done.43 = bf16[128,1152]{1,0:T(8,128)(2,1)} collective-permute-done((bf16[128,1152]{1,0:T(8,128)(2,1)S(1)}, bf16[128,1152]{1,0:T(8,128)(2,1)}, u32[]{:S(2)}, u32[]{:S(2)}) %collective-permute-start.43) | collective-permute-done | bytes 294944 | tf_op jit(solution)/shard_map/ppermute | solution.py:96
  324.1 5.5 %collective-permute-done.46 = bf16[128,1152]{1,0:T(8,128)(2,1)} collective-permute-done((bf16[128,1152]{1,0:T(8,128)(2,1)S(1)}, bf16[128,1152]{1,0:T(8,128)(2,1)}, u32[]{:S(2)}, u32[]{:S(2)}) %collective-permute-start.46) | collective-permute-done | bytes 294944 | tf_op jit(solution)/shard_map/ppermute | solution.py:96
  329.6 6.5 %convolution_convert_fusion = bf16[1152,1728]{1,0:T(8,128)(2,1)} fusion(bf16[512,1728]{0,1:T(8,128)(2,1)} %get-tuple-element.85, bf16[128,1152]{1,0:T(8,128)(2,1)} %copy-done.95, bf16[128,1152]{1,0:T(8,128)(2,1)} %copy-done.97, bf16[128,1152]{1,0:T(8,128)(2,1)} %collective-permute-done.27, bf16[128,1152]{1,0:T(8,128)(2,1)} %copy-done.50), kind=kOutput, calls=%fused_computation | convolution fusion | flops 2045140992 | bytes 6930432 | tf_op jit(solution)/shard_map/dot_general | solution.py:69
  345.8 2.8 collective-permute-start.54
  348.5 12.4 %shard_map.257 = f32[512,256]{1,0:T(8,128)} custom-call(s32[1]{0:T(128)} %bitcast.index_ref.device_ref, s32[32,128]{1,0:T(8,128)} %bitcast.122, bf16[512,256]{1,0:T(8,128)(2,1)} %fusion.36.query_ref.refs_0_, bf16[512,256]{1,0:T(8,128)(2,1)} %copy-done.36, bf16[512,256]{1,0:T(8,128)(2,1)} %get-tuple-element.51.mixed_ref, f32[512,1]{1,0:T(8,128)} %get-tuple-element.61.log_ref, ...), custom_call_target="tpu_custom_call" | custom-call | tf_op jit(solution)/shard_map/pallas_call | solution.py:390
  361.0 2.8 fusion.53
  370.2 2.4 collective-permute-start.57
  374.0 2.1 convert_element_type.254
  376.1 7.5 %collective-permute-done.55.refs_13_ = bf16[528,256]{1,0:T(8,128)(2,1)S(1)} collective-permute-done((bf16[528,256]{1,0:T(8,128)(2,1)}, bf16[528,256]{1,0:T(8,128)(2,1)S(1)}, u32[]{:S(2)}, u32[]{:S(2)}) %collective-permute-start.55) | collective-permute-done | bytes 270368 | tf_op jit(solution)/shard_map/ppermute | solution.py:96
  383.6 5.9 %collective-permute-done.56.refs_14_ = bf16[528,256]{1,0:T(8,128)(2,1)} collective-permute-done((bf16[528,256]{1,0:T(8,128)(2,1)}, bf16[528,256]{1,0:T(8,128)(2,1)}, u32[]{:S(2)}, u32[]{:S(2)}) %collective-permute-start.56) | collective-permute-done | bytes 270368 | tf_op jit(solution)/shard_map/ppermute | solution.py:96
  389.5 13.6 %shard_map.258 = f32[512,512]{1,0:T(8,128)} custom-call(s32[1]{0:T(128)} %bitcast.index_ref.device_ref, s32[32,128]{1,0:T(8,128)} %bitcast.123, bf16[512,512]{1,0:T(8,128)(2,1)} %pad_maximum_fusion.10.keyval_ref, bf16[512,256]{1,0:T(8,128)(2,1)} %fusion.36.query_ref.refs_0_, bf16[512,256]{1,0:T(8,128)(2,1)} %collective-permute-done.34.refs_1_, ...), custom_call_target="tpu_custom_call" | custom-call | tf_op jit(solution)/shard_map/pallas_call | solution.py:435
  411.4 2.1 convert_element_type.274
  416.3 11.1 %collective-permute-done.61 = bf16[576,256]{1,0:T(8,128)(2,1)} collective-permute-done((bf16[576,256]{1,0:T(8,128)(2,1)S(1)}, bf16[576,256]{1,0:T(8,128)(2,1)}, u32[]{:S(2)}, u32[]{:S(2)}) %collective-permute-start.61) | collective-permute-done | bytes 294944 | tf_op jit(solution)/shard_map/ppermute | solution.py:96
  434.5 3.7 collective-permute-start.64
  441.7 1.7 collective-permute-start.69
  443.4 2.0 subtract_add_fusion
  446.8 1.8 convolution_convert_fusion.3
  458.1 4.1 collective-permute-done.73
  463.4 2.1 convert_element_type.275
  (477 shorter events, 128.5 us)
Async XLA Ops:
  7.2 165.1 %all-gather.4.cloned.1.call-start = ((), (), s32[]{:S(2)}) async-start(), calls=%async_computation.3 | async-start | bytes 4644864 | tf_op jit(solution)/shard_map/all_gather | solution.py:494
  8.9 7.1 %collective-permute-start.5 = (bf16[40,512]{1,0:T(8,128)(2,1)S(1)}, bf16[40,512]{1,0:T(8,128)(2,1)S(1)}, u32[]{:S(2)}, u32[]{:S(2)}) collective-permute-start(bf16[40,512]{1,0:T(8,128)(2,1)S(1)} %add_convert_fusion), channel_id=1, source_target_pairs={{0,3},{1,2},{2,1},{3,0},{4,7},{5,6},{6,5},{7,4},{8,11},{9,10},{10,... | collective-permute-start | bytes 122888 | tf_op jit(solution)/shard_map/ppermute | solution.py:96
  19.0 8.0 %collective-permute-start.8 = (bf16[4,40,512]{2,1,0:T(8,128)(2,1)S(1)}, bf16[4,40,512]{2,1,0:T(8,128)(2,1)S(1)}, u32[]{:S(2)}, u32[]{:S(2)}) collective-permute-start(bf16[4,40,512]{2,1,0:T(8,128)(2,1)S(1)} %get-tuple-element.114), channel_id=1, source_target_pairs={{0,24},{1,25},{2,26},{3,27},{4,28},{5,29},{6,30},{7,31},{8,16},{9,... | collective-permute-start | bytes 491528 | tf_op jit(solution)/shard_map/ppermute | solution.py:96
  21.5 6.5 %collective-permute-start.7 = (bf16[4,40,512]{2,1,0:T(8,128)(2,1)S(1)}, bf16[4,40,512]{2,1,0:T(8,128)(2,1)S(1)}, u32[]{:S(2)}, u32[]{:S(2)}) collective-permute-start(bf16[4,40,512]{2,1,0:T(8,128)(2,1)S(1)} %get-tuple-element.114), channel_id=1, source_target_pairs={{0,16},{1,17},{2,18},{3,19},{4,20},{5,21},{6,22},{7,23},{8,24},{9,... | collective-permute-start | bytes 491528 | tf_op jit(solution)/shard_map/ppermute | solution.py:96
  28.2 150.9 %all-gather.6.cloned.1.call-start = ((), (), s32[]{:S(2)}) async-start(), calls=%async_computation.4 | async-start | bytes 4644864 | tf_op jit(solution)/shard_map/all_gather | solution.py:529
  28.2 15.0 %collective-permute-start.11 = (bf16[144,512]{1,0:T(8,128)(2,1)S(1)}, bf16[144,512]{1,0:T(8,128)(2,1)S(1)}, u32[]{:S(2)}, u32[]{:S(2)}) collective-permute-start(bf16[144,512]{1,0:T(8,128)(2,1)S(1)} %pad_maximum_fusion.14), channel_id=1, source_target_pairs={{0,2},{1,3},{2,6},{3,7},{4,0},{5,1},{6,4},{7,5},{8,10},{9,11},{10,... | collective-permute-start | bytes 442376 | tf_op jit(solution)/shard_map/ppermute | solution.py:101
  30.3 12.9 %collective-permute-start.10 = (bf16[144,512]{1,0:T(8,128)(2,1)S(1)}, bf16[144,512]{1,0:T(8,128)(2,1)S(1)}, u32[]{:S(2)}, u32[]{:S(2)}) collective-permute-start(bf16[144,512]{1,0:T(8,128)(2,1)S(1)} %pad_maximum_fusion.14), channel_id=1, source_target_pairs={{2,4},{3,5},{4,2},{5,3},{10,12},{11,13},{12,10},{13,11},{18,20},{1... | collective-permute-start | bytes 442376 | tf_op jit(solution)/shard_map/ppermute | solution.py:101
  31.8 11.0 %collective-permute-start = (bf16[128,1152]{1,0:T(8,128)(2,1)S(1)}, bf16[128,1152]{1,0:T(8,128)(2,1)S(1)}, u32[]{:S(2)}, u32[]{:S(2)}) collective-permute-start(bf16[128,1152]{1,0:T(8,128)(2,1)S(1)} %multiply_convert_fusion.4), channel_id=1, source_target_pairs={{0,1},{1,0},{2,3},{3,2},{4,5},{5,4},{6,7},{7,6},{8,9},{9,8},{10,11... | collective-permute-start | bytes 884744 | tf_op jit(solution)/shard_map/ppermute | solution.py:96
  32.4 14.7 %collective-permute-start.1 = (bf16[128,1152]{1,0:T(8,128)(2,1)S(1)}, bf16[128,1152]{1,0:T(8,128)(2,1)S(1)}, u32[]{:S(2)}, u32[]{:S(2)}) collective-permute-start(bf16[128,1152]{1,0:T(8,128)(2,1)S(1)} %multiply_convert_fusion.4), channel_id=1, source_target_pairs={{0,4},{1,5},{2,6},{3,7},{4,0},{5,1},{6,2},{7,3},{8,12},{9,13},{10,... | collective-permute-start | bytes 884744 | tf_op jit(solution)/shard_map/ppermute | solution.py:96
  33.7 15.2 %collective-permute-start.9 = (bf16[4,4,40,512]{3,2,1,0:T(8,128)(2,1)S(1)}, bf16[4,4,40,512]{3,2,1,0:T(8,128)(2,1)}, u32[]{:S(2)}, u32[]{:S(2)}) collective-permute-start(bf16[4,4,40,512]{3,2,1,0:T(8,128)(2,1)S(1)} %pad_maximum_fusion.6.near_ref), channel_id=1, source_target_pairs={{0,4},{1,5},{2,6},{3,7},{4,0},{5,1},{6,2},{7,3},{8,12},{9,13},{10,... | collective-permute-start | bytes 1966088 | tf_op jit(solution)/shard_map/ppermute | solution.py:96
  44.0 15.6 %collective-permute-start.14 = (bf16[288,512]{1,0:T(8,128)(2,1)}, bf16[288,512]{1,0:T(8,128)(2,1)}, u32[]{:S(2)}, u32[]{:S(2)}) collective-permute-start(bf16[288,512]{1,0:T(8,128)(2,1)} %pad_maximum_fusion.12), channel_id=1, source_target_pairs={{0,24},{1,25},{2,26},{3,27},{4,28},{5,29},{6,30},{7,31},{8,16},{9,... | collective-permute-start | bytes 884744 | tf_op jit(solution)/shard_map/ppermute | solution.py:96
  45.7 21.1 %collective-permute-start.13 = (bf16[288,512]{1,0:T(8,128)(2,1)}, bf16[288,512]{1,0:T(8,128)(2,1)}, u32[]{:S(2)}, u32[]{:S(2)}) collective-permute-start(bf16[288,512]{1,0:T(8,128)(2,1)} %pad_maximum_fusion.12), channel_id=1, source_target_pairs={{0,16},{1,17},{2,18},{3,19},{4,20},{5,21},{6,22},{7,23},{8,24},{9,... | collective-permute-start | bytes 884744 | tf_op jit(solution)/shard_map/ppermute | solution.py:96
  47.0 23.9 %collective-permute-start.12 = (bf16[288,512]{1,0:T(8,128)(2,1)}, bf16[288,512]{1,0:T(8,128)(2,1)}, u32[]{:S(2)}, u32[]{:S(2)}) collective-permute-start(bf16[288,512]{1,0:T(8,128)(2,1)} %pad_maximum_fusion.12), channel_id=1, source_target_pairs={{0,8},{1,9},{2,10},{3,11},{4,12},{5,13},{6,14},{7,15},{8,0},{9,1},... | collective-permute-start | bytes 884744 | tf_op jit(solution)/shard_map/ppermute | solution.py:96
  57.5 21.8 %collective-permute-start.17 = (bf16[128,512]{1,0:T(8,128)(2,1)S(1)}, bf16[128,512]{1,0:T(8,128)(2,1)}, u32[]{:S(2)}, u32[]{:S(2)}) collective-permute-start(bf16[128,512]{1,0:T(8,128)(2,1)S(1)} %pad_maximum_fusion.15), channel_id=1, source_target_pairs={{0,3},{1,2},{2,1},{3,0},{4,7},{5,6},{6,5},{7,4},{8,11},{9,10},{10,... | collective-permute-start | bytes 393224 | tf_op jit(solution)/shard_map/ppermute | solution.py:96
  57.8 21.5 %collective-permute-start.16 = (bf16[128,512]{1,0:T(8,128)(2,1)S(1)}, bf16[128,512]{1,0:T(8,128)(2,1)}, u32[]{:S(2)}, u32[]{:S(2)}) collective-permute-start(bf16[128,512]{1,0:T(8,128)(2,1)S(1)} %pad_maximum_fusion.15), channel_id=1, source_target_pairs={{0,2},{1,3},{2,0},{3,1},{4,6},{5,7},{6,4},{7,5},{8,10},{9,11},{10,... | collective-permute-start | bytes 393224 | tf_op jit(solution)/shard_map/ppermute | solution.py:96
  59.7 19.6 %collective-permute-start.15 = (bf16[128,512]{1,0:T(8,128)(2,1)S(1)}, bf16[128,512]{1,0:T(8,128)(2,1)S(1)}, u32[]{:S(2)}, u32[]{:S(2)}) collective-permute-start(bf16[128,512]{1,0:T(8,128)(2,1)S(1)} %pad_maximum_fusion.15), channel_id=1, source_target_pairs={{0,1},{1,0},{2,3},{3,2},{4,5},{5,4},{6,7},{7,6},{8,9},{9,8},{10,11... | collective-permute-start | bytes 393224 | tf_op jit(solution)/shard_map/ppermute | solution.py:96
  80.4 14.9 %collective-permute-start.18 = (bf16[512,512]{1,0:T(8,128)(2,1)S(1)}, bf16[512,512]{1,0:T(8,128)(2,1)S(1)}, u32[]{:S(2)}, u32[]{:S(2)}) collective-permute-start(bf16[512,512]{1,0:T(8,128)(2,1)S(1)} %pad_maximum_fusion.8.refs_0_), channel_id=1, source_target_pairs={{0,8},{1,9},{2,10},{3,11},{4,12},{5,13},{6,14},{7,15},{8,0},{9,1},... | collective-permute-start | bytes 1572872 | tf_op jit(solution)/shard_map/ppermute | solution.py:96
  81.7 22.3 %collective-permute-start.19 = (bf16[512,512]{1,0:T(8,128)(2,1)S(1)}, bf16[512,512]{1,0:T(8,128)(2,1)S(1)}, u32[]{:S(2)}, u32[]{:S(2)}) collective-permute-start(bf16[512,512]{1,0:T(8,128)(2,1)S(1)} %pad_maximum_fusion.8.refs_0_), channel_id=1, source_target_pairs={{0,16},{1,17},{2,18},{3,19},{4,20},{5,21},{6,22},{7,23},{8,24},{9,... | collective-permute-start | bytes 1572872 | tf_op jit(solution)/shard_map/ppermute | solution.py:96
  82.6 21.4 %collective-permute-start.20 = (bf16[512,512]{1,0:T(8,128)(2,1)S(1)}, bf16[512,512]{1,0:T(8,128)(2,1)S(1)}, u32[]{:S(2)}, u32[]{:S(2)}) collective-permute-start(bf16[512,512]{1,0:T(8,128)(2,1)S(1)} %pad_maximum_fusion.8.refs_0_), channel_id=1, source_target_pairs={{0,24},{1,25},{2,26},{3,27},{4,28},{5,29},{6,30},{7,31},{8,16},{9,... | collective-permute-start | bytes 1572872 | tf_op jit(solution)/shard_map/ppermute | solution.py:96
  104.0 85.0 %all-gather.8.cloned.1.call-start = ((), (), s32[]{:S(2)}) async-start(), calls=%async_computation.5 | async-start | bytes 4644864 | tf_op jit(solution)/shard_map/all_gather | solution.py:530
  104.8 269.2 %reduce-scatter.4.cloned.1.call-start = ((), (), s32[]{:S(2)}) async-start(), calls=%async_computation.6 | async-start | bytes 4644864 | tf_op jit(solution)/shard_map/reduce_scatter | solution.py:557
  126.5 9.2 %collective-permute-start.26 = (bf16[128,1152]{1,0:T(8,128)(2,1)S(1)}, bf16[128,1152]{1,0:T(8,128)(2,1)S(1)}, u32[]{:S(2)}, u32[]{:S(2)}) collective-permute-start(bf16[128,1152]{1,0:T(8,128)(2,1)S(1)} %slice.484), channel_id=1, source_target_pairs={{0,1},{1,0},{2,3},{3,2},{4,5},{5,4},{6,7},{7,6},{8,9},{9,8},{10,11... | collective-permute-start | bytes 884744 | tf_op jit(solution)/shard_map/ppermute | solution.py:96
  137.3 11.9 %collective-permute-start.29 = (bf16[128,1152]{1,0:T(8,128)(2,1)S(1)}, bf16[128,1152]{1,0:T(8,128)(2,1)S(1)}, u32[]{:S(2)}, u32[]{:S(2)}) collective-permute-start(bf16[128,1152]{1,0:T(8,128)(2,1)S(1)} %multiply_convert_fusion.2), channel_id=1, source_target_pairs={{0,3},{1,2},{2,1},{3,0},{4,7},{5,6},{6,5},{7,4},{8,11},{9,10},{10,... | collective-permute-start | bytes 884744 | tf_op jit(solution)/shard_map/ppermute | solution.py:96
  137.4 34.2 %collective-permute-start.28 = (bf16[128,1152]{1,0:T(8,128)(2,1)S(1)}, bf16[128,1152]{1,0:T(8,128)(2,1)S(1)}, u32[]{:S(2)}, u32[]{:S(2)}) collective-permute-start(bf16[128,1152]{1,0:T(8,128)(2,1)S(1)} %multiply_convert_fusion.2), channel_id=1, source_target_pairs={{0,2},{1,3},{2,0},{3,1},{4,6},{5,7},{6,4},{7,5},{8,10},{9,11},{10,... | collective-permute-start | bytes 884744 | tf_op jit(solution)/shard_map/ppermute | solution.py:96
  139.1 33.2 %collective-permute-start.27 = (bf16[128,1152]{1,0:T(8,128)(2,1)S(1)}, bf16[128,1152]{1,0:T(8,128)(2,1)}, u32[]{:S(2)}, u32[]{:S(2)}) collective-permute-start(bf16[128,1152]{1,0:T(8,128)(2,1)S(1)} %multiply_convert_fusion.2), channel_id=1, source_target_pairs={{0,1},{1,0},{2,3},{3,2},{4,5},{5,4},{6,7},{7,6},{8,9},{9,8},{10,11... | collective-permute-start | bytes 884744 | tf_op jit(solution)/shard_map/ppermute | solution.py:96
  141.7 46.5 %collective-permute-start.30 = (bf16[512,256]{1,0:T(8,128)(2,1)}, bf16[512,256]{1,0:T(8,128)(2,1)S(1)}, u32[]{:S(2)}, u32[]{:S(2)}) collective-permute-start(bf16[512,256]{1,0:T(8,128)(2,1)} %fusion.36.query_ref.refs_0_), channel_id=1, source_target_pairs={{0,2},{1,3},{2,0},{3,1},{4,6},{5,7},{6,4},{7,5},{8,10},{9,11},{10,... | collective-permute-start | bytes 786440 | tf_op jit(solution)/shard_map/ppermute | solution.py:96
  193.9 19.5 %collective-permute-start.33 = (bf16[128,1152]{1,0:T(8,128)(2,1)}, bf16[128,1152]{1,0:T(8,128)(2,1)}, u32[]{:S(2)}, u32[]{:S(2)}) collective-permute-start(bf16[128,1152]{1,0:T(8,128)(2,1)} %get-tuple-element.95), channel_id=1, source_target_pairs={{0,2},{1,3},{2,0},{3,1},{4,6},{5,7},{6,4},{7,5},{8,10},{9,11},{10,... | collective-permute-start | bytes 884744 | tf_op jit(solution)/shard_map/ppermute | solution.py:96
  193.9 20.9 %collective-permute-start.32 = (bf16[128,1152]{1,0:T(8,128)(2,1)}, bf16[128,1152]{1,0:T(8,128)(2,1)}, u32[]{:S(2)}, u32[]{:S(2)}) collective-permute-start(bf16[128,1152]{1,0:T(8,128)(2,1)} %get-tuple-element.94), channel_id=1, source_target_pairs={{0,3},{1,2},{2,1},{3,0},{4,7},{5,6},{6,5},{7,4},{8,11},{9,10},{10,... | collective-permute-start | bytes 884744 | tf_op jit(solution)/shard_map/ppermute | solution.py:96
  198.0 19.5 %collective-permute-start.31 = (bf16[128,1152]{1,0:T(8,128)(2,1)}, bf16[128,1152]{1,0:T(8,128)(2,1)}, u32[]{:S(2)}, u32[]{:S(2)}) collective-permute-start(bf16[128,1152]{1,0:T(8,128)(2,1)} %slice.483), channel_id=1, source_target_pairs={{0,1},{1,0},{2,3},{3,2},{4,5},{5,4},{6,7},{7,6},{8,9},{9,8},{10,11... | collective-permute-start | bytes 884744 | tf_op jit(solution)/shard_map/ppermute | solution.py:96
  200.6 6.8 %collective-permute-start.34 = (bf16[512,256]{1,0:T(8,128)(2,1)}, bf16[512,256]{1,0:T(8,128)(2,1)}, u32[]{:S(2)}, u32[]{:S(2)}) collective-permute-start(bf16[512,256]{1,0:T(8,128)(2,1)} %fusion.36.query_ref.refs_0_), channel_id=1, source_target_pairs={{0,8},{1,9},{2,10},{3,11},{4,12},{5,13},{6,14},{7,15},{8,0},{9,1},... | collective-permute-start | bytes 786440 | tf_op jit(solution)/shard_map/ppermute | solution.py:96
  202.1 18.5 %collective-permute-start.35 = (bf16[512,256]{1,0:T(8,128)(2,1)}, bf16[512,256]{1,0:T(8,128)(2,1)}, u32[]{:S(2)}, u32[]{:S(2)}) collective-permute-start(bf16[512,256]{1,0:T(8,128)(2,1)} %fusion.36.query_ref.refs_0_), channel_id=1, source_target_pairs={{0,16},{1,17},{2,18},{3,19},{4,20},{5,21},{6,22},{7,23},{8,24},{9,... | collective-permute-start | bytes 786440 | tf_op jit(solution)/shard_map/ppermute | solution.py:96
  207.4 13.2 %collective-permute-start.36 = (bf16[512,256]{1,0:T(8,128)(2,1)}, bf16[512,256]{1,0:T(8,128)(2,1)S(1)}, u32[]{:S(2)}, u32[]{:S(2)}) collective-permute-start(bf16[512,256]{1,0:T(8,128)(2,1)} %fusion.36.query_ref.refs_0_), channel_id=1, source_target_pairs={{0,24},{1,25},{2,26},{3,27},{4,28},{5,29},{6,30},{7,31},{8,16},{9,... | collective-permute-start | bytes 786440 | tf_op jit(solution)/shard_map/ppermute | solution.py:96
  213.4 9.4 %collective-permute-start.37 = (bf16[512,256]{1,0:T(8,128)(2,1)}, bf16[512,256]{1,0:T(8,128)(2,1)S(1)}, u32[]{:S(2)}, u32[]{:S(2)}) collective-permute-start(bf16[512,256]{1,0:T(8,128)(2,1)} %copy-done.55), channel_id=1, source_target_pairs={{0,8},{1,9},{2,10},{3,11},{4,12},{5,13},{6,14},{7,15},{8,0},{9,1},... | collective-permute-start | bytes 786440 | tf_op jit(solution)/shard_map/ppermute | solution.py:96
  214.7 13.7 %collective-permute-start.38 = (bf16[512,256]{1,0:T(8,128)(2,1)}, bf16[512,256]{1,0:T(8,128)(2,1)S(1)}, u32[]{:S(2)}, u32[]{:S(2)}) collective-permute-start(bf16[512,256]{1,0:T(8,128)(2,1)} %copy-done.55), channel_id=1, source_target_pairs={{0,16},{1,17},{2,18},{3,19},{4,20},{5,21},{6,22},{7,23},{8,24},{9,... | collective-permute-start | bytes 786440 | tf_op jit(solution)/shard_map/ppermute | solution.py:96
  217.6 10.9 %collective-permute-start.39 = (bf16[512,256]{1,0:T(8,128)(2,1)}, bf16[512,256]{1,0:T(8,128)(2,1)S(1)}, u32[]{:S(2)}, u32[]{:S(2)}) collective-permute-start(bf16[512,256]{1,0:T(8,128)(2,1)} %copy-done.55), channel_id=1, source_target_pairs={{0,24},{1,25},{2,26},{3,27},{4,28},{5,29},{6,30},{7,31},{8,16},{9,... | collective-permute-start | bytes 786440 | tf_op jit(solution)/shard_map/ppermute | solution.py:96
  230.4 10.2 %collective-permute-start.42 = (bf16[128,1152]{1,0:T(8,128)(2,1)S(1)}, bf16[128,1152]{1,0:T(8,128)(2,1)S(1)}, u32[]{:S(2)}, u32[]{:S(2)}) collective-permute-start(bf16[128,1152]{1,0:T(8,128)(2,1)S(1)} %get-tuple-element.90), channel_id=1, source_target_pairs={{0,3},{1,2},{2,1},{3,0},{4,7},{5,6},{6,5},{7,4},{8,11},{9,10},{10,... | collective-permute-start | bytes 884744 | tf_op jit(solution)/shard_map/ppermute | solution.py:96
  232.7 26.3 %collective-permute-start.41 = (bf16[128,1152]{1,0:T(8,128)(2,1)S(1)}, bf16[128,1152]{1,0:T(8,128)(2,1)S(1)}, u32[]{:S(2)}, u32[]{:S(2)}) collective-permute-start(bf16[128,1152]{1,0:T(8,128)(2,1)S(1)} %get-tuple-element.90), channel_id=1, source_target_pairs={{0,2},{1,3},{2,0},{3,1},{4,6},{5,7},{6,4},{7,5},{8,10},{9,11},{10,... | collective-permute-start | bytes 884744 | tf_op jit(solution)/shard_map/ppermute | solution.py:96
  237.9 21.1 %collective-permute-start.40 = (bf16[128,1152]{1,0:T(8,128)(2,1)S(1)}, bf16[128,1152]{1,0:T(8,128)(2,1)S(1)}, u32[]{:S(2)}, u32[]{:S(2)}) collective-permute-start(bf16[128,1152]{1,0:T(8,128)(2,1)S(1)} %get-tuple-element.90), channel_id=1, source_target_pairs={{0,1},{1,0},{2,3},{3,2},{4,5},{5,4},{6,7},{7,6},{8,9},{9,8},{10,11... | collective-permute-start | bytes 884744 | tf_op jit(solution)/shard_map/ppermute | solution.py:96
  264.2 147.2 %reduce-scatter.6.cloned.1.call-start = ((), (), s32[]{:S(2)}) async-start(), calls=%async_computation.7 | async-start | bytes 4644864 | tf_op jit(solution)/shard_map/reduce_scatter | solution.py:569
  282.9 180.4 %reduce-scatter.8.cloned.1.call-start = ((), (), s32[]{:S(2)}) async-start(), calls=%async_computation.8 | async-start | bytes 4644864 | tf_op jit(solution)/shard_map/reduce_scatter | solution.py:576
  290.4 21.5 %collective-permute-start.45 = (bf16[128,1152]{1,0:T(8,128)(2,1)}, bf16[128,1152]{1,0:T(8,128)(2,1)S(1)}, u32[]{:S(2)}, u32[]{:S(2)}) collective-permute-start(bf16[128,1152]{1,0:T(8,128)(2,1)} %get-tuple-element.93), channel_id=1, source_target_pairs={{0,2},{1,3},{2,0},{3,1},{4,6},{5,7},{6,4},{7,5},{8,10},{9,11},{10,... | collective-permute-start | bytes 884744 | tf_op jit(solution)/shard_map/ppermute | solution.py:96
  290.4 21.5 %collective-permute-start.44 = (bf16[128,1152]{1,0:T(8,128)(2,1)}, bf16[128,1152]{1,0:T(8,128)(2,1)}, u32[]{:S(2)}, u32[]{:S(2)}) collective-permute-start(bf16[128,1152]{1,0:T(8,128)(2,1)} %get-tuple-element.92), channel_id=1, source_target_pairs={{0,3},{1,2},{2,1},{3,0},{4,7},{5,6},{6,5},{7,4},{8,11},{9,10},{10,... | collective-permute-start | bytes 884744 | tf_op jit(solution)/shard_map/ppermute | solution.py:96
  295.8 21.4 %collective-permute-start.43 = (bf16[128,1152]{1,0:T(8,128)(2,1)S(1)}, bf16[128,1152]{1,0:T(8,128)(2,1)}, u32[]{:S(2)}, u32[]{:S(2)}) collective-permute-start(bf16[128,1152]{1,0:T(8,128)(2,1)S(1)} %slice.482), channel_id=1, source_target_pairs={{0,1},{1,0},{2,3},{3,2},{4,5},{5,4},{6,7},{7,6},{8,9},{9,8},{10,11... | collective-permute-start | bytes 884744 | tf_op jit(solution)/shard_map/ppermute | solution.py:96
  320.7 9.0 %collective-permute-start.46 = (bf16[128,1152]{1,0:T(8,128)(2,1)S(1)}, bf16[128,1152]{1,0:T(8,128)(2,1)}, u32[]{:S(2)}, u32[]{:S(2)}) collective-permute-start(bf16[128,1152]{1,0:T(8,128)(2,1)S(1)} %subtract_convert_fusion), channel_id=1, source_target_pairs={{0,1},{1,0},{2,3},{3,2},{4,5},{5,4},{6,7},{7,6},{8,9},{9,8},{10,11... | collective-permute-start | bytes 884744 | tf_op jit(solution)/shard_map/ppermute | solution.py:96
  324.1 14.1 %collective-permute-start.47 = (bf16[128,1152]{1,0:T(8,128)(2,1)S(1)}, bf16[128,1152]{1,0:T(8,128)(2,1)}, u32[]{:S(2)}, u32[]{:S(2)}) collective-permute-start(bf16[128,1152]{1,0:T(8,128)(2,1)S(1)} %subtract_convert_fusion), channel_id=1, source_target_pairs={{0,4},{1,5},{2,6},{3,7},{4,0},{5,1},{6,2},{7,3},{8,12},{9,13},{10,... | collective-permute-start | bytes 884744 | tf_op jit(solution)/shard_map/ppermute | solution.py:96
  329.6 8.6 %collective-permute-start.48 = (bf16[128,1152]{1,0:T(8,128)(2,1)}, bf16[128,1152]{1,0:T(8,128)(2,1)}, u32[]{:S(2)}, u32[]{:S(2)}) collective-permute-start(bf16[128,1152]{1,0:T(8,128)(2,1)} %collective-permute-done.46), channel_id=1, source_target_pairs={{0,4},{1,5},{2,6},{3,7},{4,0},{5,1},{6,2},{7,3},{8,12},{9,13},{10,... | collective-permute-start | bytes 884744 | tf_op jit(solution)/shard_map/ppermute | solution.py:96
  342.2 27.1 %collective-permute-start.51 = (bf16[528,256]{1,0:T(8,128)(2,1)S(1)}, bf16[528,256]{1,0:T(8,128)(2,1)}, u32[]{:S(2)}, u32[]{:S(2)}) collective-permute-start(bf16[528,256]{1,0:T(8,128)(2,1)S(1)} %concatenate.112.refs_8_), channel_id=1, source_target_pairs={{0,8},{1,9},{2,10},{3,11},{4,12},{5,13},{6,14},{7,15},{8,0},{9,1},... | collective-permute-start | bytes 811016 | tf_op jit(solution)/shard_map/ppermute | solution.py:96
  343.2 27.1 %collective-permute-start.52 = (bf16[528,256]{1,0:T(8,128)(2,1)S(1)}, bf16[528,256]{1,0:T(8,128)(2,1)}, u32[]{:S(2)}, u32[]{:S(2)}) collective-permute-start(bf16[528,256]{1,0:T(8,128)(2,1)S(1)} %concatenate.112.refs_8_), channel_id=1, source_target_pairs={{0,16},{1,17},{2,18},{3,19},{4,20},{5,21},{6,22},{7,23},{8,24},{9,... | collective-permute-start | bytes 811016 | tf_op jit(solution)/shard_map/ppermute | solution.py:96
  344.3 31.8 %collective-permute-start.53 = (bf16[528,256]{1,0:T(8,128)(2,1)S(1)}, bf16[528,256]{1,0:T(8,128)(2,1)}, u32[]{:S(2)}, u32[]{:S(2)}) collective-permute-start(bf16[528,256]{1,0:T(8,128)(2,1)S(1)} %concatenate.112.refs_8_), channel_id=1, source_target_pairs={{0,24},{1,25},{2,26},{3,27},{4,28},{5,29},{6,30},{7,31},{8,16},{9,... | collective-permute-start | bytes 811016 | tf_op jit(solution)/shard_map/ppermute | solution.py:96
  345.8 23.4 %collective-permute-start.54 = (bf16[528,256]{1,0:T(8,128)(2,1)S(1)}, bf16[528,256]{1,0:T(8,128)(2,1)}, u32[]{:S(2)}, u32[]{:S(2)}) collective-permute-start(bf16[528,256]{1,0:T(8,128)(2,1)S(1)} %concatenate.112.refs_8_), channel_id=1, source_target_pairs={{0,2},{1,3},{2,0},{3,1},{4,6},{5,7},{6,4},{7,5},{8,10},{9,11},{10,... | collective-permute-start | bytes 811016 | tf_op jit(solution)/shard_map/ppermute | solution.py:96
  367.1 41.6 %collective-permute-start.49 = (bf16[256,1152]{1,0:T(8,128)(2,1)}, bf16[256,1152]{1,0:T(8,128)(2,1)}, u32[]{:S(2)}, u32[]{:S(2)}) collective-permute-start(bf16[256,1152]{1,0:T(8,128)(2,1)} %slice.480), channel_id=1, source_target_pairs={{0,4},{1,5},{2,6},{3,7},{4,0},{5,1},{6,2},{7,3},{8,12},{9,13},{10,... | collective-permute-start | bytes 1769480 | tf_op jit(solution)/shard_map/ppermute | solution.py:96
  369.2 14.4 %collective-permute-start.55 = (bf16[528,256]{1,0:T(8,128)(2,1)}, bf16[528,256]{1,0:T(8,128)(2,1)S(1)}, u32[]{:S(2)}, u32[]{:S(2)}) collective-permute-start(bf16[528,256]{1,0:T(8,128)(2,1)} %collective-permute-done.54.refs_12_), channel_id=1, source_target_pairs={{0,8},{1,9},{2,10},{3,11},{4,12},{5,13},{6,14},{7,15},{8,0},{9,1},... | collective-permute-start | bytes 811016 | tf_op jit(solution)/shard_map/ppermute | solution.py:96
  369.4 20.1 %collective-permute-start.56 = (bf16[528,256]{1,0:T(8,128)(2,1)}, bf16[528,256]{1,0:T(8,128)(2,1)}, u32[]{:S(2)}, u32[]{:S(2)}) collective-permute-start(bf16[528,256]{1,0:T(8,128)(2,1)} %collective-permute-done.54.refs_12_), channel_id=1, source_target_pairs={{0,16},{1,17},{2,18},{3,19},{4,20},{5,21},{6,22},{7,23},{8,24},{9,... | collective-permute-start | bytes 811016 | tf_op jit(solution)/shard_map/ppermute | solution.py:96
  370.2 19.2 %collective-permute-start.57 = (bf16[528,256]{1,0:T(8,128)(2,1)}, bf16[528,256]{1,0:T(8,128)(2,1)}, u32[]{:S(2)}, u32[]{:S(2)}) collective-permute-start(bf16[528,256]{1,0:T(8,128)(2,1)} %collective-permute-done.54.refs_12_), channel_id=1, source_target_pairs={{0,24},{1,25},{2,26},{3,27},{4,28},{5,29},{6,30},{7,31},{8,16},{9,... | collective-permute-start | bytes 811016 | tf_op jit(solution)/shard_map/ppermute | solution.py:96
  404.2 9.2 %collective-permute-start.58 = (bf16[256,512]{1,0:T(8,128)(2,1)S(1)}, bf16[256,512]{1,0:T(8,128)(2,1)S(1)}, u32[]{:S(2)}, u32[]{:S(2)}) collective-permute-start(bf16[256,512]{1,0:T(8,128)(2,1)S(1)} %slice.485), channel_id=1, source_target_pairs={{0,4},{1,5},{2,6},{3,7},{4,0},{5,1},{6,2},{7,3},{8,12},{9,13},{10,... | collective-permute-start | bytes 786440 | tf_op jit(solution)/shard_map/ppermute | solution.py:96
  405.2 11.1 %collective-permute-start.62 = (bf16[576,256]{1,0:T(8,128)(2,1)}, bf16[576,256]{1,0:T(8,128)(2,1)}, u32[]{:S(2)}, u32[]{:S(2)}) collective-permute-start(bf16[576,256]{1,0:T(8,128)(2,1)} %get-tuple-element.88), channel_id=1, source_target_pairs={{0,24},{1,25},{2,26},{3,27},{4,28},{5,29},{6,30},{7,31},{8,16},{9,... | collective-permute-start | bytes 884744 | tf_op jit(solution)/shard_map/ppermute | solution.py:96
  406.7 20.7 %collective-permute-start.61 = (bf16[576,256]{1,0:T(8,128)(2,1)S(1)}, bf16[576,256]{1,0:T(8,128)(2,1)}, u32[]{:S(2)}, u32[]{:S(2)}) collective-permute-start(bf16[576,256]{1,0:T(8,128)(2,1)S(1)} %get-tuple-element.89), channel_id=1, source_target_pairs={{0,16},{1,17},{2,18},{3,19},{4,20},{5,21},{6,22},{7,23},{8,24},{9,... | collective-permute-start | bytes 884744 | tf_op jit(solution)/shard_map/ppermute | solution.py:96
  408.1 19.7 %collective-permute-start.60 = (bf16[576,256]{1,0:T(8,128)(2,1)S(1)}, bf16[576,256]{1,0:T(8,128)(2,1)}, u32[]{:S(2)}, u32[]{:S(2)}) collective-permute-start(bf16[576,256]{1,0:T(8,128)(2,1)S(1)} %get-tuple-element.87), channel_id=1, source_target_pairs={{0,8},{1,9},{2,10},{3,11},{4,12},{5,13},{6,14},{7,15},{8,0},{9,1},... | collective-permute-start | bytes 884744 | tf_op jit(solution)/shard_map/ppermute | solution.py:96
  410.7 27.6 %collective-permute-start.50 = (bf16[128,1152]{1,0:T(8,128)(2,1)}, bf16[128,1152]{1,0:T(8,128)(2,1)}, u32[]{:S(2)}, u32[]{:S(2)}) collective-permute-start(bf16[128,1152]{1,0:T(8,128)(2,1)} %slice.481), channel_id=1, source_target_pairs={{0,1},{1,0},{2,3},{3,2},{4,5},{5,4},{6,7},{7,6},{8,9},{9,8},{10,11... | collective-permute-start | bytes 884744 | tf_op jit(solution)/shard_map/ppermute | solution.py:96
  414.6 16.9 %collective-permute-start.59 = (bf16[128,512]{1,0:T(8,128)(2,1)S(1)}, bf16[128,512]{1,0:T(8,128)(2,1)S(1)}, u32[]{:S(2)}, u32[]{:S(2)}) collective-permute-start(bf16[128,512]{1,0:T(8,128)(2,1)S(1)} %slice.486), channel_id=1, source_target_pairs={{0,1},{1,0},{2,3},{3,2},{4,5},{5,4},{6,7},{7,6},{8,9},{9,8},{10,11... | collective-permute-start | bytes 393224 | tf_op jit(solution)/shard_map/ppermute | solution.py:96
  430.0 22.7 %collective-permute-start.66 = (bf16[288,256]{1,0:T(8,128)(2,1)}, bf16[288,256]{1,0:T(8,128)(2,1)}, u32[]{:S(2)}, u32[]{:S(2)}) collective-permute-start(bf16[288,256]{1,0:T(8,128)(2,1)} %get-tuple-element.110), channel_id=1, source_target_pairs={{0,4},{1,5},{2,0},{3,1},{4,6},{5,7},{6,2},{7,3},{8,12},{9,13},{10,... | collective-permute-start | bytes 442376 | tf_op jit(solution)/shard_map/ppermute | solution.py:101
  430.0 22.7 %collective-permute-start.67 = (bf16[288,256]{1,0:T(8,128)(2,1)}, bf16[288,256]{1,0:T(8,128)(2,1)}, u32[]{:S(2)}, u32[]{:S(2)}) collective-permute-start(bf16[288,256]{1,0:T(8,128)(2,1)} %get-tuple-element.109), channel_id=1, source_target_pairs={{2,4},{3,5},{4,2},{5,3},{10,12},{11,13},{12,10},{13,11},{18,20},{1... | collective-permute-start | bytes 442376 | tf_op jit(solution)/shard_map/ppermute | solution.py:101
  434.4 11.0 %collective-permute-start.63 = (bf16[128,512]{1,0:T(8,128)(2,1)S(1)}, bf16[128,512]{1,0:T(8,128)(2,1)S(1)}, u32[]{:S(2)}, u32[]{:S(2)}) collective-permute-start(bf16[128,512]{1,0:T(8,128)(2,1)S(1)} %pad_maximum_fusion.16), channel_id=1, source_target_pairs={{0,1},{1,0},{2,3},{3,2},{4,5},{5,4},{6,7},{7,6},{8,9},{9,8},{10,11... | collective-permute-start | bytes 393224 | tf_op jit(solution)/shard_map/ppermute | solution.py:96
  434.5 11.0 %collective-permute-start.64 = (bf16[128,512]{1,0:T(8,128)(2,1)S(1)}, bf16[128,512]{1,0:T(8,128)(2,1)}, u32[]{:S(2)}, u32[]{:S(2)}) collective-permute-start(bf16[128,512]{1,0:T(8,128)(2,1)S(1)} %pad_maximum_fusion.16), channel_id=1, source_target_pairs={{0,4},{1,5},{2,6},{3,7},{4,0},{5,1},{6,2},{7,3},{8,12},{9,13},{10,... | collective-permute-start | bytes 393224 | tf_op jit(solution)/shard_map/ppermute | solution.py:96
  (122 other events, 1147.8 us)
Sparse Core Ops, SparseCore 0:
  28.3 44.9 all-gather.3
  104.1 33.3 all-gather.5
  139.5 36.4 all-gather.7
  264.3 49.8 reduce-scatter.3
  317.5 67.7 reduce-scatter.5
  388.6 58.4 reduce-scatter.7

commit v3 on v2

--- a/solution.py
+++ b/solution.py
@@ -194,11 +194,11 @@
 def column_scatter(product, *rows):
     middle = rows[0].shape[0] // 2
     length = middle // 2
-    far = product(*[r[middle:] for r in rows]).astype(BF)
-    far = [flip(far[length:], 3), flip(far[:length], 2)]
+    sent = product(*[r[middle:] for r in rows]).astype(BF)
+    far = [flip(sent[length:], 3), flip(sent[:length], 2)]
     near = product(*[r[:middle] for r in rows])
     near = near[:length] + flip(near[length:].astype(BF), 1).astype(F32)
-    return near + far[0].astype(F32) + far[1].astype(F32)
+    return near + far[0].astype(F32) + far[1].astype(F32), sent
 
 
 def exchange_first(value):
@@ -546,33 +546,33 @@
     up_proj = dot(gathered_mid, up_full)
     gate_act, gate_deriv = gelu_pair(gate_pre)
     hidden = after((gate_act * up_proj).astype(BF), part_query[blocks])
-    ffn_out = column_scatter(lambda rows: dot(rows, down_full), hidden)
-    ffn_out = after(ffn_out, *part_query)
+    ffn_out, _ = column_scatter(lambda rows: dot(rows, down_full), hidden)
+    ffn_out = after(ffn_out, *part_query[: blocks + 1])
     inv_ffn = rms_inverse(ffn_out)
     block_out = resid_mid + ffn_out * inv_ffn * scale_post_ffn
     grad_ffn, grad_post_ffn = rms_backward(ffn_out, inv_ffn, scale_post_ffn, out_grad)
-    grad_ffn_all = column_gather(grad_ffn.astype(BF))
+    grad_ffn_all = after(column_gather(grad_ffn.astype(BF)), *part_query)
     grad_w_down = column_major(contract_first(hidden, grad_ffn_all).astype(BF))
     grad_ffn_all = after(grad_ffn_all, grad_w_down)
     owned_down = lax.psum_scatter(grad_w_down, "dp", scatter_dimension=1, tiled=True)
     grad_hidden = contract_last(grad_ffn_all, down_full)
     grad_gate = (grad_hidden * up_proj * gate_deriv).astype(BF)
     grad_up = (grad_hidden * gate_act).astype(BF)
-    grad_mid = column_scatter(
+    grad_mid, grad_mid_sent = column_scatter(
         lambda gate, up: contract_last(gate, gate_full) + contract_last(up, up_full),
         grad_gate,
         grad_up,
     )
-    grad_w_gate = row_major(contract_first(gathered_mid, grad_gate).astype(BF))
-    grad_w_up = row_major(contract_first(gathered_mid, grad_up).astype(BF))
-    grad_mid = after(grad_mid, grad_w_gate)
+    mid_later = after(gathered_mid, grad_mid_sent)
+    grad_w_gate = row_major(contract_first(mid_later, grad_gate).astype(BF))
+    grad_w_up = row_major(contract_first(mid_later, grad_up).astype(BF))
+    grad_mid = after(grad_mid, grad_w_gate, grad_w_up)
     owned_gate = lax.psum_scatter(grad_w_gate, "dp", scatter_dimension=0, tiled=True)
     grad_resid, grad_pre_ffn = rms_backward(resid_mid, inv_mid, scale_pre_ffn, grad_mid)
     grad_resid_mid = out_grad + grad_resid
 
     grad_attn, grad_post_attn = rms_backward(attn_out, inv_attn, scale_post_attn, grad_resid_mid)
     grad_attn_all = group_gather(grad_attn.astype(BF))
-    grad_attn_all = after(grad_attn_all, grad_w_up)
     owned_up = lax.psum_scatter(grad_w_up, "dp", scatter_dimension=0, tiled=True)
     grad_mixed = dot(grad_attn_all, out_full).astype(BF)
     delta = jnp.sum(grad_mixed.astype(F32) * mixed.astype(F32), axis=1)
@@ -584,8 +584,6 @@
     owned_down = owned_down.astype(F32)
     part_grad = [after(part_grad[0], owned_down)] + part_grad[1:]
     grad_keyval_part = keyval_grads_of(keyval_group, part_query, part_grad, documents, device)
-    grad_keyval_rows = group_scatter(lambda rows: rows, grad_keyval_part)
-
     grad_query_norm = rope_back(grad_query_rot, cosine, sine_part) * QUERY_SCALE
     grad_queries, grad_gain_query = rms_backward(queries, inv_query, scale_query, grad_query_norm)
     grad_query_bf = grad_queries.astype(BF)
@@ -599,6 +597,9 @@
             axis=2,
         ).reshape(blocks, 4 * weight_rows, HD)
     )
+    grad_keyval_part = after(grad_keyval_part, heads_pair)
+    grad_keyval_rows = group_scatter(lambda rows: rows, grad_keyval_part)
+
     grad_key_norm = rope_back(grad_keyval_rows[:, :HD], cosine[:row_count], sine_part[:row_count])
     grad_key_proj, grad_gain_key = rms_backward(key_proj, inv_key, scale_key, grad_key_norm)
     grad_keyval_bf = jnp.concatenate([grad_key_proj, grad_keyval_rows[:, HD:]], axis=1).astype(BF)

time: 480 us -> 457 us (0.952)
  waiting for transfers between devices: 179 us -> 151 us
  local copies, waits for them, and re-layouts: 29.4 us -> 38.7 us
  starting transfers between devices: 83.4 us -> 77.6 us
    ppermute x70, waiting for transfers between devices: 178 us -> 147 us  [flip(): lax.ppermute(value, AXES, [(s, s ^ mask) for s in range(device_count())])]
    ppermute x70, starting transfers between devices: 78.6 us -> 73.3 us  [flip(): lax.ppermute(value, AXES, [(s, s ^ mask) for s in range(device_count())])]
    unnamed x212 -> x196, local copies, waits for them, and re-layouts: 11.3 us -> 10.7 us
  transfers between devices with their start and end apart: 80 -> 80, of which waited for: 39 -> 37; matrix products, arithmetic and copies ran while one was open for 26% -> 30% of each run, Pallas kernels for 9% -> 10%
where the time goes in v3:
time: 457 us; the launch traced here: 449 us
  waiting for transfers between devices  151 us (33%)
  starting transfers between devices  77.6 us (17%)
  matrix products  67.8 us (15%)
  other arithmetic  53.5 us (12%)
  Pallas kernels  44.4 us (10%)
  local copies, waits for them, and re-layouts  38.7 us (8%)
  between operations  15.8 us (3%)
    ppermute x70, waiting for transfers between devices, flip(): lax.ppermute(value, AXES, [(s, s ^ mask) for s in range(device_count())])  147 us
    ppermute x70, starting transfers between devices, flip(): lax.ppermute(value, AXES, [(s, s ^ mask) for s in range(device_count())])  73.3 us
    dot_general x7, matrix products, dot(): return jnp.dot(left, right, preferred_element_type=F32)  26.6 us
    dot_general x9, matrix products, contract_last(): lax.dot_general(left, right, (((1,), (1,)), ((), ())), preferred_element_...  20.9 us
    dot_general x6, matrix products, contract_first(): lax.dot_general(left, right, (((0,), (0,)), ((), ())), preferred_element_...  20.2 us
    pallas_call x1, Pallas kernels, keyval_grads_of(): pl.pallas_call(body, grid=(rows // length,), out_shape=jax.ShapeDtypeStru...  13.8 us
    pallas_call x1, Pallas kernels, query_grads(): pl.pallas_call(body, grid=(rows // length,), out_shape=jax.ShapeDtypeStru...  12.7 us
    pallas_call x1, Pallas kernels, attend(): pl.pallas_call(body, grid=(rows // length,), out_shape=(jax.ShapeDtypeStr...  11.3 us
  transfers between devices with their start and end apart: 80, of which 37 were waited for; matrix products, arithmetic and copies ran while one was open for 30% of the time, Pallas kernels for 10%

profile of v3, /device:TPU:0, one launch (start us, length us, event | category | flops | bytes accessed | tf_op | source)
XLA Modules:
  0.0 448.5 jit_solution(2653229788884256888)
XLA Ops:
  8.9 5.1 %collective-permute-start.5 = (bf16[40,512]{1,0:T(8,128)(2,1)S(1)}, bf16[40,512]{1,0:T(8,128)(2,1)S(1)}, u32[]{:S(2)}, u32[]{:S(2)}) collective-permute-start(bf16[40,512]{1,0:T(8,128)(2,1)S(1)} %add_convert_fusion), channel_id=1, source_target_pairs={{0,3},{1,2},{2,1},{3,0},{4,7},{5,6},{6,5},{7,4},{8,11},{9,10},{10,... | collective-permute-start | bytes 122888 | tf_op jit(solution)/shard_map/ppermute | solution.py:96
  16.0 2.9 collective-permute-done.4
  19.0 2.5 collective-permute-start.8
  22.5 4.5 %collective-permute-done.8 = bf16[4,40,512]{2,1,0:T(8,128)(2,1)S(1)} collective-permute-done((bf16[4,40,512]{2,1,0:T(8,128)(2,1)S(1)}, bf16[4,40,512]{2,1,0:T(8,128)(2,1)S(1)}, u32[]{:S(2)}, u32[]{:S(2)}) %collective-permute-start.8) | collective-permute-done | bytes 163872 | tf_op jit(solution)/shard_map/ppermute | solution.py:96
  28.2 2.1 collective-permute-start.11
  33.7 2.7 fusion.33
  36.4 6.4 %collective-permute-done = bf16[128,1152]{1,0:T(8,128)(2,1)S(1)} collective-permute-done((bf16[128,1152]{1,0:T(8,128)(2,1)S(1)}, bf16[128,1152]{1,0:T(8,128)(2,1)S(1)}, u32[]{:S(2)}, u32[]{:S(2)}) %collective-permute-start) | collective-permute-done | bytes 294944 | tf_op jit(solution)/shard_map/ppermute | solution.py:96
  48.8 3.2 shard_map.254
  59.6 2.3 collective-permute-start.15
  61.9 5.0 %collective-permute-done.13 = bf16[288,512]{1,0:T(8,128)(2,1)} collective-permute-done((bf16[288,512]{1,0:T(8,128)(2,1)}, bf16[288,512]{1,0:T(8,128)(2,1)}, u32[]{:S(2)}, u32[]{:S(2)}) %collective-permute-start.13) | collective-permute-done | bytes 294944 | tf_op jit(solution)/shard_map/ppermute | solution.py:96
  66.9 4.1 collective-permute-done.12
  70.9 2.4 pad_maximum_fusion.1.item_ref
  73.3 3.5 shard_map.255
  84.2 2.9 fusion.36.query_ref.refs_0_
  87.1 8.3 %collective-permute-done.18.refs_1_ = bf16[512,512]{1,0:T(8,128)(2,1)S(1)} collective-permute-done((bf16[512,512]{1,0:T(8,128)(2,1)S(1)}, bf16[512,512]{1,0:T(8,128)(2,1)S(1)}, u32[]{:S(2)}, u32[]{:S(2)}) %collective-permute-start.18) | collective-permute-done | bytes 524320 | tf_op jit(solution)/shard_map/ppermute | solution.py:96
  95.4 8.7 %collective-permute-done.19.refs_2_ = bf16[512,512]{1,0:T(8,128)(2,1)S(1)} collective-permute-done((bf16[512,512]{1,0:T(8,128)(2,1)S(1)}, bf16[512,512]{1,0:T(8,128)(2,1)S(1)}, u32[]{:S(2)}, u32[]{:S(2)}) %collective-permute-start.19) | collective-permute-done | bytes 524320 | tf_op jit(solution)/shard_map/ppermute | solution.py:96
  110.0 11.3 %shard_map.256 = (bf16[512,256]{1,0:T(8,128)(2,1)}, f32[512,1]{1,0:T(8,128)}) custom-call(s32[1]{0:T(128)} %bitcast.index_ref.device_ref, s32[32,128]{1,0:T(8,128)} %bitcast.122, bf16[512,256]{1,0:T(8,128)(2,1)} %fusion.36.query_ref.refs_0_, bf16[512,512]{1,0:T(8,128)(2,1)} %copy-done.14, bf16[512,512]{1,0:T(8,128)(2,1)} %copy-done.27, ...), custom_call_target="tpu_custom_call" | custom-call | tf_op jit(solution)/shard_map/pallas_call | solution.py:357
  122.8 2.4 collective-permute-done.25
  128.9 6.8 %collective-permute-done.26 = bf16[128,1152]{1,0:T(8,128)(2,1)S(1)} collective-permute-done((bf16[128,1152]{1,0:T(8,128)(2,1)S(1)}, bf16[128,1152]{1,0:T(8,128)(2,1)S(1)}, u32[]{:S(2)}, u32[]{:S(2)}) %collective-permute-start.26) | collective-permute-done | bytes 294944 | tf_op jit(solution)/shard_map/ppermute | solution.py:96
  139.7 2.6 collective-permute-start.27
  142.4 7.5 %collective-permute-done.29 = bf16[128,1152]{1,0:T(8,128)(2,1)S(1)} collective-permute-done((bf16[128,1152]{1,0:T(8,128)(2,1)S(1)}, bf16[128,1152]{1,0:T(8,128)(2,1)S(1)}, u32[]{:S(2)}, u32[]{:S(2)}) %collective-permute-start.29) | collective-permute-done | bytes 294944 | tf_op jit(solution)/shard_map/ppermute | solution.py:96
  149.8 15.5 %collective-permute-done.28 = bf16[128,1152]{1,0:T(8,128)(2,1)S(1)} collective-permute-done((bf16[128,1152]{1,0:T(8,128)(2,1)S(1)}, bf16[128,1152]{1,0:T(8,128)(2,1)S(1)}, u32[]{:S(2)}, u32[]{:S(2)}) %collective-permute-start.28) | collective-permute-done | bytes 294944 | tf_op jit(solution)/shard_map/ppermute | solution.py:96
  167.3 6.9 %fusion.73 = f32[512,1728]{0,1:T(8,128)} fusion(bf16[1152,1728]{1,0:T(8,128)(2,1)} %all-gather.4.cloned.1.call-done, bf16[128,1152]{1,0:T(8,128)(2,1)} %copy-done.49, bf16[128,1152]{1,0:T(8,128)(2,1)} %copy-done.50, bf16[128,1152]{1,0:T(8,128)(2,1)} %copy-done.51, bf16[128,1152]{1,0:T(8,128)(2,1)} %copy-done.33), kind=kOutput, calls=%fused_computation.242 | convolution fusion | flops 2043150336 | bytes 8699904 | tf_op jit(solution)/shard_map/dot_general | solution.py:65
  174.2 9.3 %multiply_convert_fusion.1 = (bf16[512,1728]{0,1:T(8,128)(2,1)}, f32[512,1728]{0,1:T(8,128)}) fusion(f32[512,1728]{0,1:T(8,128)} %fusion.73, bf16[1152,1728]{1,0:T(8,128)(2,1)} %all-gather.6.cloned.1.call-done, bf16[128,1152]{1,0:T(8,128)(2,1)} %copy-done.49, bf16[128,1152]{1,0:T(8,128)(2,1)} %copy-done.50, bf16[128,1152]{1,0:T(8,128)(2,1)} %copy-done.51, ...), kind=kOutput, calls=%fused_computation.13 | convolution fusion | flops 2051997696 | bytes 14008320 | tf_op jit(solution)/shard_map/dot_general | solution.py:65
  183.5 4.0 convolution_convert_fusion.6
  188.4 2.9 collective-permute-start.33
  198.4 13.1 %collective-permute-done.33 = bf16[128,1152]{1,0:T(8,128)(2,1)} collective-permute-done((bf16[128,1152]{1,0:T(8,128)(2,1)}, bf16[128,1152]{1,0:T(8,128)(2,1)}, u32[]{:S(2)}, u32[]{:S(2)}) %collective-permute-start.33) | collective-permute-done | bytes 294944 | tf_op jit(solution)/shard_map/ppermute | solution.py:96
  212.1 2.4 collective-permute-done.31
  216.1 2.9 collective-permute-done.36.refs_3_
  220.9 2.1 collective-permute-start.39
  223.0 2.3 collective-permute-start.37
  227.0 5.6 %collective-permute-done.39 = bf16[128,1152]{1,0:T(8,128)(2,1)S(1)} collective-permute-done((bf16[128,1152]{1,0:T(8,128)(2,1)S(1)}, bf16[128,1152]{1,0:T(8,128)(2,1)S(1)}, u32[]{:S(2)}, u32[]{:S(2)}) %collective-permute-start.39) | collective-permute-done | bytes 294944 | tf_op jit(solution)/shard_map/ppermute | solution.py:96
  233.4 13.3 %collective-permute-done.38 = bf16[128,1152]{1,0:T(8,128)(2,1)S(1)} collective-permute-done((bf16[128,1152]{1,0:T(8,128)(2,1)S(1)}, bf16[128,1152]{1,0:T(8,128)(2,1)S(1)}, u32[]{:S(2)}, u32[]{:S(2)}) %collective-permute-start.38) | collective-permute-done | bytes 294944 | tf_op jit(solution)/shard_map/ppermute | solution.py:96
  247.8 4.4 convolution_convert_fusion.2
  252.3 9.9 %multiply_convert_fusion = (bf16[512,1728]{0,1:T(8,128)(2,1)S(1)}, bf16[512,1728]{0,1:T(8,128)(2,1)S(1)}) fusion(f32[512,1728]{0,1:T(8,128)} %fusion.73, f32[512,1728]{0,1:T(8,128)} %get-tuple-element.162, bf16[512,1152]{1,0:T(8,128)(2,1)} %copy-done.36, bf16[1728,1152]{0,1:T(8,128)(2,1)} %all-gather.8.cloned.1.call-done), kind=kOutput, calls=%fused_computation.12 | convolution fusion | flops 2058780672 | bytes 15777792 | tf_op jit(solution)/shard_map/dot_general | solution.py:73
  267.6 2.2 collective-permute-start.45
  269.8 2.3 collective-permute-start.44
  276.8 4.6 %convolution_convert_fusion.1 = bf16[1152,1728]{1,0:T(8,128)(2,1)} fusion(bf16[512,1152]{1,0:T(8,128)(2,1)S(1)} %copy-done.35, bf16[512,1728]{0,1:T(8,128)(2,1)S(1)} %get-tuple-element.90), kind=kOutput, calls=%fused_computation.1 | convolution fusion | flops 2040422400 | bytes 6930432 | tf_op jit(solution)/shard_map/dot_general | solution.py:69
  281.5 6.3 %convolution_convert_fusion = bf16[1152,1728]{1,0:T(8,128)(2,1)} fusion(bf16[512,1152]{1,0:T(8,128)(2,1)} %pad_maximum_fusion.2, bf16[512,1728]{0,1:T(8,128)(2,1)} %copy-done.94), kind=kOutput, calls=%fused_computation | convolution fusion | flops 2040422400 | bytes 6930432 | tf_op jit(solution)/shard_map/dot_general | solution.py:69
  287.8 2.4 collective-permute-done.45
  290.2 4.4 collective-permute-done.43
  298.8 2.2 collective-permute-start.46
  301.0 7.2 %collective-permute-done.46 = bf16[128,1152]{1,0:T(8,128)(2,1)S(1)} collective-permute-done((bf16[128,1152]{1,0:T(8,128)(2,1)}, bf16[128,1152]{1,0:T(8,128)(2,1)S(1)}, u32[]{:S(2)}, u32[]{:S(2)}) %collective-permute-start.46) | collective-permute-done | bytes 294944 | tf_op jit(solution)/shard_map/ppermute | solution.py:96
  314.1 2.1 collective-permute-start.53
  317.2 12.7 %shard_map.257 = f32[512,256]{1,0:T(8,128)} custom-call(s32[1]{0:T(128)} %bitcast.index_ref.device_ref, s32[32,128]{1,0:T(8,128)} %bitcast.123, bf16[512,256]{1,0:T(8,128)(2,1)} %fusion.36.query_ref.refs_0_, bf16[512,256]{1,0:T(8,128)(2,1)} %copy-done.39, bf16[512,256]{1,0:T(8,128)(2,1)} %get-tuple-element.53.mixed_ref, f32[512,1]{1,0:T(8,128)} %get-tuple-element.64.log_ref, ...), custom_call_target="tpu_custom_call" | custom-call | tf_op jit(solution)/shard_map/pallas_call | solution.py:390
  329.9 2.7 fusion.53
  332.8 1.9 multiply_reduce_fusion.12
  342.2 2.1 convert_element_type.254
  344.3 2.7 collective-permute-done.55.refs_13_
  347.0 6.4 %collective-permute-done.57.refs_15_ = bf16[528,256]{1,0:T(8,128)(2,1)} collective-permute-done((bf16[528,256]{1,0:T(8,128)(2,1)}, bf16[528,256]{1,0:T(8,128)(2,1)}, u32[]{:S(2)}, u32[]{:S(2)}) %collective-permute-start.57) | collective-permute-done | bytes 270368 | tf_op jit(solution)/shard_map/ppermute | solution.py:96
  363.3 13.8 %shard_map.258 = f32[512,512]{1,0:T(8,128)} custom-call(s32[1]{0:T(128)} %bitcast.index_ref.device_ref, s32[32,128]{1,0:T(8,128)} %bitcast.124, bf16[512,512]{1,0:T(8,128)(2,1)} %pad_maximum_fusion.10.keyval_ref, bf16[512,256]{1,0:T(8,128)(2,1)} %fusion.36.query_ref.refs_0_, bf16[512,256]{1,0:T(8,128)(2,1)} %copy-done.56, bf16[512,256]{1,0:T(8,128)(2,1)} %copy-done.57, ...), custom_call_target="tpu_custom_call" | custom-call | tf_op jit(solution)/shard_map/pallas_call | solution.py:435
  378.6 1.9 slice.484
  384.3 2.1 convert_element_type.274
  389.5 3.1 collective-permute-done.66
  393.3 2.3 collective-permute-done.62
  398.5 2.2 multiply_reduce_fusion.3
  406.4 4.4 collective-permute-start.68
  412.6 2.1 collective-permute-start.69
  418.7 2.8 convolution_convert_fusion.3
  421.4 2.9 reshape.272
  429.2 2.7 collective-permute-done.72
  433.5 2.0 subtract_add_fusion
  435.5 2.0 collective-permute-done.73
  438.7 2.1 convert_element_type.275
  (461 shorter events, 132.5 us)
Async XLA Ops:
  7.2 160.1 %all-gather.4.cloned.1.call-start = ((), (), s32[]{:S(2)}) async-start(), calls=%async_computation.3 | async-start | bytes 4644864 | tf_op jit(solution)/shard_map/all_gather | solution.py:494
  8.9 7.1 %collective-permute-start.5 = (bf16[40,512]{1,0:T(8,128)(2,1)S(1)}, bf16[40,512]{1,0:T(8,128)(2,1)S(1)}, u32[]{:S(2)}, u32[]{:S(2)}) collective-permute-start(bf16[40,512]{1,0:T(8,128)(2,1)S(1)} %add_convert_fusion), channel_id=1, source_target_pairs={{0,3},{1,2},{2,1},{3,0},{4,7},{5,6},{6,5},{7,4},{8,11},{9,10},{10,... | collective-permute-start | bytes 122888 | tf_op jit(solution)/shard_map/ppermute | solution.py:96
  19.0 8.0 %collective-permute-start.8 = (bf16[4,40,512]{2,1,0:T(8,128)(2,1)S(1)}, bf16[4,40,512]{2,1,0:T(8,128)(2,1)S(1)}, u32[]{:S(2)}, u32[]{:S(2)}) collective-permute-start(bf16[4,40,512]{2,1,0:T(8,128)(2,1)S(1)} %get-tuple-element.118), channel_id=1, source_target_pairs={{0,24},{1,25},{2,26},{3,27},{4,28},{5,29},{6,30},{7,31},{8,16},{9,... | collective-permute-start | bytes 491528 | tf_op jit(solution)/shard_map/ppermute | solution.py:96
  21.5 6.5 %collective-permute-start.7 = (bf16[4,40,512]{2,1,0:T(8,128)(2,1)S(1)}, bf16[4,40,512]{2,1,0:T(8,128)(2,1)S(1)}, u32[]{:S(2)}, u32[]{:S(2)}) collective-permute-start(bf16[4,40,512]{2,1,0:T(8,128)(2,1)S(1)} %get-tuple-element.118), channel_id=1, source_target_pairs={{0,16},{1,17},{2,18},{3,19},{4,20},{5,21},{6,22},{7,23},{8,24},{9,... | collective-permute-start | bytes 491528 | tf_op jit(solution)/shard_map/ppermute | solution.py:96
  22.0 6.0 %collective-permute-start.6 = (bf16[4,40,512]{2,1,0:T(8,128)(2,1)S(1)}, bf16[4,40,512]{2,1,0:T(8,128)(2,1)S(1)}, u32[]{:S(2)}, u32[]{:S(2)}) collective-permute-start(bf16[4,40,512]{2,1,0:T(8,128)(2,1)S(1)} %get-tuple-element.118), channel_id=1, source_target_pairs={{0,8},{1,9},{2,10},{3,11},{4,12},{5,13},{6,14},{7,15},{8,0},{9,1},... | collective-permute-start | bytes 491528 | tf_op jit(solution)/shard_map/ppermute | solution.py:96
  28.2 146.1 %all-gather.6.cloned.1.call-start = ((), (), s32[]{:S(2)}) async-start(), calls=%async_computation.4 | async-start | bytes 4644864 | tf_op jit(solution)/shard_map/all_gather | solution.py:529
  28.2 15.0 %collective-permute-start.11 = (bf16[144,512]{1,0:T(8,128)(2,1)S(1)}, bf16[144,512]{1,0:T(8,128)(2,1)S(1)}, u32[]{:S(2)}, u32[]{:S(2)}) collective-permute-start(bf16[144,512]{1,0:T(8,128)(2,1)S(1)} %pad_maximum_fusion.16), channel_id=1, source_target_pairs={{0,2},{1,3},{2,6},{3,7},{4,0},{5,1},{6,4},{7,5},{8,10},{9,11},{10,... | collective-permute-start | bytes 442376 | tf_op jit(solution)/shard_map/ppermute | solution.py:101
  30.3 12.9 %collective-permute-start.10 = (bf16[144,512]{1,0:T(8,128)(2,1)S(1)}, bf16[144,512]{1,0:T(8,128)(2,1)S(1)}, u32[]{:S(2)}, u32[]{:S(2)}) collective-permute-start(bf16[144,512]{1,0:T(8,128)(2,1)S(1)} %pad_maximum_fusion.16), channel_id=1, source_target_pairs={{2,4},{3,5},{4,2},{5,3},{10,12},{11,13},{12,10},{13,11},{18,20},{1... | collective-permute-start | bytes 442376 | tf_op jit(solution)/shard_map/ppermute | solution.py:101
  31.8 11.0 %collective-permute-start = (bf16[128,1152]{1,0:T(8,128)(2,1)S(1)}, bf16[128,1152]{1,0:T(8,128)(2,1)S(1)}, u32[]{:S(2)}, u32[]{:S(2)}) collective-permute-start(bf16[128,1152]{1,0:T(8,128)(2,1)S(1)} %multiply_convert_fusion.4), channel_id=1, source_target_pairs={{0,1},{1,0},{2,3},{3,2},{4,5},{5,4},{6,7},{7,6},{8,9},{9,8},{10,11... | collective-permute-start | bytes 884744 | tf_op jit(solution)/shard_map/ppermute | solution.py:96
  32.4 14.7 %collective-permute-start.1 = (bf16[128,1152]{1,0:T(8,128)(2,1)S(1)}, bf16[128,1152]{1,0:T(8,128)(2,1)S(1)}, u32[]{:S(2)}, u32[]{:S(2)}) collective-permute-start(bf16[128,1152]{1,0:T(8,128)(2,1)S(1)} %multiply_convert_fusion.4), channel_id=1, source_target_pairs={{0,4},{1,5},{2,6},{3,7},{4,0},{5,1},{6,2},{7,3},{8,12},{9,13},{10,... | collective-permute-start | bytes 884744 | tf_op jit(solution)/shard_map/ppermute | solution.py:96
  33.7 15.2 %collective-permute-start.9 = (bf16[4,4,40,512]{3,2,1,0:T(8,128)(2,1)S(1)}, bf16[4,4,40,512]{3,2,1,0:T(8,128)(2,1)}, u32[]{:S(2)}, u32[]{:S(2)}) collective-permute-start(bf16[4,4,40,512]{3,2,1,0:T(8,128)(2,1)S(1)} %pad_maximum_fusion.6.near_ref), channel_id=1, source_target_pairs={{0,4},{1,5},{2,6},{3,7},{4,0},{5,1},{6,2},{7,3},{8,12},{9,13},{10,... | collective-permute-start | bytes 1966088 | tf_op jit(solution)/shard_map/ppermute | solution.py:96
  44.0 15.6 %collective-permute-start.14 = (bf16[288,512]{1,0:T(8,128)(2,1)}, bf16[288,512]{1,0:T(8,128)(2,1)}, u32[]{:S(2)}, u32[]{:S(2)}) collective-permute-start(bf16[288,512]{1,0:T(8,128)(2,1)} %pad_maximum_fusion.12), channel_id=1, source_target_pairs={{0,24},{1,25},{2,26},{3,27},{4,28},{5,29},{6,30},{7,31},{8,16},{9,... | collective-permute-start | bytes 884744 | tf_op jit(solution)/shard_map/ppermute | solution.py:96
  45.7 21.1 %collective-permute-start.13 = (bf16[288,512]{1,0:T(8,128)(2,1)}, bf16[288,512]{1,0:T(8,128)(2,1)}, u32[]{:S(2)}, u32[]{:S(2)}) collective-permute-start(bf16[288,512]{1,0:T(8,128)(2,1)} %pad_maximum_fusion.12), channel_id=1, source_target_pairs={{0,16},{1,17},{2,18},{3,19},{4,20},{5,21},{6,22},{7,23},{8,24},{9,... | collective-permute-start | bytes 884744 | tf_op jit(solution)/shard_map/ppermute | solution.py:96
  47.0 23.9 %collective-permute-start.12 = (bf16[288,512]{1,0:T(8,128)(2,1)}, bf16[288,512]{1,0:T(8,128)(2,1)}, u32[]{:S(2)}, u32[]{:S(2)}) collective-permute-start(bf16[288,512]{1,0:T(8,128)(2,1)} %pad_maximum_fusion.12), channel_id=1, source_target_pairs={{0,8},{1,9},{2,10},{3,11},{4,12},{5,13},{6,14},{7,15},{8,0},{9,1},... | collective-permute-start | bytes 884744 | tf_op jit(solution)/shard_map/ppermute | solution.py:96
  57.4 21.9 %collective-permute-start.17 = (bf16[128,512]{1,0:T(8,128)(2,1)S(1)}, bf16[128,512]{1,0:T(8,128)(2,1)}, u32[]{:S(2)}, u32[]{:S(2)}) collective-permute-start(bf16[128,512]{1,0:T(8,128)(2,1)S(1)} %pad_maximum_fusion.17), channel_id=1, source_target_pairs={{0,3},{1,2},{2,1},{3,0},{4,7},{5,6},{6,5},{7,4},{8,11},{9,10},{10,... | collective-permute-start | bytes 393224 | tf_op jit(solution)/shard_map/ppermute | solution.py:96
  57.7 21.6 %collective-permute-start.16 = (bf16[128,512]{1,0:T(8,128)(2,1)S(1)}, bf16[128,512]{1,0:T(8,128)(2,1)}, u32[]{:S(2)}, u32[]{:S(2)}) collective-permute-start(bf16[128,512]{1,0:T(8,128)(2,1)S(1)} %pad_maximum_fusion.17), channel_id=1, source_target_pairs={{0,2},{1,3},{2,0},{3,1},{4,6},{5,7},{6,4},{7,5},{8,10},{9,11},{10,... | collective-permute-start | bytes 393224 | tf_op jit(solution)/shard_map/ppermute | solution.py:96
  59.6 19.8 %collective-permute-start.15 = (bf16[128,512]{1,0:T(8,128)(2,1)S(1)}, bf16[128,512]{1,0:T(8,128)(2,1)S(1)}, u32[]{:S(2)}, u32[]{:S(2)}) collective-permute-start(bf16[128,512]{1,0:T(8,128)(2,1)S(1)} %pad_maximum_fusion.17), channel_id=1, source_target_pairs={{0,1},{1,0},{2,3},{3,2},{4,5},{5,4},{6,7},{7,6},{8,9},{9,8},{10,11... | collective-permute-start | bytes 393224 | tf_op jit(solution)/shard_map/ppermute | solution.py:96
  80.4 14.9 %collective-permute-start.18 = (bf16[512,512]{1,0:T(8,128)(2,1)S(1)}, bf16[512,512]{1,0:T(8,128)(2,1)S(1)}, u32[]{:S(2)}, u32[]{:S(2)}) collective-permute-start(bf16[512,512]{1,0:T(8,128)(2,1)S(1)} %pad_maximum_fusion.8.refs_0_), channel_id=1, source_target_pairs={{0,8},{1,9},{2,10},{3,11},{4,12},{5,13},{6,14},{7,15},{8,0},{9,1},... | collective-permute-start | bytes 1572872 | tf_op jit(solution)/shard_map/ppermute | solution.py:96
  81.8 22.3 %collective-permute-start.19 = (bf16[512,512]{1,0:T(8,128)(2,1)S(1)}, bf16[512,512]{1,0:T(8,128)(2,1)S(1)}, u32[]{:S(2)}, u32[]{:S(2)}) collective-permute-start(bf16[512,512]{1,0:T(8,128)(2,1)S(1)} %pad_maximum_fusion.8.refs_0_), channel_id=1, source_target_pairs={{0,16},{1,17},{2,18},{3,19},{4,20},{5,21},{6,22},{7,23},{8,24},{9,... | collective-permute-start | bytes 1572872 | tf_op jit(solution)/shard_map/ppermute | solution.py:96
  82.7 21.4 %collective-permute-start.20 = (bf16[512,512]{1,0:T(8,128)(2,1)S(1)}, bf16[512,512]{1,0:T(8,128)(2,1)S(1)}, u32[]{:S(2)}, u32[]{:S(2)}) collective-permute-start(bf16[512,512]{1,0:T(8,128)(2,1)S(1)} %pad_maximum_fusion.8.refs_0_), channel_id=1, source_target_pairs={{0,24},{1,25},{2,26},{3,27},{4,28},{5,29},{6,30},{7,31},{8,16},{9,... | collective-permute-start | bytes 1572872 | tf_op jit(solution)/shard_map/ppermute | solution.py:96
  104.1 79.4 %all-gather.8.cloned.1.call-start = ((), (), s32[]{:S(2)}) async-start(), calls=%async_computation.5 | async-start | bytes 4644864 | tf_op jit(solution)/shard_map/all_gather | solution.py:530
  104.8 237.3 %reduce-scatter.4.cloned.1.call-start = ((), (), s32[]{:S(2)}) async-start(), calls=%async_computation.6 | async-start | bytes 4644864 | tf_op jit(solution)/shard_map/reduce_scatter | solution.py:557
  126.6 9.2 %collective-permute-start.26 = (bf16[128,1152]{1,0:T(8,128)(2,1)S(1)}, bf16[128,1152]{1,0:T(8,128)(2,1)S(1)}, u32[]{:S(2)}, u32[]{:S(2)}) collective-permute-start(bf16[128,1152]{1,0:T(8,128)(2,1)S(1)} %slice.483), channel_id=1, source_target_pairs={{0,1},{1,0},{2,3},{3,2},{4,5},{5,4},{6,7},{7,6},{8,9},{9,8},{10,11... | collective-permute-start | bytes 884744 | tf_op jit(solution)/shard_map/ppermute | solution.py:96
  137.9 11.9 %collective-permute-start.29 = (bf16[128,1152]{1,0:T(8,128)(2,1)S(1)}, bf16[128,1152]{1,0:T(8,128)(2,1)S(1)}, u32[]{:S(2)}, u32[]{:S(2)}) collective-permute-start(bf16[128,1152]{1,0:T(8,128)(2,1)S(1)} %multiply_convert_fusion.2), channel_id=1, source_target_pairs={{0,3},{1,2},{2,1},{3,0},{4,7},{5,6},{6,5},{7,4},{8,11},{9,10},{10,... | collective-permute-start | bytes 884744 | tf_op jit(solution)/shard_map/ppermute | solution.py:96
  138.0 27.4 %collective-permute-start.28 = (bf16[128,1152]{1,0:T(8,128)(2,1)S(1)}, bf16[128,1152]{1,0:T(8,128)(2,1)S(1)}, u32[]{:S(2)}, u32[]{:S(2)}) collective-permute-start(bf16[128,1152]{1,0:T(8,128)(2,1)S(1)} %multiply_convert_fusion.2), channel_id=1, source_target_pairs={{0,2},{1,3},{2,0},{3,1},{4,6},{5,7},{6,4},{7,5},{8,10},{9,11},{10,... | collective-permute-start | bytes 884744 | tf_op jit(solution)/shard_map/ppermute | solution.py:96
  139.7 25.6 %collective-permute-start.27 = (bf16[128,1152]{1,0:T(8,128)(2,1)S(1)}, bf16[128,1152]{1,0:T(8,128)(2,1)S(1)}, u32[]{:S(2)}, u32[]{:S(2)}) collective-permute-start(bf16[128,1152]{1,0:T(8,128)(2,1)S(1)} %multiply_convert_fusion.2), channel_id=1, source_target_pairs={{0,1},{1,0},{2,3},{3,2},{4,5},{5,4},{6,7},{7,6},{8,9},{9,8},{10,11... | collective-permute-start | bytes 884744 | tf_op jit(solution)/shard_map/ppermute | solution.py:96
  167.2 16.3 %collective-permute-start.30 = (bf16[512,256]{1,0:T(8,128)(2,1)S(1)}, bf16[512,256]{1,0:T(8,128)(2,1)}, u32[]{:S(2)}, u32[]{:S(2)}) collective-permute-start(bf16[512,256]{1,0:T(8,128)(2,1)S(1)} %copy-done.21), channel_id=1, source_target_pairs={{0,2},{1,3},{2,0},{3,1},{4,6},{5,7},{6,4},{7,5},{8,10},{9,11},{10,... | collective-permute-start | bytes 786440 | tf_op jit(solution)/shard_map/ppermute | solution.py:96
  188.4 23.1 %collective-permute-start.33 = (bf16[128,1152]{1,0:T(8,128)(2,1)}, bf16[128,1152]{1,0:T(8,128)(2,1)}, u32[]{:S(2)}, u32[]{:S(2)}) collective-permute-start(bf16[128,1152]{1,0:T(8,128)(2,1)} %get-tuple-element.99), channel_id=1, source_target_pairs={{0,2},{1,3},{2,0},{3,1},{4,6},{5,7},{6,4},{7,5},{8,10},{9,11},{10,... | collective-permute-start | bytes 884744 | tf_op jit(solution)/shard_map/ppermute | solution.py:96
  191.3 20.9 %collective-permute-start.32 = (bf16[128,1152]{1,0:T(8,128)(2,1)}, bf16[128,1152]{1,0:T(8,128)(2,1)}, u32[]{:S(2)}, u32[]{:S(2)}) collective-permute-start(bf16[128,1152]{1,0:T(8,128)(2,1)} %get-tuple-element.98), channel_id=1, source_target_pairs={{0,3},{1,2},{2,1},{3,0},{4,7},{5,6},{6,5},{7,4},{8,11},{9,10},{10,... | collective-permute-start | bytes 884744 | tf_op jit(solution)/shard_map/ppermute | solution.py:96
  195.7 18.8 %collective-permute-start.31 = (bf16[128,1152]{1,0:T(8,128)(2,1)}, bf16[128,1152]{1,0:T(8,128)(2,1)}, u32[]{:S(2)}, u32[]{:S(2)}) collective-permute-start(bf16[128,1152]{1,0:T(8,128)(2,1)} %slice.482), channel_id=1, source_target_pairs={{0,1},{1,0},{2,3},{3,2},{4,5},{5,4},{6,7},{7,6},{8,9},{9,8},{10,11... | collective-permute-start | bytes 884744 | tf_op jit(solution)/shard_map/ppermute | solution.py:96
  197.1 18.9 %collective-permute-start.34 = (bf16[512,256]{1,0:T(8,128)(2,1)}, bf16[512,256]{1,0:T(8,128)(2,1)S(1)}, u32[]{:S(2)}, u32[]{:S(2)}) collective-permute-start(bf16[512,256]{1,0:T(8,128)(2,1)} %fusion.36.query_ref.refs_0_), channel_id=1, source_target_pairs={{0,8},{1,9},{2,10},{3,11},{4,12},{5,13},{6,14},{7,15},{8,0},{9,1},... | collective-permute-start | bytes 786440 | tf_op jit(solution)/shard_map/ppermute | solution.py:96
  198.2 17.9 %collective-permute-start.35 = (bf16[512,256]{1,0:T(8,128)(2,1)}, bf16[512,256]{1,0:T(8,128)(2,1)S(1)}, u32[]{:S(2)}, u32[]{:S(2)}) collective-permute-start(bf16[512,256]{1,0:T(8,128)(2,1)} %fusion.36.query_ref.refs_0_), channel_id=1, source_target_pairs={{0,16},{1,17},{2,18},{3,19},{4,20},{5,21},{6,22},{7,23},{8,24},{9,... | collective-permute-start | bytes 786440 | tf_op jit(solution)/shard_map/ppermute | solution.py:96
  211.5 7.5 %collective-permute-start.36 = (bf16[512,256]{1,0:T(8,128)(2,1)}, bf16[512,256]{1,0:T(8,128)(2,1)S(1)}, u32[]{:S(2)}, u32[]{:S(2)}) collective-permute-start(bf16[512,256]{1,0:T(8,128)(2,1)} %fusion.36.query_ref.refs_0_), channel_id=1, source_target_pairs={{0,24},{1,25},{2,26},{3,27},{4,28},{5,29},{6,30},{7,31},{8,16},{9,... | collective-permute-start | bytes 786440 | tf_op jit(solution)/shard_map/ppermute | solution.py:96
  220.9 11.7 %collective-permute-start.39 = (bf16[128,1152]{1,0:T(8,128)(2,1)S(1)}, bf16[128,1152]{1,0:T(8,128)(2,1)S(1)}, u32[]{:S(2)}, u32[]{:S(2)}) collective-permute-start(bf16[128,1152]{1,0:T(8,128)(2,1)S(1)} %get-tuple-element.94), channel_id=1, source_target_pairs={{0,3},{1,2},{2,1},{3,0},{4,7},{5,6},{6,5},{7,4},{8,11},{9,10},{10,... | collective-permute-start | bytes 884744 | tf_op jit(solution)/shard_map/ppermute | solution.py:96
  223.0 23.7 %collective-permute-start.38 = (bf16[128,1152]{1,0:T(8,128)(2,1)S(1)}, bf16[128,1152]{1,0:T(8,128)(2,1)S(1)}, u32[]{:S(2)}, u32[]{:S(2)}) collective-permute-start(bf16[128,1152]{1,0:T(8,128)(2,1)S(1)} %get-tuple-element.94), channel_id=1, source_target_pairs={{0,2},{1,3},{2,0},{3,1},{4,6},{5,7},{6,4},{7,5},{8,10},{9,11},{10,... | collective-permute-start | bytes 884744 | tf_op jit(solution)/shard_map/ppermute | solution.py:96
  223.0 23.7 %collective-permute-start.37 = (bf16[128,1152]{1,0:T(8,128)(2,1)S(1)}, bf16[128,1152]{1,0:T(8,128)(2,1)S(1)}, u32[]{:S(2)}, u32[]{:S(2)}) collective-permute-start(bf16[128,1152]{1,0:T(8,128)(2,1)S(1)} %get-tuple-element.94), channel_id=1, source_target_pairs={{0,1},{1,0},{2,3},{3,2},{4,5},{5,4},{6,7},{7,6},{8,9},{9,8},{10,11... | collective-permute-start | bytes 884744 | tf_op jit(solution)/shard_map/ppermute | solution.py:96
  225.3 21.4 %collective-permute-start.40 = (bf16[512,256]{1,0:T(8,128)(2,1)}, bf16[512,256]{1,0:T(8,128)(2,1)}, u32[]{:S(2)}, u32[]{:S(2)}) collective-permute-start(bf16[512,256]{1,0:T(8,128)(2,1)} %collective-permute-done.30.refs_4_), channel_id=1, source_target_pairs={{0,8},{1,9},{2,10},{3,11},{4,12},{5,13},{6,14},{7,15},{8,0},{9,1},... | collective-permute-start | bytes 786440 | tf_op jit(solution)/shard_map/ppermute | solution.py:96
  226.8 20.0 %collective-permute-start.41 = (bf16[512,256]{1,0:T(8,128)(2,1)}, bf16[512,256]{1,0:T(8,128)(2,1)}, u32[]{:S(2)}, u32[]{:S(2)}) collective-permute-start(bf16[512,256]{1,0:T(8,128)(2,1)} %collective-permute-done.30.refs_4_), channel_id=1, source_target_pairs={{0,16},{1,17},{2,18},{3,19},{4,20},{5,21},{6,22},{7,23},{8,24},{9,... | collective-permute-start | bytes 786440 | tf_op jit(solution)/shard_map/ppermute | solution.py:96
  232.7 14.1 %collective-permute-start.42 = (bf16[512,256]{1,0:T(8,128)(2,1)}, bf16[512,256]{1,0:T(8,128)(2,1)}, u32[]{:S(2)}, u32[]{:S(2)}) collective-permute-start(bf16[512,256]{1,0:T(8,128)(2,1)} %collective-permute-done.30.refs_4_), channel_id=1, source_target_pairs={{0,24},{1,25},{2,26},{3,27},{4,28},{5,29},{6,30},{7,31},{8,16},{9,... | collective-permute-start | bytes 786440 | tf_op jit(solution)/shard_map/ppermute | solution.py:96
  252.2 132.0 %reduce-scatter.6.cloned.1.call-start = ((), (), s32[]{:S(2)}) async-start(), calls=%async_computation.7 | async-start | bytes 4644864 | tf_op jit(solution)/shard_map/reduce_scatter | solution.py:570
  267.6 22.6 %collective-permute-start.45 = (bf16[128,1152]{1,0:T(8,128)(2,1)}, bf16[128,1152]{1,0:T(8,128)(2,1)}, u32[]{:S(2)}, u32[]{:S(2)}) collective-permute-start(bf16[128,1152]{1,0:T(8,128)(2,1)} %get-tuple-element.97), channel_id=1, source_target_pairs={{0,2},{1,3},{2,0},{3,1},{4,6},{5,7},{6,4},{7,5},{8,10},{9,11},{10,... | collective-permute-start | bytes 884744 | tf_op jit(solution)/shard_map/ppermute | solution.py:96
  269.8 20.4 %collective-permute-start.44 = (bf16[128,1152]{1,0:T(8,128)(2,1)}, bf16[128,1152]{1,0:T(8,128)(2,1)}, u32[]{:S(2)}, u32[]{:S(2)}) collective-permute-start(bf16[128,1152]{1,0:T(8,128)(2,1)} %get-tuple-element.96), channel_id=1, source_target_pairs={{0,3},{1,2},{2,1},{3,0},{4,7},{5,6},{6,5},{7,4},{8,11},{9,10},{10,... | collective-permute-start | bytes 884744 | tf_op jit(solution)/shard_map/ppermute | solution.py:96
  276.7 17.8 %collective-permute-start.43 = (bf16[128,1152]{1,0:T(8,128)(2,1)}, bf16[128,1152]{1,0:T(8,128)(2,1)}, u32[]{:S(2)}, u32[]{:S(2)}) collective-permute-start(bf16[128,1152]{1,0:T(8,128)(2,1)} %slice.481), channel_id=1, source_target_pairs={{0,1},{1,0},{2,3},{3,2},{4,5},{5,4},{6,7},{7,6},{8,9},{9,8},{10,11... | collective-permute-start | bytes 884744 | tf_op jit(solution)/shard_map/ppermute | solution.py:96
  281.4 157.3 %reduce-scatter.8.cloned.1.call-start = ((), (), s32[]{:S(2)}) async-start(), calls=%async_computation.8 | async-start | bytes 4644864 | tf_op jit(solution)/shard_map/reduce_scatter | solution.py:576
  298.8 9.4 %collective-permute-start.46 = (bf16[128,1152]{1,0:T(8,128)(2,1)}, bf16[128,1152]{1,0:T(8,128)(2,1)S(1)}, u32[]{:S(2)}, u32[]{:S(2)}) collective-permute-start(bf16[128,1152]{1,0:T(8,128)(2,1)} %subtract_convert_fusion), channel_id=1, source_target_pairs={{0,1},{1,0},{2,3},{3,2},{4,5},{5,4},{6,7},{7,6},{8,9},{9,8},{10,11... | collective-permute-start | bytes 884744 | tf_op jit(solution)/shard_map/ppermute | solution.py:96
  301.0 8.9 %collective-permute-start.47 = (bf16[128,1152]{1,0:T(8,128)(2,1)}, bf16[128,1152]{1,0:T(8,128)(2,1)S(1)}, u32[]{:S(2)}, u32[]{:S(2)}) collective-permute-start(bf16[128,1152]{1,0:T(8,128)(2,1)} %subtract_convert_fusion), channel_id=1, source_target_pairs={{0,4},{1,5},{2,6},{3,7},{4,0},{5,1},{6,2},{7,3},{8,12},{9,13},{10,... | collective-permute-start | bytes 884744 | tf_op jit(solution)/shard_map/ppermute | solution.py:96
  312.7 24.7 %collective-permute-start.51 = (bf16[528,256]{1,0:T(8,128)(2,1)S(1)}, bf16[528,256]{1,0:T(8,128)(2,1)}, u32[]{:S(2)}, u32[]{:S(2)}) collective-permute-start(bf16[528,256]{1,0:T(8,128)(2,1)S(1)} %concatenate.112.refs_8_), channel_id=1, source_target_pairs={{0,8},{1,9},{2,10},{3,11},{4,12},{5,13},{6,14},{7,15},{8,0},{9,1},... | collective-permute-start | bytes 811016 | tf_op jit(solution)/shard_map/ppermute | solution.py:96
  313.7 30.6 %collective-permute-start.52 = (bf16[528,256]{1,0:T(8,128)(2,1)S(1)}, bf16[528,256]{1,0:T(8,128)(2,1)}, u32[]{:S(2)}, u32[]{:S(2)}) collective-permute-start(bf16[528,256]{1,0:T(8,128)(2,1)S(1)} %concatenate.112.refs_8_), channel_id=1, source_target_pairs={{0,16},{1,17},{2,18},{3,19},{4,20},{5,21},{6,22},{7,23},{8,24},{9,... | collective-permute-start | bytes 811016 | tf_op jit(solution)/shard_map/ppermute | solution.py:96
  314.1 30.2 %collective-permute-start.53 = (bf16[528,256]{1,0:T(8,128)(2,1)S(1)}, bf16[528,256]{1,0:T(8,128)(2,1)}, u32[]{:S(2)}, u32[]{:S(2)}) collective-permute-start(bf16[528,256]{1,0:T(8,128)(2,1)S(1)} %concatenate.112.refs_8_), channel_id=1, source_target_pairs={{0,24},{1,25},{2,26},{3,27},{4,28},{5,29},{6,30},{7,31},{8,16},{9,... | collective-permute-start | bytes 811016 | tf_op jit(solution)/shard_map/ppermute | solution.py:96
  316.2 19.4 %collective-permute-start.54 = (bf16[528,256]{1,0:T(8,128)(2,1)S(1)}, bf16[528,256]{1,0:T(8,128)(2,1)}, u32[]{:S(2)}, u32[]{:S(2)}) collective-permute-start(bf16[528,256]{1,0:T(8,128)(2,1)S(1)} %concatenate.112.refs_8_), channel_id=1, source_target_pairs={{0,2},{1,3},{2,0},{3,1},{4,6},{5,7},{6,4},{7,5},{8,10},{9,11},{10,... | collective-permute-start | bytes 811016 | tf_op jit(solution)/shard_map/ppermute | solution.py:96
  335.6 11.4 %collective-permute-start.55 = (bf16[528,256]{1,0:T(8,128)(2,1)}, bf16[528,256]{1,0:T(8,128)(2,1)S(1)}, u32[]{:S(2)}, u32[]{:S(2)}) collective-permute-start(bf16[528,256]{1,0:T(8,128)(2,1)} %collective-permute-done.54.refs_12_), channel_id=1, source_target_pairs={{0,8},{1,9},{2,10},{3,11},{4,12},{5,13},{6,14},{7,15},{8,0},{9,1},... | collective-permute-start | bytes 811016 | tf_op jit(solution)/shard_map/ppermute | solution.py:96
  337.1 9.9 %collective-permute-start.56 = (bf16[528,256]{1,0:T(8,128)(2,1)}, bf16[528,256]{1,0:T(8,128)(2,1)S(1)}, u32[]{:S(2)}, u32[]{:S(2)}) collective-permute-start(bf16[528,256]{1,0:T(8,128)(2,1)} %collective-permute-done.54.refs_12_), channel_id=1, source_target_pairs={{0,16},{1,17},{2,18},{3,19},{4,20},{5,21},{6,22},{7,23},{8,24},{9,... | collective-permute-start | bytes 811016 | tf_op jit(solution)/shard_map/ppermute | solution.py:96
  337.3 16.1 %collective-permute-start.57 = (bf16[528,256]{1,0:T(8,128)(2,1)}, bf16[528,256]{1,0:T(8,128)(2,1)}, u32[]{:S(2)}, u32[]{:S(2)}) collective-permute-start(bf16[528,256]{1,0:T(8,128)(2,1)} %collective-permute-done.54.refs_12_), channel_id=1, source_target_pairs={{0,24},{1,25},{2,26},{3,27},{4,28},{5,29},{6,30},{7,31},{8,16},{9,... | collective-permute-start | bytes 811016 | tf_op jit(solution)/shard_map/ppermute | solution.py:96
  344.3 36.2 %collective-permute-start.49 = (bf16[256,1152]{1,0:T(8,128)(2,1)}, bf16[256,1152]{1,0:T(8,128)(2,1)}, u32[]{:S(2)}, u32[]{:S(2)}) collective-permute-start(bf16[256,1152]{1,0:T(8,128)(2,1)} %slice.479), channel_id=1, source_target_pairs={{0,4},{1,5},{2,6},{3,7},{4,0},{5,1},{6,2},{7,3},{8,12},{9,13},{10,... | collective-permute-start | bytes 1769480 | tf_op jit(solution)/shard_map/ppermute | solution.py:96
  355.5 21.6 %collective-permute-start.60 = (bf16[576,256]{1,0:T(8,128)(2,1)}, bf16[576,256]{1,0:T(8,128)(2,1)}, u32[]{:S(2)}, u32[]{:S(2)}) collective-permute-start(bf16[576,256]{1,0:T(8,128)(2,1)} %get-tuple-element.92), channel_id=1, source_target_pairs={{0,24},{1,25},{2,26},{3,27},{4,28},{5,29},{6,30},{7,31},{8,16},{9,... | collective-permute-start | bytes 884744 | tf_op jit(solution)/shard_map/ppermute | solution.py:96
  355.9 21.2 %collective-permute-start.59 = (bf16[576,256]{1,0:T(8,128)(2,1)}, bf16[576,256]{1,0:T(8,128)(2,1)}, u32[]{:S(2)}, u32[]{:S(2)}) collective-permute-start(bf16[576,256]{1,0:T(8,128)(2,1)} %get-tuple-element.93), channel_id=1, source_target_pairs={{0,16},{1,17},{2,18},{3,19},{4,20},{5,21},{6,22},{7,23},{8,24},{9,... | collective-permute-start | bytes 884744 | tf_op jit(solution)/shard_map/ppermute | solution.py:96
  357.4 19.7 %collective-permute-start.58 = (bf16[576,256]{1,0:T(8,128)(2,1)S(1)}, bf16[576,256]{1,0:T(8,128)(2,1)}, u32[]{:S(2)}, u32[]{:S(2)}) collective-permute-start(bf16[576,256]{1,0:T(8,128)(2,1)S(1)} %get-tuple-element.91), channel_id=1, source_target_pairs={{0,8},{1,9},{2,10},{3,11},{4,12},{5,13},{6,14},{7,15},{8,0},{9,1},... | collective-permute-start | bytes 884744 | tf_op jit(solution)/shard_map/ppermute | solution.py:96
  380.5 7.2 %collective-permute-start.61 = (bf16[256,512]{1,0:T(8,128)(2,1)}, bf16[256,512]{1,0:T(8,128)(2,1)}, u32[]{:S(2)}, u32[]{:S(2)}) collective-permute-start(bf16[256,512]{1,0:T(8,128)(2,1)} %slice.484), channel_id=1, source_target_pairs={{0,4},{1,5},{2,6},{3,7},{4,0},{5,1},{6,2},{7,3},{8,12},{9,13},{10,... | collective-permute-start | bytes 786440 | tf_op jit(solution)/shard_map/ppermute | solution.py:96
  382.8 15.7 %collective-permute-start.50 = (bf16[128,1152]{1,0:T(8,128)(2,1)S(1)}, bf16[128,1152]{1,0:T(8,128)(2,1)}, u32[]{:S(2)}, u32[]{:S(2)}) collective-permute-start(bf16[128,1152]{1,0:T(8,128)(2,1)S(1)} %slice.480), channel_id=1, source_target_pairs={{0,1},{1,0},{2,3},{3,2},{4,5},{5,4},{6,7},{7,6},{8,9},{9,8},{10,11... | collective-permute-start | bytes 884744 | tf_op jit(solution)/shard_map/ppermute | solution.py:96
  386.4 6.2 %collective-permute-start.66 = (bf16[288,256]{1,0:T(8,128)(2,1)S(1)}, bf16[288,256]{1,0:T(8,128)(2,1)S(1)}, u32[]{:S(2)}, u32[]{:S(2)}) collective-permute-start(bf16[288,256]{1,0:T(8,128)(2,1)S(1)} %get-tuple-element.114), channel_id=1, source_target_pairs={{0,4},{1,5},{2,0},{3,1},{4,6},{5,7},{6,2},{7,3},{8,12},{9,13},{10,... | collective-permute-start | bytes 442376 | tf_op jit(solution)/shard_map/ppermute | solution.py:101
  386.7 5.9 %collective-permute-start.67 = (bf16[288,256]{1,0:T(8,128)(2,1)S(1)}, bf16[288,256]{1,0:T(8,128)(2,1)S(1)}, u32[]{:S(2)}, u32[]{:S(2)}) collective-permute-start(bf16[288,256]{1,0:T(8,128)(2,1)S(1)} %get-tuple-element.113), channel_id=1, source_target_pairs={{2,4},{3,5},{4,2},{5,3},{10,12},{11,13},{12,10},{13,11},{18,20},{1... | collective-permute-start | bytes 442376 | tf_op jit(solution)/shard_map/ppermute | solution.py:101
  388.8 6.8 %collective-permute-start.62 = (bf16[128,512]{1,0:T(8,128)(2,1)S(1)}, bf16[128,512]{1,0:T(8,128)(2,1)S(1)}, u32[]{:S(2)}, u32[]{:S(2)}) collective-permute-start(bf16[128,512]{1,0:T(8,128)(2,1)S(1)} %slice.485), channel_id=1, source_target_pairs={{0,1},{1,0},{2,3},{3,2},{4,5},{5,4},{6,7},{7,6},{8,9},{9,8},{10,11... | collective-permute-start | bytes 393224 | tf_op jit(solution)/shard_map/ppermute | solution.py:96
  425.6 6.3 %collective-permute-start.72 = (bf16[160,256]{1,0:T(8,128)(2,1)S(1)}, bf16[160,256]{1,0:T(8,128)(2,1)S(1)}, u32[]{:S(2)}, u32[]{:S(2)}) collective-permute-start(bf16[160,256]{1,0:T(8,128)(2,1)S(1)} %get-tuple-element.107), channel_id=1, source_target_pairs={{0,24},{1,25},{2,26},{3,27},{4,28},{5,29},{6,30},{7,31},{8,16},{9,... | collective-permute-start | bytes 245768 | tf_op jit(solution)/shard_map/ppermute | solution.py:96
  426.2 6.0 %collective-permute-start.71 = (bf16[160,256]{1,0:T(8,128)(2,1)S(1)}, bf16[160,256]{1,0:T(8,128)(2,1)S(1)}, u32[]{:S(2)}, u32[]{:S(2)}) collective-permute-start(bf16[160,256]{1,0:T(8,128)(2,1)S(1)} %get-tuple-element.108), channel_id=1, source_target_pairs={{0,16},{1,17},{2,18},{3,19},{4,20},{5,21},{6,22},{7,23},{8,24},{9,... | collective-permute-start | bytes 245768 | tf_op jit(solution)/shard_map/ppermute | solution.py:96
  (114 other events, 973.1 us)
Sparse Core Ops, SparseCore 0:
  28.3 44.9 all-gather.3
  104.2 33.3 all-gather.5
  139.5 36.4 all-gather.7
  252.4 49.5 reduce-scatter.3
  305.2 60.4 reduce-scatter.5
  369.0 50.5 reduce-scatter.7

commit v4 on v3

--- a/solution.py
+++ b/solution.py
@@ -490,6 +490,7 @@
     scale_query = gains[:, 4 * big : 4 * big + little].reshape(HD)
     scale_key = gains[:, 4 * big + little :].reshape(HD)
     head_weights = weight_pair(jnp.concatenate([w_query, w_out.T], axis=1), 0)
+    head_weights = after(head_weights, keyval_full)
     head_weights = [head_weights] + [flip(head_weights, mask) for mask in block_masks()[1:]]
     gate_full = lax.all_gather(after(w_gate, near), "dp", axis=0, tiled=True)
 
@@ -503,7 +504,7 @@
     inv_in = rms_inverse(block_in)
     unit_in = block_in * inv_in
     unit_own = unit_in.astype(BF)
-    unit_all = group_gather(unit_own)
+    unit_all = group_gather(after(unit_own, keyval_full))
     keyval = dot((unit_own.astype(F32) * scale_pre_attn).astype(BF), keyval_full)
     cosine, sine_part = rope_tables(own_index)
     key_proj = keyval[:, :HD]

time: 457 us -> 451 us (0.987)
  waiting for transfers between devices: 151 us -> 136 us
  starting transfers between devices: 77.6 us -> 86.9 us
    ppermute x70, waiting for transfers between devices: 147 us -> 132 us  [flip(): lax.ppermute(value, AXES, [(s, s ^ mask) for s in range(device_count())])]
    ppermute x70, starting transfers between devices: 73.3 us -> 82.1 us  [flip(): lax.ppermute(value, AXES, [(s, s ^ mask) for s in range(device_count())])]
    unnamed x196 -> x198, local copies, waits for them, and re-layouts: 10.7 us -> 13.1 us
  transfers between devices with their start and end apart: 80 -> 80, of which waited for: 37 -> 36; matrix products, arithmetic and copies ran while one was open for 30% -> 30% of each run, Pallas kernels for 10% -> 10%
where the time goes in v4:
time: 451 us; the launch traced here: 443 us
  waiting for transfers between devices  136 us (30%)
  starting transfers between devices  86.9 us (19%)
  matrix products  67.1 us (15%)
  other arithmetic  51.5 us (11%)
  Pallas kernels  44.3 us (10%)
  local copies, waits for them, and re-layouts  42 us (9%)
  between operations  15.8 us (4%)
    ppermute x70, waiting for transfers between devices, flip(): lax.ppermute(value, AXES, [(s, s ^ mask) for s in range(device_count())])  132 us
    ppermute x70, starting transfers between devices, flip(): lax.ppermute(value, AXES, [(s, s ^ mask) for s in range(device_count())])  82.1 us
    dot_general x7, matrix products, dot(): return jnp.dot(left, right, preferred_element_type=F32)  26.4 us
    dot_general x9, matrix products, contract_last(): lax.dot_general(left, right, (((1,), (1,)), ((), ())), preferred_element_...  20.6 us
    dot_general x6, matrix products, contract_first(): lax.dot_general(left, right, (((0,), (0,)), ((), ())), preferred_element_...  20.2 us
    pallas_call x1, Pallas kernels, keyval_grads_of(): pl.pallas_call(body, grid=(rows // length,), out_shape=jax.ShapeDtypeStru...  13.7 us
    unnamed x198, local copies, waits for them, and re-layouts  13.1 us
    pallas_call x1, Pallas kernels, query_grads(): pl.pallas_call(body, grid=(rows // length,), out_shape=jax.ShapeDtypeStru...  12.6 us
  transfers between devices with their start and end apart: 80, of which 36 were waited for; matrix products, arithmetic and copies ran while one was open for 30% of the time, Pallas kernels for 10%

profile of v4, /device:TPU:0, one launch (start us, length us, event | category | flops | bytes accessed | tf_op | source)
XLA Modules:
  0.0 443.2 jit_solution(9627077469294028797)
XLA Ops:
  8.9 5.1 %collective-permute-start.2 = (bf16[40,512]{1,0:T(8,128)(2,1)S(1)}, bf16[40,512]{1,0:T(8,128)(2,1)S(1)}, u32[]{:S(2)}, u32[]{:S(2)}) collective-permute-start(bf16[40,512]{1,0:T(8,128)(2,1)S(1)} %add_convert_fusion), channel_id=1, source_target_pairs={{0,3},{1,2},{2,1},{3,0},{4,7},{5,6},{6,5},{7,4},{8,11},{9,10},{10,... | collective-permute-start | bytes 122888 | tf_op jit(solution)/shard_map/ppermute | solution.py:96
  16.1 2.9 collective-permute-done.1
  19.0 2.5 collective-permute-start.5
  22.5 4.5 %collective-permute-done.5 = bf16[4,40,512]{2,1,0:T(8,128)(2,1)S(1)} collective-permute-done((bf16[4,40,512]{2,1,0:T(8,128)(2,1)S(1)}, bf16[4,40,512]{2,1,0:T(8,128)(2,1)S(1)}, u32[]{:S(2)}, u32[]{:S(2)}) %collective-permute-start.5) | collective-permute-done | bytes 163872 | tf_op jit(solution)/shard_map/ppermute | solution.py:96
  29.0 2.0 collective-permute-start.11
  34.0 1.8 fusion.33
  36.0 3.0 shard_map.254
  48.2 1.9 collective-permute-start.14
  51.3 4.4 collective-permute-done.17
  57.3 1.8 collective-permute-done.16
  59.1 5.0 %collective-permute-done.15 = bf16[128,512]{1,0:T(8,128)(2,1)S(1)} collective-permute-done((bf16[128,512]{1,0:T(8,128)(2,1)S(1)}, bf16[128,512]{1,0:T(8,128)(2,1)S(1)}, u32[]{:S(2)}, u32[]{:S(2)}) %collective-permute-start.15) | collective-permute-done | bytes 131104 | tf_op jit(solution)/shard_map/ppermute | solution.py:96
  67.3 3.2 collective-permute-done.13
  70.5 1.9 collective-permute-start.19
  72.4 2.8 collective-permute-done.12
  77.9 3.4 shard_map.255
  86.2 2.9 fusion.36.query_ref.refs_0_
  89.1 8.1 %collective-permute-done.20.refs_3_ = bf16[512,512]{1,0:T(8,128)(2,1)} collective-permute-done((bf16[512,512]{1,0:T(8,128)(2,1)S(1)}, bf16[512,512]{1,0:T(8,128)(2,1)}, u32[]{:S(2)}, u32[]{:S(2)}) %collective-permute-start.20) | collective-permute-done | bytes 524320 | tf_op jit(solution)/shard_map/ppermute | solution.py:96
  103.3 11.5 %shard_map.256 = (bf16[512,256]{1,0:T(8,128)(2,1)}, f32[512,1]{1,0:T(8,128)}) custom-call(s32[1]{0:T(128)} %bitcast.index_ref.device_ref, s32[32,128]{1,0:T(8,128)} %bitcast.126, bf16[512,256]{1,0:T(8,128)(2,1)} %fusion.36.query_ref.refs_0_, bf16[512,512]{1,0:T(8,128)(2,1)} %copy-done.14, bf16[512,512]{1,0:T(8,128)(2,1)} %collective-permute-done.18.refs_1_, ...), custom_call_target="tpu_custom_call" | custom-call | tf_op jit(solution)/shard_map/pallas_call | solution.py:357
  116.3 1.8 collective-permute-done.25
  123.4 5.2 %collective-permute-done.26 = bf16[128,1152]{1,0:T(8,128)(2,1)S(1)} collective-permute-done((bf16[128,1152]{1,0:T(8,128)(2,1)S(1)}, bf16[128,1152]{1,0:T(8,128)(2,1)S(1)}, u32[]{:S(2)}, u32[]{:S(2)}) %collective-permute-start.26) | collective-permute-done | bytes 294944 | tf_op jit(solution)/shard_map/ppermute | solution.py:96
  130.8 2.3 collective-permute-start.29
  135.2 7.5 %collective-permute-done.29 = bf16[128,1152]{1,0:T(8,128)(2,1)S(1)} collective-permute-done((bf16[128,1152]{1,0:T(8,128)(2,1)S(1)}, bf16[128,1152]{1,0:T(8,128)(2,1)S(1)}, u32[]{:S(2)}, u32[]{:S(2)}) %collective-permute-start.29) | collective-permute-done | bytes 294944 | tf_op jit(solution)/shard_map/ppermute | solution.py:96
  142.7 16.5 %collective-permute-done.28 = bf16[128,1152]{1,0:T(8,128)(2,1)S(1)} collective-permute-done((bf16[128,1152]{1,0:T(8,128)(2,1)S(1)}, bf16[128,1152]{1,0:T(8,128)(2,1)S(1)}, u32[]{:S(2)}, u32[]{:S(2)}) %collective-permute-start.28) | collective-permute-done | bytes 294944 | tf_op jit(solution)/shard_map/ppermute | solution.py:96
  161.1 6.9 %fusion.73 = f32[512,1728]{0,1:T(8,128)} fusion(bf16[1152,1728]{1,0:T(8,128)(2,1)} %all-gather.4.cloned.1.call-done, bf16[128,1152]{1,0:T(8,128)(2,1)} %copy-done.47, bf16[128,1152]{1,0:T(8,128)(2,1)} %copy-done.48, bf16[128,1152]{1,0:T(8,128)(2,1)} %copy-done.49, bf16[128,1152]{1,0:T(8,128)(2,1)} %copy-done.30), kind=kOutput, calls=%fused_computation.242 | convolution fusion | flops 2043150336 | bytes 8699904 | tf_op jit(solution)/shard_map/dot_general | solution.py:65
  168.1 9.3 %multiply_convert_fusion.1 = (bf16[512,1728]{0,1:T(8,128)(2,1)}, f32[512,1728]{0,1:T(8,128)}) fusion(f32[512,1728]{0,1:T(8,128)} %fusion.73, bf16[1152,1728]{1,0:T(8,128)(2,1)} %all-gather.6.cloned.1.call-done, bf16[128,1152]{1,0:T(8,128)(2,1)} %copy-done.47, bf16[128,1152]{1,0:T(8,128)(2,1)} %copy-done.48, bf16[128,1152]{1,0:T(8,128)(2,1)} %copy-done.49, ...), kind=kOutput, calls=%fused_computation.13 | convolution fusion | flops 2051997696 | bytes 14008320 | tf_op jit(solution)/shard_map/dot_general | solution.py:65
  177.4 4.0 convolution_convert_fusion.6
  182.2 2.9 collective-permute-start.33
  185.1 2.3 collective-permute-start.32
  194.0 12.1 %collective-permute-done.33 = bf16[128,1152]{1,0:T(8,128)(2,1)} collective-permute-done((bf16[128,1152]{1,0:T(8,128)(2,1)}, bf16[128,1152]{1,0:T(8,128)(2,1)}, u32[]{:S(2)}, u32[]{:S(2)}) %collective-permute-start.33) | collective-permute-done | bytes 294944 | tf_op jit(solution)/shard_map/ppermute | solution.py:96
  209.9 3.6 collective-permute-done.36.refs_3_
  217.3 2.6 collective-permute-start.37
  219.9 1.9 collective-permute-start.40
  222.3 5.0 %collective-permute-done.39 = bf16[128,1152]{1,0:T(8,128)(2,1)S(1)} collective-permute-done((bf16[128,1152]{1,0:T(8,128)(2,1)S(1)}, bf16[128,1152]{1,0:T(8,128)(2,1)S(1)}, u32[]{:S(2)}, u32[]{:S(2)}) %collective-permute-start.39) | collective-permute-done | bytes 294944 | tf_op jit(solution)/shard_map/ppermute | solution.py:96
  228.7 11.4 %collective-permute-done.38 = bf16[128,1152]{1,0:T(8,128)(2,1)S(1)} collective-permute-done((bf16[128,1152]{1,0:T(8,128)(2,1)S(1)}, bf16[128,1152]{1,0:T(8,128)(2,1)S(1)}, u32[]{:S(2)}, u32[]{:S(2)}) %collective-permute-start.38) | collective-permute-done | bytes 294944 | tf_op jit(solution)/shard_map/ppermute | solution.py:96
  241.2 4.4 %convolution_convert_fusion.2 = bf16[1728,1152]{0,1:T(8,128)(2,1)} fusion(bf16[512,1728]{0,1:T(8,128)(2,1)S(1)} %copy-done.97, bf16[512,1152]{1,0:T(8,128)(2,1)S(1)} %pad_maximum_fusion.3), kind=kOutput, calls=%fused_computation.2 | convolution fusion | flops 2040422400 | bytes 6930432 | tf_op jit(solution)/shard_map/dot_general | solution.py:69
  245.7 9.6 %multiply_convert_fusion = (bf16[512,1728]{0,1:T(8,128)(2,1)S(1)}, bf16[512,1728]{0,1:T(8,128)(2,1)S(1)}) fusion(f32[512,1728]{0,1:T(8,128)} %fusion.73, f32[512,1728]{0,1:T(8,128)} %get-tuple-element.166, bf16[512,1152]{1,0:T(8,128)(2,1)} %copy-done.33, bf16[1728,1152]{0,1:T(8,128)(2,1)} %all-gather.8.cloned.1.call-done), kind=kOutput, calls=%fused_computation.12 | convolution fusion | flops 2058780672 | bytes 15777792 | tf_op jit(solution)/shard_map/dot_general | solution.py:73
  260.8 3.4 collective-permute-start.45
  270.2 4.6 %convolution_convert_fusion.1 = bf16[1152,1728]{1,0:T(8,128)(2,1)} fusion(bf16[512,1152]{1,0:T(8,128)(2,1)S(1)} %copy-done.32, bf16[512,1728]{0,1:T(8,128)(2,1)S(1)} %get-tuple-element.94), kind=kOutput, calls=%fused_computation.1 | convolution fusion | flops 2040422400 | bytes 6930432 | tf_op jit(solution)/shard_map/dot_general | solution.py:69
  274.9 6.2 %convolution_convert_fusion = bf16[1152,1728]{1,0:T(8,128)(2,1)} fusion(bf16[512,1152]{1,0:T(8,128)(2,1)} %pad_maximum_fusion.2, bf16[512,1728]{0,1:T(8,128)(2,1)} %copy-done.95), kind=kOutput, calls=%fused_computation | convolution fusion | flops 2040422400 | bytes 6930432 | tf_op jit(solution)/shard_map/dot_general | solution.py:69
  281.1 3.0 collective-permute-done.45
  284.1 4.2 collective-permute-done.43
  292.6 2.0 collective-permute-start.46
  294.5 6.9 %collective-permute-done.46 = bf16[128,1152]{1,0:T(8,128)(2,1)S(1)} collective-permute-done((bf16[128,1152]{1,0:T(8,128)(2,1)}, bf16[128,1152]{1,0:T(8,128)(2,1)S(1)}, u32[]{:S(2)}, u32[]{:S(2)}) %collective-permute-start.46) | collective-permute-done | bytes 294944 | tf_op jit(solution)/shard_map/ppermute | solution.py:96
  307.7 1.8 collective-permute-start.53
  309.5 2.9 collective-permute-start.54
  312.4 12.6 %shard_map.257 = f32[512,256]{1,0:T(8,128)} custom-call(s32[1]{0:T(128)} %bitcast.index_ref.device_ref, s32[32,128]{1,0:T(8,128)} %bitcast.127, bf16[512,256]{1,0:T(8,128)(2,1)} %fusion.36.query_ref.refs_0_, bf16[512,256]{1,0:T(8,128)(2,1)} %copy-done.38, bf16[512,256]{1,0:T(8,128)(2,1)} %get-tuple-element.57.mixed_ref, f32[512,1]{1,0:T(8,128)} %get-tuple-element.68.log_ref, ...), custom_call_target="tpu_custom_call" | custom-call | tf_op jit(solution)/shard_map/pallas_call | solution.py:390
  325.1 2.7 fusion.53
  328.0 2.0 multiply_reduce_fusion.12
  337.4 2.1 convert_element_type.254
  339.5 2.6 collective-permute-done.55.refs_13_
  342.1 6.3 %collective-permute-done.57.refs_15_ = bf16[528,256]{1,0:T(8,128)(2,1)} collective-permute-done((bf16[528,256]{1,0:T(8,128)(2,1)}, bf16[528,256]{1,0:T(8,128)(2,1)}, u32[]{:S(2)}, u32[]{:S(2)}) %collective-permute-start.57) | collective-permute-done | bytes 270368 | tf_op jit(solution)/shard_map/ppermute | solution.py:96
  358.3 13.7 %shard_map.258 = f32[512,512]{1,0:T(8,128)} custom-call(s32[1]{0:T(128)} %bitcast.index_ref.device_ref, s32[32,128]{1,0:T(8,128)} %bitcast.128, bf16[512,512]{1,0:T(8,128)(2,1)} %pad_maximum_fusion.10.keyval_ref, bf16[512,256]{1,0:T(8,128)(2,1)} %fusion.36.query_ref.refs_0_, bf16[512,256]{1,0:T(8,128)(2,1)} %copy-done.55, bf16[512,256]{1,0:T(8,128)(2,1)} %copy-done.56, ...), custom_call_target="tpu_custom_call" | custom-call | tf_op jit(solution)/shard_map/pallas_call | solution.py:435
  379.2 2.1 convert_element_type.274
  384.5 3.1 collective-permute-done.66
  388.3 2.0 collective-permute-done.62
  393.1 2.2 multiply_reduce_fusion.3
  401.0 4.7 %collective-permute-start.68 = (f32[4,2,2,160]{3,2,1,0:T(2,128)S(1)}, f32[4,2,2,160]{3,2,1,0:T(2,128)S(1)}, u32[]{:S(2)}, u32[]{:S(2)}) collective-permute-start(f32[4,2,2,160]{3,2,1,0:T(2,128)S(1)} %dynamic-slice_bitcast_fusion.8), channel_id=1, source_target_pairs={{0,4},{1,5},{2,6},{3,7},{4,0},{5,1},{6,2},{7,3},{8,12},{9,13},{10,... | collective-permute-start | bytes 30728 | tf_op jit(solution)/shard_map/ppermute | solution.py:96
  407.4 2.1 collective-permute-start.69
  413.5 2.8 convolution_convert_fusion.3
  416.3 3.0 reshape.272
  424.1 2.7 collective-permute-done.72
  428.1 2.0 subtract_add_fusion
  430.2 2.0 collective-permute-done.73
  433.4 2.1 convert_element_type.275
  (463 shorter events, 141.5 us)
Async XLA Ops:
  7.2 153.9 %all-gather.4.cloned.1.call-start = ((), (), s32[]{:S(2)}) async-start(), calls=%async_computation.3 | async-start | bytes 4644864 | tf_op jit(solution)/shard_map/all_gather | solution.py:495
  8.9 7.1 %collective-permute-start.2 = (bf16[40,512]{1,0:T(8,128)(2,1)S(1)}, bf16[40,512]{1,0:T(8,128)(2,1)S(1)}, u32[]{:S(2)}, u32[]{:S(2)}) collective-permute-start(bf16[40,512]{1,0:T(8,128)(2,1)S(1)} %add_convert_fusion), channel_id=1, source_target_pairs={{0,3},{1,2},{2,1},{3,0},{4,7},{5,6},{6,5},{7,4},{8,11},{9,10},{10,... | collective-permute-start | bytes 122888 | tf_op jit(solution)/shard_map/ppermute | solution.py:96
  19.0 8.0 %collective-permute-start.5 = (bf16[4,40,512]{2,1,0:T(8,128)(2,1)S(1)}, bf16[4,40,512]{2,1,0:T(8,128)(2,1)S(1)}, u32[]{:S(2)}, u32[]{:S(2)}) collective-permute-start(bf16[4,40,512]{2,1,0:T(8,128)(2,1)S(1)} %get-tuple-element.122), channel_id=1, source_target_pairs={{0,24},{1,25},{2,26},{3,27},{4,28},{5,29},{6,30},{7,31},{8,16},{9,... | collective-permute-start | bytes 491528 | tf_op jit(solution)/shard_map/ppermute | solution.py:96
  21.5 6.5 %collective-permute-start.4 = (bf16[4,40,512]{2,1,0:T(8,128)(2,1)S(1)}, bf16[4,40,512]{2,1,0:T(8,128)(2,1)S(1)}, u32[]{:S(2)}, u32[]{:S(2)}) collective-permute-start(bf16[4,40,512]{2,1,0:T(8,128)(2,1)S(1)} %get-tuple-element.122), channel_id=1, source_target_pairs={{0,16},{1,17},{2,18},{3,19},{4,20},{5,21},{6,22},{7,23},{8,24},{9,... | collective-permute-start | bytes 491528 | tf_op jit(solution)/shard_map/ppermute | solution.py:96
  22.0 6.0 %collective-permute-start.3 = (bf16[4,40,512]{2,1,0:T(8,128)(2,1)S(1)}, bf16[4,40,512]{2,1,0:T(8,128)(2,1)S(1)}, u32[]{:S(2)}, u32[]{:S(2)}) collective-permute-start(bf16[4,40,512]{2,1,0:T(8,128)(2,1)S(1)} %get-tuple-element.122), channel_id=1, source_target_pairs={{0,8},{1,9},{2,10},{3,11},{4,12},{5,13},{6,14},{7,15},{8,0},{9,1},... | collective-permute-start | bytes 491528 | tf_op jit(solution)/shard_map/ppermute | solution.py:96
  28.2 139.9 %all-gather.6.cloned.1.call-start = ((), (), s32[]{:S(2)}) async-start(), calls=%async_computation.4 | async-start | bytes 4644864 | tf_op jit(solution)/shard_map/all_gather | solution.py:530
  29.0 17.0 %collective-permute-start.11 = (bf16[144,512]{1,0:T(8,128)(2,1)}, bf16[144,512]{1,0:T(8,128)(2,1)}, u32[]{:S(2)}, u32[]{:S(2)}) collective-permute-start(bf16[144,512]{1,0:T(8,128)(2,1)} %pad_maximum_fusion.16), channel_id=1, source_target_pairs={{0,2},{1,3},{2,6},{3,7},{4,0},{5,1},{6,4},{7,5},{8,10},{9,11},{10,... | collective-permute-start | bytes 442376 | tf_op jit(solution)/shard_map/ppermute | solution.py:101
  31.0 15.0 %collective-permute-start.10 = (bf16[144,512]{1,0:T(8,128)(2,1)}, bf16[144,512]{1,0:T(8,128)(2,1)}, u32[]{:S(2)}, u32[]{:S(2)}) collective-permute-start(bf16[144,512]{1,0:T(8,128)(2,1)} %pad_maximum_fusion.16), channel_id=1, source_target_pairs={{2,4},{3,5},{4,2},{5,3},{10,12},{11,13},{12,10},{13,11},{18,20},{1... | collective-permute-start | bytes 442376 | tf_op jit(solution)/shard_map/ppermute | solution.py:101
  42.5 21.5 %collective-permute-start.7 = (bf16[128,1152]{1,0:T(8,128)(2,1)S(1)}, bf16[128,1152]{1,0:T(8,128)(2,1)}, u32[]{:S(2)}, u32[]{:S(2)}) collective-permute-start(bf16[128,1152]{1,0:T(8,128)(2,1)S(1)} %multiply_convert_fusion.4), channel_id=1, source_target_pairs={{0,1},{1,0},{2,3},{3,2},{4,5},{5,4},{6,7},{7,6},{8,9},{9,8},{10,11... | collective-permute-start | bytes 884744 | tf_op jit(solution)/shard_map/ppermute | solution.py:96
  44.2 11.5 %collective-permute-start.17 = (bf16[128,512]{1,0:T(8,128)(2,1)S(1)}, bf16[128,512]{1,0:T(8,128)(2,1)S(1)}, u32[]{:S(2)}, u32[]{:S(2)}) collective-permute-start(bf16[128,512]{1,0:T(8,128)(2,1)S(1)} %pad_maximum_fusion.17), channel_id=1, source_target_pairs={{0,3},{1,2},{2,1},{3,0},{4,7},{5,6},{6,5},{7,4},{8,11},{9,10},{10,... | collective-permute-start | bytes 393224 | tf_op jit(solution)/shard_map/ppermute | solution.py:96
  47.0 12.0 %collective-permute-start.16 = (bf16[128,512]{1,0:T(8,128)(2,1)S(1)}, bf16[128,512]{1,0:T(8,128)(2,1)S(1)}, u32[]{:S(2)}, u32[]{:S(2)}) collective-permute-start(bf16[128,512]{1,0:T(8,128)(2,1)S(1)} %pad_maximum_fusion.17), channel_id=1, source_target_pairs={{0,2},{1,3},{2,0},{3,1},{4,6},{5,7},{6,4},{7,5},{8,10},{9,11},{10,... | collective-permute-start | bytes 393224 | tf_op jit(solution)/shard_map/ppermute | solution.py:96
  48.2 17.5 %collective-permute-start.14 = (bf16[288,512]{1,0:T(8,128)(2,1)S(1)}, bf16[288,512]{1,0:T(8,128)(2,1)S(1)}, u32[]{:S(2)}, u32[]{:S(2)}) collective-permute-start(bf16[288,512]{1,0:T(8,128)(2,1)S(1)} %pad_maximum_fusion.12), channel_id=1, source_target_pairs={{0,24},{1,25},{2,26},{3,27},{4,28},{5,29},{6,30},{7,31},{8,16},{9,... | collective-permute-start | bytes 884744 | tf_op jit(solution)/shard_map/ppermute | solution.py:96
  50.1 20.4 %collective-permute-start.13 = (bf16[288,512]{1,0:T(8,128)(2,1)S(1)}, bf16[288,512]{1,0:T(8,128)(2,1)S(1)}, u32[]{:S(2)}, u32[]{:S(2)}) collective-permute-start(bf16[288,512]{1,0:T(8,128)(2,1)S(1)} %pad_maximum_fusion.12), channel_id=1, source_target_pairs={{0,16},{1,17},{2,18},{3,19},{4,20},{5,21},{6,22},{7,23},{8,24},{9,... | collective-permute-start | bytes 884744 | tf_op jit(solution)/shard_map/ppermute | solution.py:96
  55.7 19.5 %collective-permute-start.12 = (bf16[288,512]{1,0:T(8,128)(2,1)S(1)}, bf16[288,512]{1,0:T(8,128)(2,1)S(1)}, u32[]{:S(2)}, u32[]{:S(2)}) collective-permute-start(bf16[288,512]{1,0:T(8,128)(2,1)S(1)} %pad_maximum_fusion.12), channel_id=1, source_target_pairs={{0,8},{1,9},{2,10},{3,11},{4,12},{5,13},{6,14},{7,15},{8,0},{9,1},... | collective-permute-start | bytes 884744 | tf_op jit(solution)/shard_map/ppermute | solution.py:96
  64.1 17.3 %collective-permute-start.8 = (bf16[128,1152]{1,0:T(8,128)(2,1)S(1)}, bf16[128,1152]{1,0:T(8,128)(2,1)}, u32[]{:S(2)}, u32[]{:S(2)}) collective-permute-start(bf16[128,1152]{1,0:T(8,128)(2,1)S(1)} %multiply_convert_fusion.4), channel_id=1, source_target_pairs={{0,4},{1,5},{2,6},{3,7},{4,0},{5,1},{6,2},{7,3},{8,12},{9,13},{10,... | collective-permute-start | bytes 884744 | tf_op jit(solution)/shard_map/ppermute | solution.py:96
  64.1 17.2 %collective-permute-start.9 = (bf16[128,1152]{1,0:T(8,128)(2,1)}, bf16[128,1152]{1,0:T(8,128)(2,1)}, u32[]{:S(2)}, u32[]{:S(2)}) collective-permute-start(bf16[128,1152]{1,0:T(8,128)(2,1)} %collective-permute-done.7), channel_id=1, source_target_pairs={{0,4},{1,5},{2,6},{3,7},{4,0},{5,1},{6,2},{7,3},{8,12},{9,13},{10,... | collective-permute-start | bytes 884744 | tf_op jit(solution)/shard_map/ppermute | solution.py:96
  65.7 23.4 %collective-permute-start.18 = (bf16[512,512]{1,0:T(8,128)(2,1)S(1)}, bf16[512,512]{1,0:T(8,128)(2,1)}, u32[]{:S(2)}, u32[]{:S(2)}) collective-permute-start(bf16[512,512]{1,0:T(8,128)(2,1)S(1)} %pad_maximum_fusion.8.refs_0_), channel_id=1, source_target_pairs={{0,8},{1,9},{2,10},{3,11},{4,12},{5,13},{6,14},{7,15},{8,0},{9,1},... | collective-permute-start | bytes 1572872 | tf_op jit(solution)/shard_map/ppermute | solution.py:96
  70.5 18.6 %collective-permute-start.19 = (bf16[512,512]{1,0:T(8,128)(2,1)S(1)}, bf16[512,512]{1,0:T(8,128)(2,1)}, u32[]{:S(2)}, u32[]{:S(2)}) collective-permute-start(bf16[512,512]{1,0:T(8,128)(2,1)S(1)} %pad_maximum_fusion.8.refs_0_), channel_id=1, source_target_pairs={{0,16},{1,17},{2,18},{3,19},{4,20},{5,21},{6,22},{7,23},{8,24},{9,... | collective-permute-start | bytes 1572872 | tf_op jit(solution)/shard_map/ppermute | solution.py:96
  75.2 22.0 %collective-permute-start.20 = (bf16[512,512]{1,0:T(8,128)(2,1)S(1)}, bf16[512,512]{1,0:T(8,128)(2,1)}, u32[]{:S(2)}, u32[]{:S(2)}) collective-permute-start(bf16[512,512]{1,0:T(8,128)(2,1)S(1)} %pad_maximum_fusion.8.refs_0_), channel_id=1, source_target_pairs={{0,24},{1,25},{2,26},{3,27},{4,28},{5,29},{6,30},{7,31},{8,16},{9,... | collective-permute-start | bytes 1572872 | tf_op jit(solution)/shard_map/ppermute | solution.py:96
  97.2 80.1 %all-gather.8.cloned.1.call-start = ((), (), s32[]{:S(2)}) async-start(), calls=%async_computation.5 | async-start | bytes 4644864 | tf_op jit(solution)/shard_map/all_gather | solution.py:531
  98.0 239.4 %reduce-scatter.4.cloned.1.call-start = ((), (), s32[]{:S(2)}) async-start(), calls=%async_computation.6 | async-start | bytes 4644864 | tf_op jit(solution)/shard_map/reduce_scatter | solution.py:558
  119.5 9.2 %collective-permute-start.26 = (bf16[128,1152]{1,0:T(8,128)(2,1)S(1)}, bf16[128,1152]{1,0:T(8,128)(2,1)S(1)}, u32[]{:S(2)}, u32[]{:S(2)}) collective-permute-start(bf16[128,1152]{1,0:T(8,128)(2,1)S(1)} %slice.483), channel_id=1, source_target_pairs={{0,1},{1,0},{2,3},{3,2},{4,5},{5,4},{6,7},{7,6},{8,9},{9,8},{10,11... | collective-permute-start | bytes 884744 | tf_op jit(solution)/shard_map/ppermute | solution.py:96
  130.8 11.9 %collective-permute-start.29 = (bf16[128,1152]{1,0:T(8,128)(2,1)S(1)}, bf16[128,1152]{1,0:T(8,128)(2,1)S(1)}, u32[]{:S(2)}, u32[]{:S(2)}) collective-permute-start(bf16[128,1152]{1,0:T(8,128)(2,1)S(1)} %multiply_convert_fusion.2), channel_id=1, source_target_pairs={{0,3},{1,2},{2,1},{3,0},{4,7},{5,6},{6,5},{7,4},{8,11},{9,10},{10,... | collective-permute-start | bytes 884744 | tf_op jit(solution)/shard_map/ppermute | solution.py:96
  133.1 26.1 %collective-permute-start.28 = (bf16[128,1152]{1,0:T(8,128)(2,1)S(1)}, bf16[128,1152]{1,0:T(8,128)(2,1)S(1)}, u32[]{:S(2)}, u32[]{:S(2)}) collective-permute-start(bf16[128,1152]{1,0:T(8,128)(2,1)S(1)} %multiply_convert_fusion.2), channel_id=1, source_target_pairs={{0,2},{1,3},{2,0},{3,1},{4,6},{5,7},{6,4},{7,5},{8,10},{9,11},{10,... | collective-permute-start | bytes 884744 | tf_op jit(solution)/shard_map/ppermute | solution.py:96
  133.9 25.3 %collective-permute-start.27 = (bf16[128,1152]{1,0:T(8,128)(2,1)S(1)}, bf16[128,1152]{1,0:T(8,128)(2,1)S(1)}, u32[]{:S(2)}, u32[]{:S(2)}) collective-permute-start(bf16[128,1152]{1,0:T(8,128)(2,1)S(1)} %multiply_convert_fusion.2), channel_id=1, source_target_pairs={{0,1},{1,0},{2,3},{3,2},{4,5},{5,4},{6,7},{7,6},{8,9},{9,8},{10,11... | collective-permute-start | bytes 884744 | tf_op jit(solution)/shard_map/ppermute | solution.py:96
  161.0 16.3 %collective-permute-start.30 = (bf16[512,256]{1,0:T(8,128)(2,1)S(1)}, bf16[512,256]{1,0:T(8,128)(2,1)}, u32[]{:S(2)}, u32[]{:S(2)}) collective-permute-start(bf16[512,256]{1,0:T(8,128)(2,1)S(1)} %copy-done.21), channel_id=1, source_target_pairs={{0,2},{1,3},{2,0},{3,1},{4,6},{5,7},{6,4},{7,5},{8,10},{9,11},{10,... | collective-permute-start | bytes 786440 | tf_op jit(solution)/shard_map/ppermute | solution.py:96
  182.2 23.8 %collective-permute-start.33 = (bf16[128,1152]{1,0:T(8,128)(2,1)}, bf16[128,1152]{1,0:T(8,128)(2,1)}, u32[]{:S(2)}, u32[]{:S(2)}) collective-permute-start(bf16[128,1152]{1,0:T(8,128)(2,1)} %get-tuple-element.103), channel_id=1, source_target_pairs={{0,2},{1,3},{2,0},{3,1},{4,6},{5,7},{6,4},{7,5},{8,10},{9,11},{10,... | collective-permute-start | bytes 884744 | tf_op jit(solution)/shard_map/ppermute | solution.py:96
  185.1 22.3 %collective-permute-start.32 = (bf16[128,1152]{1,0:T(8,128)(2,1)}, bf16[128,1152]{1,0:T(8,128)(2,1)}, u32[]{:S(2)}, u32[]{:S(2)}) collective-permute-start(bf16[128,1152]{1,0:T(8,128)(2,1)} %get-tuple-element.102), channel_id=1, source_target_pairs={{0,3},{1,2},{2,1},{3,0},{4,7},{5,6},{6,5},{7,4},{8,11},{9,10},{10,... | collective-permute-start | bytes 884744 | tf_op jit(solution)/shard_map/ppermute | solution.py:96
  190.7 17.8 %collective-permute-start.31 = (bf16[128,1152]{1,0:T(8,128)(2,1)}, bf16[128,1152]{1,0:T(8,128)(2,1)}, u32[]{:S(2)}, u32[]{:S(2)}) collective-permute-start(bf16[128,1152]{1,0:T(8,128)(2,1)} %slice.482), channel_id=1, source_target_pairs={{0,1},{1,0},{2,3},{3,2},{4,5},{5,4},{6,7},{7,6},{8,9},{9,8},{10,11... | collective-permute-start | bytes 884744 | tf_op jit(solution)/shard_map/ppermute | solution.py:96
  192.1 17.8 %collective-permute-start.34 = (bf16[512,256]{1,0:T(8,128)(2,1)}, bf16[512,256]{1,0:T(8,128)(2,1)S(1)}, u32[]{:S(2)}, u32[]{:S(2)}) collective-permute-start(bf16[512,256]{1,0:T(8,128)(2,1)} %fusion.36.query_ref.refs_0_), channel_id=1, source_target_pairs={{0,8},{1,9},{2,10},{3,11},{4,12},{5,13},{6,14},{7,15},{8,0},{9,1},... | collective-permute-start | bytes 786440 | tf_op jit(solution)/shard_map/ppermute | solution.py:96
  193.6 16.4 %collective-permute-start.35 = (bf16[512,256]{1,0:T(8,128)(2,1)}, bf16[512,256]{1,0:T(8,128)(2,1)S(1)}, u32[]{:S(2)}, u32[]{:S(2)}) collective-permute-start(bf16[512,256]{1,0:T(8,128)(2,1)} %fusion.36.query_ref.refs_0_), channel_id=1, source_target_pairs={{0,16},{1,17},{2,18},{3,19},{4,20},{5,21},{6,22},{7,23},{8,24},{9,... | collective-permute-start | bytes 786440 | tf_op jit(solution)/shard_map/ppermute | solution.py:96
  206.1 7.5 %collective-permute-start.36 = (bf16[512,256]{1,0:T(8,128)(2,1)}, bf16[512,256]{1,0:T(8,128)(2,1)S(1)}, u32[]{:S(2)}, u32[]{:S(2)}) collective-permute-start(bf16[512,256]{1,0:T(8,128)(2,1)} %fusion.36.query_ref.refs_0_), channel_id=1, source_target_pairs={{0,24},{1,25},{2,26},{3,27},{4,28},{5,29},{6,30},{7,31},{8,16},{9,... | collective-permute-start | bytes 786440 | tf_op jit(solution)/shard_map/ppermute | solution.py:96
  215.6 11.7 %collective-permute-start.39 = (bf16[128,1152]{1,0:T(8,128)(2,1)S(1)}, bf16[128,1152]{1,0:T(8,128)(2,1)S(1)}, u32[]{:S(2)}, u32[]{:S(2)}) collective-permute-start(bf16[128,1152]{1,0:T(8,128)(2,1)S(1)} %get-tuple-element.98), channel_id=1, source_target_pairs={{0,3},{1,2},{2,1},{3,0},{4,7},{5,6},{6,5},{7,4},{8,11},{9,10},{10,... | collective-permute-start | bytes 884744 | tf_op jit(solution)/shard_map/ppermute | solution.py:96
  217.3 22.8 %collective-permute-start.38 = (bf16[128,1152]{1,0:T(8,128)(2,1)S(1)}, bf16[128,1152]{1,0:T(8,128)(2,1)S(1)}, u32[]{:S(2)}, u32[]{:S(2)}) collective-permute-start(bf16[128,1152]{1,0:T(8,128)(2,1)S(1)} %get-tuple-element.98), channel_id=1, source_target_pairs={{0,2},{1,3},{2,0},{3,1},{4,6},{5,7},{6,4},{7,5},{8,10},{9,11},{10,... | collective-permute-start | bytes 884744 | tf_op jit(solution)/shard_map/ppermute | solution.py:96
  217.3 22.8 %collective-permute-start.37 = (bf16[128,1152]{1,0:T(8,128)(2,1)S(1)}, bf16[128,1152]{1,0:T(8,128)(2,1)S(1)}, u32[]{:S(2)}, u32[]{:S(2)}) collective-permute-start(bf16[128,1152]{1,0:T(8,128)(2,1)S(1)} %get-tuple-element.98), channel_id=1, source_target_pairs={{0,1},{1,0},{2,3},{3,2},{4,5},{5,4},{6,7},{7,6},{8,9},{9,8},{10,11... | collective-permute-start | bytes 884744 | tf_op jit(solution)/shard_map/ppermute | solution.py:96
  219.9 20.3 %collective-permute-start.40 = (bf16[512,256]{1,0:T(8,128)(2,1)}, bf16[512,256]{1,0:T(8,128)(2,1)}, u32[]{:S(2)}, u32[]{:S(2)}) collective-permute-start(bf16[512,256]{1,0:T(8,128)(2,1)} %collective-permute-done.30.refs_4_), channel_id=1, source_target_pairs={{0,8},{1,9},{2,10},{3,11},{4,12},{5,13},{6,14},{7,15},{8,0},{9,1},... | collective-permute-start | bytes 786440 | tf_op jit(solution)/shard_map/ppermute | solution.py:96
  221.8 18.4 %collective-permute-start.41 = (bf16[512,256]{1,0:T(8,128)(2,1)}, bf16[512,256]{1,0:T(8,128)(2,1)}, u32[]{:S(2)}, u32[]{:S(2)}) collective-permute-start(bf16[512,256]{1,0:T(8,128)(2,1)} %collective-permute-done.30.refs_4_), channel_id=1, source_target_pairs={{0,16},{1,17},{2,18},{3,19},{4,20},{5,21},{6,22},{7,23},{8,24},{9,... | collective-permute-start | bytes 786440 | tf_op jit(solution)/shard_map/ppermute | solution.py:96
  227.3 12.9 %collective-permute-start.42 = (bf16[512,256]{1,0:T(8,128)(2,1)}, bf16[512,256]{1,0:T(8,128)(2,1)}, u32[]{:S(2)}, u32[]{:S(2)}) collective-permute-start(bf16[512,256]{1,0:T(8,128)(2,1)} %collective-permute-done.30.refs_4_), channel_id=1, source_target_pairs={{0,24},{1,25},{2,26},{3,27},{4,28},{5,29},{6,30},{7,31},{8,16},{9,... | collective-permute-start | bytes 786440 | tf_op jit(solution)/shard_map/ppermute | solution.py:96
  245.7 133.5 %reduce-scatter.6.cloned.1.call-start = ((), (), s32[]{:S(2)}) async-start(), calls=%async_computation.7 | async-start | bytes 4644864 | tf_op jit(solution)/shard_map/reduce_scatter | solution.py:571
  260.8 23.3 %collective-permute-start.45 = (bf16[128,1152]{1,0:T(8,128)(2,1)}, bf16[128,1152]{1,0:T(8,128)(2,1)}, u32[]{:S(2)}, u32[]{:S(2)}) collective-permute-start(bf16[128,1152]{1,0:T(8,128)(2,1)} %get-tuple-element.101), channel_id=1, source_target_pairs={{0,2},{1,3},{2,0},{3,1},{4,6},{5,7},{6,4},{7,5},{8,10},{9,11},{10,... | collective-permute-start | bytes 884744 | tf_op jit(solution)/shard_map/ppermute | solution.py:96
  264.2 20.0 %collective-permute-start.44 = (bf16[128,1152]{1,0:T(8,128)(2,1)}, bf16[128,1152]{1,0:T(8,128)(2,1)}, u32[]{:S(2)}, u32[]{:S(2)}) collective-permute-start(bf16[128,1152]{1,0:T(8,128)(2,1)} %get-tuple-element.100), channel_id=1, source_target_pairs={{0,3},{1,2},{2,1},{3,0},{4,7},{5,6},{6,5},{7,4},{8,11},{9,10},{10,... | collective-permute-start | bytes 884744 | tf_op jit(solution)/shard_map/ppermute | solution.py:96
  270.2 18.2 %collective-permute-start.43 = (bf16[128,1152]{1,0:T(8,128)(2,1)}, bf16[128,1152]{1,0:T(8,128)(2,1)}, u32[]{:S(2)}, u32[]{:S(2)}) collective-permute-start(bf16[128,1152]{1,0:T(8,128)(2,1)} %slice.481), channel_id=1, source_target_pairs={{0,1},{1,0},{2,3},{3,2},{4,5},{5,4},{6,7},{7,6},{8,9},{9,8},{10,11... | collective-permute-start | bytes 884744 | tf_op jit(solution)/shard_map/ppermute | solution.py:96
  274.8 158.5 %reduce-scatter.8.cloned.1.call-start = ((), (), s32[]{:S(2)}) async-start(), calls=%async_computation.8 | async-start | bytes 4644864 | tf_op jit(solution)/shard_map/reduce_scatter | solution.py:577
  292.6 8.9 %collective-permute-start.46 = (bf16[128,1152]{1,0:T(8,128)(2,1)}, bf16[128,1152]{1,0:T(8,128)(2,1)S(1)}, u32[]{:S(2)}, u32[]{:S(2)}) collective-permute-start(bf16[128,1152]{1,0:T(8,128)(2,1)} %subtract_convert_fusion), channel_id=1, source_target_pairs={{0,1},{1,0},{2,3},{3,2},{4,5},{5,4},{6,7},{7,6},{8,9},{9,8},{10,11... | collective-permute-start | bytes 884744 | tf_op jit(solution)/shard_map/ppermute | solution.py:96
  294.5 8.7 %collective-permute-start.47 = (bf16[128,1152]{1,0:T(8,128)(2,1)}, bf16[128,1152]{1,0:T(8,128)(2,1)S(1)}, u32[]{:S(2)}, u32[]{:S(2)}) collective-permute-start(bf16[128,1152]{1,0:T(8,128)(2,1)} %subtract_convert_fusion), channel_id=1, source_target_pairs={{0,4},{1,5},{2,6},{3,7},{4,0},{5,1},{6,2},{7,3},{8,12},{9,13},{10,... | collective-permute-start | bytes 884744 | tf_op jit(solution)/shard_map/ppermute | solution.py:96
  306.0 27.5 %collective-permute-start.51 = (bf16[528,256]{1,0:T(8,128)(2,1)S(1)}, bf16[528,256]{1,0:T(8,128)(2,1)}, u32[]{:S(2)}, u32[]{:S(2)}) collective-permute-start(bf16[528,256]{1,0:T(8,128)(2,1)S(1)} %concatenate.112.refs_8_), channel_id=1, source_target_pairs={{0,8},{1,9},{2,10},{3,11},{4,12},{5,13},{6,14},{7,15},{8,0},{9,1},... | collective-permute-start | bytes 811016 | tf_op jit(solution)/shard_map/ppermute | solution.py:96
  307.4 32.0 %collective-permute-start.52 = (bf16[528,256]{1,0:T(8,128)(2,1)S(1)}, bf16[528,256]{1,0:T(8,128)(2,1)}, u32[]{:S(2)}, u32[]{:S(2)}) collective-permute-start(bf16[528,256]{1,0:T(8,128)(2,1)S(1)} %concatenate.112.refs_8_), channel_id=1, source_target_pairs={{0,16},{1,17},{2,18},{3,19},{4,20},{5,21},{6,22},{7,23},{8,24},{9,... | collective-permute-start | bytes 811016 | tf_op jit(solution)/shard_map/ppermute | solution.py:96
  307.7 31.8 %collective-permute-start.53 = (bf16[528,256]{1,0:T(8,128)(2,1)S(1)}, bf16[528,256]{1,0:T(8,128)(2,1)}, u32[]{:S(2)}, u32[]{:S(2)}) collective-permute-start(bf16[528,256]{1,0:T(8,128)(2,1)S(1)} %concatenate.112.refs_8_), channel_id=1, source_target_pairs={{0,24},{1,25},{2,26},{3,27},{4,28},{5,29},{6,30},{7,31},{8,16},{9,... | collective-permute-start | bytes 811016 | tf_op jit(solution)/shard_map/ppermute | solution.py:96
  309.5 21.3 %collective-permute-start.54 = (bf16[528,256]{1,0:T(8,128)(2,1)S(1)}, bf16[528,256]{1,0:T(8,128)(2,1)}, u32[]{:S(2)}, u32[]{:S(2)}) collective-permute-start(bf16[528,256]{1,0:T(8,128)(2,1)S(1)} %concatenate.112.refs_8_), channel_id=1, source_target_pairs={{0,2},{1,3},{2,0},{3,1},{4,6},{5,7},{6,4},{7,5},{8,10},{9,11},{10,... | collective-permute-start | bytes 811016 | tf_op jit(solution)/shard_map/ppermute | solution.py:96
  330.8 11.2 %collective-permute-start.55 = (bf16[528,256]{1,0:T(8,128)(2,1)}, bf16[528,256]{1,0:T(8,128)(2,1)S(1)}, u32[]{:S(2)}, u32[]{:S(2)}) collective-permute-start(bf16[528,256]{1,0:T(8,128)(2,1)} %collective-permute-done.54.refs_12_), channel_id=1, source_target_pairs={{0,8},{1,9},{2,10},{3,11},{4,12},{5,13},{6,14},{7,15},{8,0},{9,1},... | collective-permute-start | bytes 811016 | tf_op jit(solution)/shard_map/ppermute | solution.py:96
  332.4 9.6 %collective-permute-start.56 = (bf16[528,256]{1,0:T(8,128)(2,1)}, bf16[528,256]{1,0:T(8,128)(2,1)S(1)}, u32[]{:S(2)}, u32[]{:S(2)}) collective-permute-start(bf16[528,256]{1,0:T(8,128)(2,1)} %collective-permute-done.54.refs_12_), channel_id=1, source_target_pairs={{0,16},{1,17},{2,18},{3,19},{4,20},{5,21},{6,22},{7,23},{8,24},{9,... | collective-permute-start | bytes 811016 | tf_op jit(solution)/shard_map/ppermute | solution.py:96
  333.5 14.9 %collective-permute-start.57 = (bf16[528,256]{1,0:T(8,128)(2,1)}, bf16[528,256]{1,0:T(8,128)(2,1)}, u32[]{:S(2)}, u32[]{:S(2)}) collective-permute-start(bf16[528,256]{1,0:T(8,128)(2,1)} %collective-permute-done.54.refs_12_), channel_id=1, source_target_pairs={{0,24},{1,25},{2,26},{3,27},{4,28},{5,29},{6,30},{7,31},{8,16},{9,... | collective-permute-start | bytes 811016 | tf_op jit(solution)/shard_map/ppermute | solution.py:96
  339.5 35.8 %collective-permute-start.49 = (bf16[256,1152]{1,0:T(8,128)(2,1)}, bf16[256,1152]{1,0:T(8,128)(2,1)}, u32[]{:S(2)}, u32[]{:S(2)}) collective-permute-start(bf16[256,1152]{1,0:T(8,128)(2,1)} %slice.479), channel_id=1, source_target_pairs={{0,4},{1,5},{2,6},{3,7},{4,0},{5,1},{6,2},{7,3},{8,12},{9,13},{10,... | collective-permute-start | bytes 1769480 | tf_op jit(solution)/shard_map/ppermute | solution.py:96
  350.4 21.6 %collective-permute-start.60 = (bf16[576,256]{1,0:T(8,128)(2,1)}, bf16[576,256]{1,0:T(8,128)(2,1)}, u32[]{:S(2)}, u32[]{:S(2)}) collective-permute-start(bf16[576,256]{1,0:T(8,128)(2,1)} %get-tuple-element.96), channel_id=1, source_target_pairs={{0,24},{1,25},{2,26},{3,27},{4,28},{5,29},{6,30},{7,31},{8,16},{9,... | collective-permute-start | bytes 884744 | tf_op jit(solution)/shard_map/ppermute | solution.py:96
  350.9 21.1 %collective-permute-start.59 = (bf16[576,256]{1,0:T(8,128)(2,1)}, bf16[576,256]{1,0:T(8,128)(2,1)}, u32[]{:S(2)}, u32[]{:S(2)}) collective-permute-start(bf16[576,256]{1,0:T(8,128)(2,1)} %get-tuple-element.97), channel_id=1, source_target_pairs={{0,16},{1,17},{2,18},{3,19},{4,20},{5,21},{6,22},{7,23},{8,24},{9,... | collective-permute-start | bytes 884744 | tf_op jit(solution)/shard_map/ppermute | solution.py:96
  352.4 19.6 %collective-permute-start.58 = (bf16[576,256]{1,0:T(8,128)(2,1)S(1)}, bf16[576,256]{1,0:T(8,128)(2,1)}, u32[]{:S(2)}, u32[]{:S(2)}) collective-permute-start(bf16[576,256]{1,0:T(8,128)(2,1)S(1)} %get-tuple-element.95), channel_id=1, source_target_pairs={{0,8},{1,9},{2,10},{3,11},{4,12},{5,13},{6,14},{7,15},{8,0},{9,1},... | collective-permute-start | bytes 884744 | tf_op jit(solution)/shard_map/ppermute | solution.py:96
  375.3 7.3 %collective-permute-start.61 = (bf16[256,512]{1,0:T(8,128)(2,1)}, bf16[256,512]{1,0:T(8,128)(2,1)}, u32[]{:S(2)}, u32[]{:S(2)}) collective-permute-start(bf16[256,512]{1,0:T(8,128)(2,1)} %slice.484), channel_id=1, source_target_pairs={{0,4},{1,5},{2,6},{3,7},{4,0},{5,1},{6,2},{7,3},{8,12},{9,13},{10,... | collective-permute-start | bytes 786440 | tf_op jit(solution)/shard_map/ppermute | solution.py:96
  377.6 15.5 %collective-permute-start.50 = (bf16[128,1152]{1,0:T(8,128)(2,1)S(1)}, bf16[128,1152]{1,0:T(8,128)(2,1)}, u32[]{:S(2)}, u32[]{:S(2)}) collective-permute-start(bf16[128,1152]{1,0:T(8,128)(2,1)S(1)} %slice.480), channel_id=1, source_target_pairs={{0,1},{1,0},{2,3},{3,2},{4,5},{5,4},{6,7},{7,6},{8,9},{9,8},{10,11... | collective-permute-start | bytes 884744 | tf_op jit(solution)/shard_map/ppermute | solution.py:96
  381.3 6.2 %collective-permute-start.66 = (bf16[288,256]{1,0:T(8,128)(2,1)S(1)}, bf16[288,256]{1,0:T(8,128)(2,1)S(1)}, u32[]{:S(2)}, u32[]{:S(2)}) collective-permute-start(bf16[288,256]{1,0:T(8,128)(2,1)S(1)} %get-tuple-element.118), channel_id=1, source_target_pairs={{0,4},{1,5},{2,0},{3,1},{4,6},{5,7},{6,2},{7,3},{8,12},{9,13},{10,... | collective-permute-start | bytes 442376 | tf_op jit(solution)/shard_map/ppermute | solution.py:101
  381.6 5.9 %collective-permute-start.67 = (bf16[288,256]{1,0:T(8,128)(2,1)S(1)}, bf16[288,256]{1,0:T(8,128)(2,1)S(1)}, u32[]{:S(2)}, u32[]{:S(2)}) collective-permute-start(bf16[288,256]{1,0:T(8,128)(2,1)S(1)} %get-tuple-element.117), channel_id=1, source_target_pairs={{2,4},{3,5},{4,2},{5,3},{10,12},{11,13},{12,10},{13,11},{18,20},{1... | collective-permute-start | bytes 442376 | tf_op jit(solution)/shard_map/ppermute | solution.py:101
  383.8 6.6 %collective-permute-start.62 = (bf16[128,512]{1,0:T(8,128)(2,1)S(1)}, bf16[128,512]{1,0:T(8,128)(2,1)S(1)}, u32[]{:S(2)}, u32[]{:S(2)}) collective-permute-start(bf16[128,512]{1,0:T(8,128)(2,1)S(1)} %slice.485), channel_id=1, source_target_pairs={{0,1},{1,0},{2,3},{3,2},{4,5},{5,4},{6,7},{7,6},{8,9},{9,8},{10,11... | collective-permute-start | bytes 393224 | tf_op jit(solution)/shard_map/ppermute | solution.py:96
  401.0 5.7 %collective-permute-start.68 = (f32[4,2,2,160]{3,2,1,0:T(2,128)S(1)}, f32[4,2,2,160]{3,2,1,0:T(2,128)S(1)}, u32[]{:S(2)}, u32[]{:S(2)}) collective-permute-start(f32[4,2,2,160]{3,2,1,0:T(2,128)S(1)} %dynamic-slice_bitcast_fusion.8), channel_id=1, source_target_pairs={{0,4},{1,5},{2,6},{3,7},{4,0},{5,1},{6,2},{7,3},{8,12},{9,13},{10,... | collective-permute-start | bytes 30728 | tf_op jit(solution)/shard_map/ppermute | solution.py:96
  420.5 6.3 %collective-permute-start.72 = (bf16[160,256]{1,0:T(8,128)(2,1)S(1)}, bf16[160,256]{1,0:T(8,128)(2,1)S(1)}, u32[]{:S(2)}, u32[]{:S(2)}) collective-permute-start(bf16[160,256]{1,0:T(8,128)(2,1)S(1)} %get-tuple-element.111), channel_id=1, source_target_pairs={{0,24},{1,25},{2,26},{3,27},{4,28},{5,29},{6,30},{7,31},{8,16},{9,... | collective-permute-start | bytes 245768 | tf_op jit(solution)/shard_map/ppermute | solution.py:96
  420.9 6.0 %collective-permute-start.71 = (bf16[160,256]{1,0:T(8,128)(2,1)S(1)}, bf16[160,256]{1,0:T(8,128)(2,1)S(1)}, u32[]{:S(2)}, u32[]{:S(2)}) collective-permute-start(bf16[160,256]{1,0:T(8,128)(2,1)S(1)} %get-tuple-element.112), channel_id=1, source_target_pairs={{0,16},{1,17},{2,18},{3,19},{4,20},{5,21},{6,22},{7,23},{8,24},{9,... | collective-permute-start | bytes 245768 | tf_op jit(solution)/shard_map/ppermute | solution.py:96
  (115 other events, 967.9 us)
Sparse Core Ops, SparseCore 0:
  28.3 49.7 all-gather.3
  97.3 35.5 all-gather.5
  134.8 36.4 all-gather.7
  245.8 51.1 reduce-scatter.3
  300.3 63.2 reduce-scatter.5
  366.9 51.2 reduce-scatter.7
